TPU v7x, 512 devices: a whole 4x8x8 slice. The times are simulated.
512 devices in a mesh: genome: 32 (over x, z_lo, core), cols: 16 (over z_hi, y).
Axes of the slice: x: 4, y: 8, z: 8 (z_hi: 2, z_lo: 4; z = z_hi * 4 + z_lo), core: 2. Of those that a mesh axis runs over, the one named last changes fastest.
Arguments:
- genotypes: int32 [30720, 16384], P('cols', 'genome'), may hold values from 0 to 2
- z_scores: float32 [16384, 2944], P('genome', 'cols'), may hold values from -90 to 90
Outputs:
- effects: float32 [16384, 2944], P('genome', 'cols')
- residual: float32 [16384, 2944], P('genome', 'cols')
All inputs are finite; a program needn't handle non-finite values.
Results may differ from a plain program's by a relative error of at most 0.0034.
Values may be sent and summed in bfloat16 or wider, within the bound.
No kernel may reach another device: no remote copies, remote signals or barrier semaphores. Data moves between devices by JAX's collectives and lax.ppermute only.
A program may use at most 64 MiB of HBM per device.

v0:
```python
import jax
import jax.numpy as jnp
from jax import lax
from jax.sharding import PartitionSpec as P

W = 512
ITERS = 3


ridge_term = 0.1
floor_variance = 0.02


def with_halo(cells, sides, width):
    for axis, dim in sides:
        count = lax.axis_size(axis)
        ends = count - 1
        head = lax.slice_in_dim(cells, 0, width, axis=dim)
        tail = lax.slice_in_dim(cells, cells.shape[dim] - width, cells.shape[dim], axis=dim)
        cells = jnp.concatenate(
            [
                lax.ppermute(tail, axis, [(i, (i + 1) % count) for i in range(ends)]),
                cells,
                lax.ppermute(head, axis, [((i + 1) % count, i) for i in range(ends)]),
            ],
            axis=dim,
        )
    return cells


def tapering_table(block_rows, band_reach):
    row_index = jnp.arange(block_rows, dtype=jnp.int32)[:, None]
    col_index = jnp.arange(block_rows + 2 * band_reach, dtype=jnp.int32)[None, :]
    offset = jnp.abs(col_index - band_reach - row_index).astype(jnp.float32)
    return jnp.maximum(1.0 - offset / (band_reach + 1), 0.0)


def sample_product(left_side, right_side):
    return lax.dot_general(
        left_side, right_side, (((0,), (0,)), ((), ())), preferred_element_type=jnp.float32
    )


def shards(genotypes, z_scores):
    local_samples, variants = genotypes.shape
    sample_count = local_samples * lax.axis_size("cols")
    band_reach = W
    dosage = genotypes.astype(jnp.float32)
    dose_sums, square_sums = lax.psum(
        (jnp.sum(dosage, axis=0), jnp.sum(dosage * dosage, axis=0)), "cols"
    )
    allele_mean = dose_sums / sample_count
    variance = jnp.maximum(square_sums / sample_count - allele_mean * allele_mean, floor_variance)
    standard = ((dosage - allele_mean) / jnp.sqrt(variance)).astype(jnp.bfloat16)
    widened = with_halo(standard, (("genome", 1),), band_reach)
    summed = lax.psum(sample_product(standard, widened), "cols")
    linkage = tapering_table(variants, band_reach) * (summed / sample_count)

    def squares(vector):
        return lax.psum(jnp.sum(vector * vector, axis=0), "genome")

    effects = jnp.zeros_like(z_scores)
    residual = z_scores
    direction = z_scores
    norm_now = squares(residual)
    for iteration in range(ITERS):
        rims = with_halo(direction, (("genome", 0),), band_reach)
        product = jnp.dot(
            linkage, rims, precision=lax.Precision.HIGHEST, preferred_element_type=jnp.float32
        )
        image = product + ridge_term * direction
        step_size = norm_now / lax.psum(jnp.sum(direction * image, axis=0), "genome")
        effects = effects + step_size * direction
        residual = residual - step_size * image
        norm_next = squares(residual)
        direction = residual + norm_next / norm_now * direction
        norm_now = norm_next
    return (effects, residual)


def solution(mesh):
    return jax.shard_map(
        shards,
        mesh=mesh,
        in_specs=(P("cols", "genome"), P("genome", "cols")),
        out_specs=(P("genome", "cols"), P("genome", "cols")),
        check_vma=False,
    )
```

profile of v0, /device:TPU:1, one launch (start us, length us, event | category | flops | bytes accessed | tf_op | source)
XLA Modules:
  0.0 718.7 jit_solution(7148833967904362729)
XLA Ops:
  7.2 0.0 all-reduce.4.cloned.1.call-start
  7.2 2.7 convert_reduce_fusion
  9.9 51.9 %all-reduce.1 = (f32[512]{0:T(512)S(1)}, f32[512]{0:T(512)S(1)}) all-reduce(f32[512]{0:T(512)S(1)} %get-tuple-element.3, f32[512]{0:T(512)S(1)} %get-tuple-element.2), channel_id=1, replica_groups=mesh['genome'=32,'cols'=16] {'cols'}, use_global_device_ids=true, to_apply=%region_5.0 | all-reduce | flops 1024 | bytes 8192 | tf_op jit(solution)/shard_map/psum | solution.py:49
  61.8 2.7 divide_convert_fusion
  64.5 10.7 %collective-permute-start = (bf16[1920,512]{1,0:T(8,128)(2,1)S(1)}, bf16[1920,512]{1,0:T(8,128)(2,1)S(1)}, u32[]{:S(2)}, u32[]{:S(2)}) collective-permute-start(bf16[1920,512]{1,0:T(8,128)(2,1)S(1)} %divide_convert_fusion), channel_id=1, source_target_pairs={{0,16},{16,32},{32,48},{48,64},{64,80},{80,96},{96,112},{112,128},... | collective-permute-start | bytes 5898248 | tf_op jit(solution)/shard_map/ppermute | solution.py:22
  75.2 1.9 collective-permute-start.1
  77.1 19.6 %collective-permute-done = bf16[1920,512]{1,0:T(8,128)(2,1)S(1)} collective-permute-done((bf16[1920,512]{1,0:T(8,128)(2,1)S(1)}, bf16[1920,512]{1,0:T(8,128)(2,1)S(1)}, u32[]{:S(2)}, u32[]{:S(2)}) %collective-permute-start) | collective-permute-done | bytes 1966112 | tf_op jit(solution)/shard_map/ppermute | solution.py:22
  96.8 24.7 %collective-permute-done.1 = bf16[1920,512]{1,0:T(8,128)(2,1)S(1)} collective-permute-done((bf16[1920,512]{1,0:T(8,128)(2,1)S(1)}, bf16[1920,512]{1,0:T(8,128)(2,1)S(1)}, u32[]{:S(2)}, u32[]{:S(2)}) %collective-permute-start.1) | collective-permute-done | bytes 1966112 | tf_op jit(solution)/shard_map/ppermute | solution.py:24
  121.4 5.3 fusion
  126.8 0.0 copy-start
  126.8 0.0 all-reduce.4.cloned.1.call-update
  126.8 1.0 copy-done
  127.7 1.9 collective-permute-start.2
  129.7 2.4 collective-permute-start.3
  132.1 2.1 collective-permute-done.2
  134.2 17.1 %collective-permute-done.3 = f32[512,184]{0,1:T(8,128)S(1)} collective-permute-done((f32[512,184]{0,1:T(8,128)S(1)}, f32[512,184]{0,1:T(8,128)S(1)}, u32[]{:S(2)}, u32[]{:S(2)}) %collective-permute-start.3) | collective-permute-done | bytes 376864 | tf_op jit(solution)/shard_map/ppermute | solution.py:24
  151.3 175.3 %all-reduce.4.cloned.1.call-done = f32[512,1536]{1,0:T(8,128)} async-done(((f32[512,1536]{1,0:T(8,128)}), f32[512,1536]{1,0:T(8,128)}) %all-reduce.4.cloned.1.call-update) | async-done | bytes 3145744 | tf_op jit(solution)/shard_map/psum | solution.py:56
  326.6 6.5 multiply_reduce_fusion.5
  333.1 77.9 %all-reduce = (f32[184]{0:T(256)S(1)}, f32[184]{0:T(256)S(1)}) all-reduce(f32[184]{0:T(256)S(1)} %get-tuple-element.5, f32[184]{0:T(256)S(1)} %get-tuple-element.4), channel_id=1, replica_groups=mesh['genome'=32,'cols'=16] {'genome'}, use_global_device_ids=true, to_apply=%region_1.0 | all-reduce | flops 368 | bytes 2944 | tf_op jit(solution)/shard_map/psum | solution.py:60
  411.1 0.2 multiply_reduce_fusion.4
  411.3 67.6 %psum.68 = f32[184]{0:T(256)S(1)} all-reduce(f32[184]{0:T(256)S(1)} %multiply_reduce_fusion.4), channel_id=1, replica_groups=mesh['genome'=32,'cols'=16] {'genome'}, use_global_device_ids=true, to_apply=%region_10.0 | all-reduce | flops 184 | bytes 1472 | tf_op jit(solution)/shard_map/psum | solution.py:60
  478.9 0.2 multiply_add_fusion.2
  479.1 1.9 collective-permute-start.4
  481.0 2.6 collective-permute-start.5
  483.6 1.9 collective-permute-done.4
  485.5 4.4 collective-permute-done.5
  490.0 6.4 multiply_reduce_fusion.3
  496.4 61.9 %psum.69 = f32[184]{0:T(256)S(1)} all-reduce(f32[184]{0:T(256)S(1)} %get-tuple-element.17), channel_id=1, replica_groups=mesh['genome'=32,'cols'=16] {'genome'}, use_global_device_ids=true, to_apply=%region_12.0 | all-reduce | flops 184 | bytes 1472 | tf_op jit(solution)/shard_map/psum | solution.py:72
  558.3 0.3 multiply_reduce_fusion.2
  558.6 72.9 %psum.70 = f32[184]{0:T(256)S(1)} all-reduce(f32[184]{0:T(256)S(1)} %get-tuple-element.10), channel_id=1, replica_groups=mesh['genome'=32,'cols'=16] {'genome'}, use_global_device_ids=true, to_apply=%region_14.0 | all-reduce | flops 184 | bytes 1472 | tf_op jit(solution)/shard_map/psum | solution.py:60
  631.5 0.1 multiply_add_fusion.1
  631.6 1.9 collective-permute-start.6
  633.6 2.4 collective-permute-start.7
  636.0 2.1 collective-permute-done.6
  638.1 4.4 collective-permute-done.7
  642.5 6.4 multiply_reduce_fusion.1
  649.0 61.9 %psum.71 = f32[184]{0:T(256)S(1)} all-reduce(f32[184]{0:T(256)S(1)} %get-tuple-element.19), channel_id=1, replica_groups=mesh['genome'=32,'cols'=16] {'genome'}, use_global_device_ids=true, to_apply=%region_16.0 | all-reduce | flops 184 | bytes 1472 | tf_op jit(solution)/shard_map/psum | solution.py:72
  710.8 1.0 multiply_subtract_fusion
  (7 shorter events, 0.1 us)
Async XLA Ops:
  7.2 319.5 %all-reduce.4.cloned.1.call-start = ((), (), s32[]{:S(2)}) async-start(), calls=%async_computation | async-start | bytes 6291456 | tf_op jit(solution)/shard_map/psum | solution.py:56
  64.5 32.3 %collective-permute-start = (bf16[1920,512]{1,0:T(8,128)(2,1)S(1)}, bf16[1920,512]{1,0:T(8,128)(2,1)S(1)}, u32[]{:S(2)}, u32[]{:S(2)}) collective-permute-start(bf16[1920,512]{1,0:T(8,128)(2,1)S(1)} %divide_convert_fusion), channel_id=1, source_target_pairs={{0,16},{16,32},{32,48},{48,64},{64,80},{80,96},{96,112},{112,128},... | collective-permute-start | bytes 5898248 | tf_op jit(solution)/shard_map/ppermute | solution.py:22
  75.2 46.2 %collective-permute-start.1 = (bf16[1920,512]{1,0:T(8,128)(2,1)S(1)}, bf16[1920,512]{1,0:T(8,128)(2,1)S(1)}, u32[]{:S(2)}, u32[]{:S(2)}) collective-permute-start(bf16[1920,512]{1,0:T(8,128)(2,1)S(1)} %divide_convert_fusion), channel_id=1, source_target_pairs={{16,0},{32,16},{48,32},{64,48},{80,64},{96,80},{112,96},{128,112},... | collective-permute-start | bytes 5898248 | tf_op jit(solution)/shard_map/ppermute | solution.py:24
  126.8 1.0 copy-start
  127.7 6.4 collective-permute-start.2
  129.7 21.6 %collective-permute-start.3 = (f32[512,184]{0,1:T(8,128)S(1)}, f32[512,184]{0,1:T(8,128)S(1)}, u32[]{:S(2)}, u32[]{:S(2)}) collective-permute-start(f32[512,184]{0,1:T(8,128)S(1)} %copy-done), channel_id=1, source_target_pairs={{16,0},{32,16},{48,32},{64,48},{80,64},{96,80},{112,96},{128,112},... | collective-permute-start | bytes 1130504 | tf_op jit(solution)/shard_map/ppermute | solution.py:24
  479.1 6.5 collective-permute-start.4
  481.0 9.0 %collective-permute-start.5 = (f32[512,184]{0,1:T(8,128)S(1)}, f32[512,184]{0,1:T(8,128)S(1)}, u32[]{:S(2)}, u32[]{:S(2)}) collective-permute-start(f32[512,184]{0,1:T(8,128)S(1)} %multiply_add_fusion.2), channel_id=1, source_target_pairs={{16,0},{32,16},{48,32},{64,48},{80,64},{96,80},{112,96},{128,112},... | collective-permute-start | bytes 1130504 | tf_op jit(solution)/shard_map/ppermute | solution.py:24
  631.6 6.5 collective-permute-start.6
  633.6 9.0 %collective-permute-start.7 = (f32[512,184]{0,1:T(8,128)S(1)}, f32[512,184]{0,1:T(8,128)S(1)}, u32[]{:S(2)}, u32[]{:S(2)}) collective-permute-start(f32[512,184]{0,1:T(8,128)S(1)} %multiply_add_fusion.1), channel_id=1, source_target_pairs={{16,0},{32,16},{48,32},{64,48},{80,64},{96,80},{112,96},{128,112},... | collective-permute-start | bytes 1130504 | tf_op jit(solution)/shard_map/ppermute | solution.py:24
Sparse Core Ops, SparseCore 0:
  126.9 199.6 all-reduce.3
where the time goes:
time: 722 us; the launch traced here: 719 us
  blocking collectives  394 us (55%)
  waiting for transfers between devices  252 us (35%)
  starting transfers between devices  25.9 us (4%)
  matrix products  24.7 us (3%)
  between operations  14.1 us (2%)
    psum x3, blocking collectives, squares(): return lax.psum(jnp.sum(vector * vector, axis=0), 'genome')  218 us
    psum x1, waiting for transfers between devices, shards(): summed = lax.psum(sample_product(standard, widened), 'cols')  175 us
    psum x2, blocking collectives, shards(): lax.psum(jnp.sum(direction * image, axis=0), 'genome')  124 us
    psum x1, blocking collectives, shards(): lax.psum((jnp.sum(dosage, axis=0), jnp.sum(dosage * dosage, axis=0)), 'co...  51.9 us
    ppermute x4, waiting for transfers between devices, with_halo(): lax.ppermute(head, axis, [((i + 1) % count, i) for i in range(ends)])  50.7 us
    ppermute x4, waiting for transfers between devices, with_halo(): lax.ppermute(tail, axis, [(i, (i + 1) % count) for i in range(ends)])  25.7 us
    dot_general x3, matrix products, shards(): jnp.dot(linkage, rims, precision=lax.Precision.HIGHEST, preferred_element...  19.4 us
    ppermute x4, starting transfers between devices, with_halo(): lax.ppermute(tail, axis, [(i, (i + 1) % count) for i in range(ends)])  16.5 us
  transfers between devices with their start and end apart: 9, of which 9 were waited for; matrix products, arithmetic and copies ran while one was open for 0% of the time, Pallas kernels for 0%

commit v1 on v0

v1 whole, which is shorter than its diff:
```python
import functools

import jax
import jax.numpy as jnp
from jax import lax
from jax.experimental import pallas as pl
from jax.experimental.pallas import tpu as pltpu
from jax.sharding import PartitionSpec as P

W = 512
RIDGE = 0.1
FLOOR = 0.02
TILE = 128
SIDE = W // TILE
TILES = tuple((p, q) for p in range(SIDE) for q in range(p + 1))
NT = len(TILES)
CODE = 32000.0
f32, bf16, i16, i32 = jnp.float32, jnp.bfloat16, jnp.int16, jnp.int32


def dot(a, b):
    return jnp.dot(a, b, preferred_element_type=f32)


def halves(a):
    high = a.astype(bf16)
    return high, (a - high.astype(f32)).astype(bf16)


def call(kernel, outs, *args):
    spec = pl.BlockSpec(memory_space=pltpu.VMEM)
    scalars = [a.dtype == i32 and a.ndim == 1 for a in args]
    return pl.pallas_call(
        kernel,
        out_shape=outs,
        in_specs=[pl.BlockSpec(memory_space=pltpu.SMEM) if s else spec for s in scalars],
        out_specs=jax.tree.map(lambda _: spec, outs, is_leaf=lambda o: not isinstance(o, tuple)),
        compiler_params=pltpu.CompilerParams(vmem_limit_bytes=16 << 20),
    )(*(a if s else pltpu.with_memory_space_constraint(a, pltpu.VMEM) for a, s in zip(args, scalars)))


def shape(*dims, dtype=f32):
    return pltpu.VMEM(dims, dtype)


def pack_products(gram, block, out_ref):
    peers = out_ref.shape[0]
    rows = TILE // peers
    pieces = [
        gram[p * TILE : (p + 1) * TILE, q * TILE : (q + 1) * TILE].reshape(peers, rows, TILE) for p, q in TILES
    ]
    ones = jnp.ones((8, block.shape[0]), bf16)
    sums = dot(ones, block)[:1]
    squares = dot(ones, block * block)[:1]
    stats = [v[:, q * TILE : (q + 1) * TILE] for v in (sums, squares) for q in range(SIDE)]
    stats = jnp.concatenate(stats + [jnp.zeros((8, TILE), f32)], axis=0)
    for u in range(NT // 2):
        pair = jnp.concatenate(pieces[2 * u : 2 * u + 2], axis=1)
        out_ref[:, 2 * rows * u : 2 * rows * (u + 1), :] = pair.astype(i32).astype(i16)
    stats = stats.astype(i32).astype(i16)
    for k in range(peers):
        out_ref[k, NT * rows : NT * rows + 16, :] = stats


def own_products(x_ref, out_ref, turned_ref):
    block = x_ref[...]
    turned = block.T
    turned_ref[...] = turned
    pack_products(dot(turned, block), block, out_ref)


def next_products(turned_ref, x_ref, out_ref):
    block = x_ref[...]
    pack_products(dot(turned_ref[...], block), block, out_ref)


def correlate(samples, me_ref, own_ref, next_ref, out_ref):
    peers = own_ref.shape[0]
    rows = TILE // peers

    def total(ref):
        acc = ref[0].astype(i32)
        for k in range(1, peers):
            acc = acc + ref[k].astype(i32)
        return acc.astype(f32) / samples

    def stats(means):
        mean = means[NT * rows : NT * rows + SIDE]
        square = means[NT * rows + SIDE : NT * rows + 2 * SIDE]
        return mean, 1.0 / jnp.sqrt(jnp.maximum(square - mean * mean, FLOOR))

    own, nxt = total(own_ref), total(next_ref)
    own_stats, next_stats = stats(own), stats(nxt)
    lane = lax.broadcasted_iota(i32, (rows, TILE), 1)
    row = lax.broadcasted_iota(i32, (rows, TILE), 0) + me_ref[0] * rows

    def at_rows(vector, p):
        return jnp.sum(jnp.where(lane == row, vector[p : p + 1], 0.0), axis=1, keepdims=True)

    row_mean = [at_rows(own_stats[0], p) for p in range(SIDE)]
    row_scale = [at_rows(own_stats[1], p) * CODE for p in range(SIDE)]
    base = 0
    for means, (mean, scale) in ((own, own_stats), (nxt, next_stats)):
        codes = []
        for t, (p, q) in enumerate(TILES):
            cov = means[t * rows : (t + 1) * rows] - row_mean[p] * mean[q : q + 1]
            codes.append(jnp.round(cov * row_scale[p] * scale[q : q + 1]))
        codes = jnp.concatenate(codes, axis=0).astype(i32).astype(i16)
        for k in range(peers):
            out_ref[k, base : base + NT * rows, :] = codes
        base += NT * rows


def taper(p, q, shift):
    row = lax.broadcasted_iota(i32, (TILE, TILE), 0) + p * TILE
    col = lax.broadcasted_iota(i32, (TILE, TILE), 1) + q * TILE + shift
    reach = jnp.abs(col - row).astype(f32)
    return jnp.maximum(1.0 - reach / (W + 1), 0.0)


def unpack(codes_ref, near_high, near_low, next_high, next_low, back_high, back_low):
    peers = codes_ref.shape[0]
    rows = TILE // peers

    def tiles(base):
        for u in range(NT // 2):
            lo = base + 2 * rows * u
            pair = codes_ref[:, lo : lo + 2 * rows, :].astype(i32).astype(f32)
            yield TILES[2 * u], pair[:, :rows].reshape(TILE, TILE)
            yield TILES[2 * u + 1], pair[:, rows:].reshape(TILE, TILE)

    def put(high_ref, low_ref, p, q, value):
        high, low = halves(value)
        high_ref[p * TILE : (p + 1) * TILE, q * TILE : (q + 1) * TILE] = high
        low_ref[p * TILE : (p + 1) * TILE, q * TILE : (q + 1) * TILE] = low

    for (p, q), code in tiles(0):
        value = code * (taper(p, q, 0) * (1.0 / CODE))
        put(near_high, near_low, p, q, value)
        if p != q:
            put(near_high, near_low, q, p, value.T)
    zero = jnp.zeros((TILE, TILE), f32)
    for (p, q), code in tiles(NT * rows):
        value = code * (taper(p, q, W) * (1.0 / CODE))
        put(next_high, next_low, p, q, value)
        put(back_high, back_low, q, p, value.T)
        if p != q:
            put(next_high, next_low, q, p, zero)
            put(back_high, back_low, p, q, zero)


def product(v, high_ref, low_ref):
    high, low = halves(v)
    return dot(high, high_ref[...]) + dot(low, high_ref[...]) + dot(high, low_ref[...])


def outward(v_ref, high_ref, low_ref, out_ref):
    out_ref[...] = product(v_ref[...], high_ref, low_ref)


def inward(v_ref, high_ref, low_ref, out_ref):
    out_ref[...] = product(v_ref[...], high_ref, low_ref) + RIDGE * v_ref[...]


def gather_in(part_ref, came_ref, next_ref, high_ref, low_ref, out_ref):
    out_ref[...] = part_ref[...] + came_ref[...] + product(next_ref[...], high_ref, low_ref)


def along(a, b):
    return jnp.sum(a * b, axis=1, keepdims=True)


def early_moments(a_ref, b_ref, c_ref, out_ref):
    a, b, c = a_ref[...], b_ref[...], c_ref[...]
    lane = lax.broadcasted_iota(i32, out_ref.shape, 1)
    total = jnp.zeros(out_ref.shape, f32)
    for k, m in enumerate((along(a, a), along(a, b), along(b, b), along(b, c), along(c, c))):
        total = jnp.where(lane == k, m, total)
    out_ref[...] = total


def last_vector(part_ref, came_ref, next_ref, high_ref, low_ref, c_ref, early_ref, out_ref, moments_ref):
    w = part_ref[...] + came_ref[...] + product(next_ref[...], high_ref, low_ref)
    out_ref[...] = w
    lane = lax.broadcasted_iota(i32, early_ref.shape, 1)
    total = jnp.where(lane == 5, along(c_ref[...], w), early_ref[...])
    fill = moments_ref.shape[2] - total.shape[0]
    turned = jnp.concatenate([total, jnp.zeros((fill, TILE), f32)], axis=0).T[:8]
    for k in range(moments_ref.shape[0]):
        moments_ref[k] = turned


def combine(moments_ref, a_ref, b_ref, c_ref, d_ref, effects_ref, residual_ref):
    total = moments_ref[0]
    for k in range(1, moments_ref.shape[0]):
        total = total + moments_ref[k]
    moment = [total[k : k + 1] / total[:1] for k in range(6)]

    def inner(x, y, power):
        return sum(
            x[i] * y[j] * moment[i + j + power] for i in range(len(x)) for j in range(len(y))
        )

    one = jnp.ones_like(moment[0])
    residual, direction, effects = [one], [one], []
    norm_now = inner(residual, residual, 0)
    for step in range(3):
        step_size = norm_now / inner(direction, direction, 1)
        effects = [
            (effects[k] if k < len(effects) else 0.0) + step_size * direction[k] for k in range(len(direction))
        ]
        image = [0.0] + direction
        residual = [
            (residual[k] if k < len(residual) else 0.0) - step_size * image[k] for k in range(len(image))
        ]
        if step < 2:
            norm_next = inner(residual, residual, 0)
            ratio = norm_next / norm_now
            direction = [
                residual[k] + (ratio * direction[k] if k < len(direction) else 0.0) for k in range(len(residual))
            ]
            norm_now = norm_next
    rows = effects + residual
    table = jnp.concatenate(rows + [jnp.zeros((TILE - len(rows), total.shape[1]), f32)], axis=0).T
    table = table[: a_ref.shape[0]]
    col = [table[:, k : k + 1] for k in range(len(rows))]
    a, b, c, d = a_ref[...], b_ref[...], c_ref[...], d_ref[...]
    effects_ref[...] = col[0] * a + col[1] * b + col[2] * c
    residual_ref[...] = col[3] * a + col[4] * b + col[5] * c + col[6] * d


def shards(genotypes, z_scores):
    local_samples, variants = genotypes.shape
    blocks = lax.axis_size("genome")
    peers = lax.axis_size("cols")
    samples = local_samples * peers
    to_left = [(k + 1, k) for k in range(blocks - 1)]
    to_right = [(k, k + 1) for k in range(blocks - 1)]
    rows = TILE // peers

    dosage = genotypes.astype(bf16)
    next_dosage = lax.ppermute(dosage, "genome", to_left)
    packed = shape(peers, NT * rows + 16, TILE, dtype=i16)
    own, turned = call(own_products, (packed, shape(variants, local_samples, dtype=bf16)), dosage)
    own = lax.all_to_all(own, "cols", 0, 0)
    own, next_dosage = lax.optimization_barrier((own, next_dosage))
    nxt = call(next_products, packed, turned, next_dosage)
    z = z_scores.T
    z, nxt = lax.optimization_barrier((z, nxt))
    z_next = lax.ppermute(z, "genome", to_left)
    nxt = lax.all_to_all(nxt, "cols", 0, 0)
    me = lax.axis_index("cols").astype(i32).reshape(1)
    codes = call(functools.partial(correlate, samples), shape(peers, 2 * NT * rows, TILE, dtype=i16), me, own, nxt)
    codes = lax.all_to_all(codes, "cols", 0, 0)
    square = shape(W, W, dtype=bf16)
    near_h, near_l, next_h, next_l, back_h, back_l = call(unpack, (square,) * 6, codes)

    vector = shape(*z.shape)

    def spread(v):
        came = lax.ppermute(call(outward, vector, v, next_h, next_l), "genome", to_right)
        return came, call(inward, vector, v, near_h, near_l)

    came, part = spread(z)
    one = call(gather_in, vector, part, came, z_next, back_h, back_l)
    one_next = lax.ppermute(one, "genome", to_left)
    came, part = spread(one)
    two = call(gather_in, vector, part, came, one_next, back_h, back_l)
    two_next = lax.ppermute(two, "genome", to_left)
    came, part = spread(two)
    early = call(early_moments, shape(z.shape[0], TILE), z, one, two)
    three, moments = call(
        last_vector, (vector, shape(blocks, 8, 256)), part, came, two_next, back_h, back_l, two, early
    )
    moments = lax.all_to_all(moments, "genome", 0, 0)
    effects, residual = call(combine, (jax.ShapeDtypeStruct(z.shape, f32),) * 2, moments, z, one, two, three)
    return effects.T, residual.T


def solution(mesh):
    return jax.shard_map(
        shards,
        mesh=mesh,
        in_specs=(P("cols", "genome"), P("genome", "cols")),
        out_specs=(P("genome", "cols"), P("genome", "cols")),
        check_vma=False,
    )
```

time: 722 us -> 164 us (0.23)
  blocking collectives: 394 us -> 45.2 us
  waiting for transfers between devices: 252 us -> 50.8 us
  starting transfers between devices: 25.9 us -> 51.2 us
  matrix products: 24.7 us -> 0 us
  between operations: 14.1 us -> 0.8 us
  Pallas kernels: 0 us -> 12.3 us
    psum x6 -> x0, blocking collectives: 394 us -> none  [the longest x3 218 us: squares(): return lax.psum(jnp.sum(vector * vector, axis=0), 'genome')]
    psum x1 -> x0, waiting for transfers between devices: 175 us -> none  [shards(): summed = lax.psum(sample_product(standard, widened), 'cols')]
    ppermute x8 -> x7, waiting for transfers between devices: 76.4 us -> 22.2 us  [the longest x1 7.64 us: shards(): one_next = lax.ppermute(one, 'genome', to_left)]
    all_to_all x0 -> x2, blocking collectives: none -> 45.2 us  [the longest x1 27.2 us: shards(): own = lax.all_to_all(own, 'cols', 0, 0)]
    all_to_all x0 -> x2, waiting for transfers between devices: none -> 28.6 us  [the longest x1 15.4 us: shards(): codes = lax.all_to_all(codes, 'cols', 0, 0)]
    dot_general x4 -> x0, matrix products: 24.7 us -> none  [the longest x3 19.4 us: shards(): jnp.dot(linkage, rims, precision=lax.Precision.HIGHEST, preferred_element...]
    all_to_all x0 -> x2, starting transfers between devices: none -> 16.4 us  [the longest x1 12.5 us: shards(): nxt = lax.all_to_all(nxt, 'cols', 0, 0)]
    pallas_call x0 -> x15, Pallas kernels: none -> 12.3 us  [call(): pl.pallas_call(kernel, out_shape=outs, in_specs=[pl.BlockSpec(memory_spac...]
  transfers between devices with their start and end apart: 9 -> 9, of which waited for: 9 -> 7; matrix products, arithmetic and copies ran while one was open for 0% -> 0% of each run, Pallas kernels for 0% -> 3%
where the time goes in v1:
time: 164 us; the launch traced here: 163 us
  starting transfers between devices  51.2 us (31%)
  waiting for transfers between devices  50.8 us (31%)
  blocking collectives  45.2 us (28%)
  Pallas kernels  12.3 us (8%)
  other arithmetic  2.65 us (2%)
    all_to_all x1, blocking collectives, shards(): own = lax.all_to_all(own, 'cols', 0, 0)  27.2 us
    ppermute x3, starting transfers between devices, spread(): lax.ppermute(call(outward, vector, v, next_h, next_l), 'genome', to_right)  19.7 us
    all_to_all x1, blocking collectives, shards(): moments = lax.all_to_all(moments, 'genome', 0, 0)  18 us
    all_to_all x1, waiting for transfers between devices, shards(): codes = lax.all_to_all(codes, 'cols', 0, 0)  15.4 us
    all_to_all x1, waiting for transfers between devices, shards(): nxt = lax.all_to_all(nxt, 'cols', 0, 0)  13.2 us
    all_to_all x1, starting transfers between devices, shards(): nxt = lax.all_to_all(nxt, 'cols', 0, 0)  12.5 us
    pallas_call x15, Pallas kernels, call(): pl.pallas_call(kernel, out_shape=outs, in_specs=[pl.BlockSpec(memory_spac...  12.3 us
    ppermute x1, starting transfers between devices, shards(): next_dosage = lax.ppermute(dosage, 'genome', to_left)  8.75 us
  transfers between devices with their start and end apart: 9, of which 7 were waited for; matrix products, arithmetic and copies ran while one was open for 0% of the time, Pallas kernels for 3%

profile of v1, /device:TPU:1, one launch (start us, length us, event | category | flops | bytes accessed | tf_op | source)
XLA Modules:
  0.0 163.0 jit_solution(3647277739066971037)
XLA Ops:
  0.6 2.6 %convert_element_type.3.x_ref = bf16[1920,512]{1,0:T(8,128)(2,1)S(1)} convert(s32[1920,512]{1,0:T(8,128)} %param.2) | non-fusion elementwise | flops 983040 | bytes 5898240 | tf_op jit(solution)/shard_map/convert_element_type | solution.py:241
  3.3 8.7 %collective-permute-start = (bf16[1920,512]{1,0:T(8,128)(2,1)S(1)}, bf16[1920,512]{1,0:T(8,128)(2,1)S(1)}, u32[]{:S(2)}, u32[]{:S(2)}) collective-permute-start(bf16[1920,512]{1,0:T(8,128)(2,1)S(1)} %convert_element_type.3.x_ref), channel_id=1, source_target_pairs={{16,0},{32,16},{48,32},{64,48},{80,64},{96,80},{112,96},{128,112},... | collective-permute-start | bytes 5898248 | tf_op jit(solution)/shard_map/ppermute | solution.py:242
  12.0 1.8 %shard_map.41 = (s16[16,96,128]{2,1,0:T(8,128)(2,1)S(1)}, bf16[512,1920]{1,0:T(8,128)(2,1)S(1)}) custom-call(bf16[1920,512]{1,0:T(8,128)(2,1)S(1)} %convert_element_type.3.x_ref), custom_call_target="tpu_custom_call" | custom-call | tf_op jit(solution)/shard_map/pallas_call | solution.py:33
  13.8 27.2 %all_to_all.20.own_ref = s16[16,96,128]{2,1,0:T(8,128)(2,1)S(1)} all-to-all(s16[16,96,128]{2,1,0:T(8,128)(2,1)S(1)} %get-tuple-element.19), channel_id=1, replica_groups=mesh['genome'=32,'cols'=16] {'cols'}, dimensions={0} | all-to-all | bytes 786432 | tf_op jit(solution)/shard_map/all_to_all | solution.py:245
  41.0 0.0 collective-permute-done.x_ref
  41.0 2.5 %shard_map.42 = s16[16,96,128]{2,1,0:T(8,128)(2,1)} custom-call(bf16[512,1920]{1,0:T(8,128)(2,1)S(1)} %get-tuple-element.18.turned_ref, bf16[1920,512]{1,0:T(8,128)(2,1)S(1)} %collective-permute-done.x_ref), custom_call_target="tpu_custom_call" | custom-call | tf_op jit(solution)/shard_map/pallas_call | solution.py:33
  43.5 0.0 copy-start
  43.5 12.5 %all-to-all-start.1 = ((s16[16,96,128]{2,1,0:T(8,128)(2,1)}), s16[16,96,128]{2,1,0:T(8,128)(2,1)S(1)}, u32[]{:S(2)}, u32[]{:S(2)}) async-start(s16[16,96,128]{2,1,0:T(8,128)(2,1)} %shard_map.42), calls=%async_computation.1 | async-start | bytes 786432 | tf_op jit(solution)/shard_map/all_to_all | solution.py:251
  56.0 13.2 %all-to-all-done.1.next_ref = s16[16,96,128]{2,1,0:T(8,128)(2,1)S(1)} async-done(((s16[16,96,128]{2,1,0:T(8,128)(2,1)}), s16[16,96,128]{2,1,0:T(8,128)(2,1)S(1)}, u32[]{:S(2)}, u32[]{:S(2)}) %all-to-all-start.1) | async-done | bytes 393248 | tf_op jit(solution)/shard_map/all_to_all | solution.py:251
  69.1 1.0 shard_map.43
  70.2 3.9 %all-to-all-start.2 = ((s16[16,160,128]{2,1,0:T(8,128)(2,1)}), s16[16,160,128]{2,1,0:T(8,128)(2,1)S(1)}, u32[]{:S(2)}, u32[]{:S(2)}) async-start(s16[16,160,128]{2,1,0:T(8,128)(2,1)} %shard_map.43), calls=%async_computation.2 | async-start | bytes 1310720 | tf_op jit(solution)/shard_map/all_to_all | solution.py:254
  74.1 0.0 copy-done
  74.1 1.9 %collective-permute-start.2 = (f32[184,512]{1,0:T(8,128)S(1)}, f32[184,512]{1,0:T(8,128)S(1)}, u32[]{:S(2)}, u32[]{:S(2)}) collective-permute-start(f32[184,512]{1,0:T(8,128)S(1)} %bitcast.4), channel_id=1, source_target_pairs={{16,0},{32,16},{48,32},{64,48},{80,64},{96,80},{112,96},{128,112},... | collective-permute-start | bytes 1130504 | tf_op jit(solution)/shard_map/ppermute | solution.py:250
  76.1 15.4 %all-to-all-done.2.codes_ref = s16[16,160,128]{2,1,0:T(8,128)(2,1)S(1)} async-done(((s16[16,160,128]{2,1,0:T(8,128)(2,1)}), s16[16,160,128]{2,1,0:T(8,128)(2,1)S(1)}, u32[]{:S(2)}, u32[]{:S(2)}) %all-to-all-start.2) | async-done | bytes 655392 | tf_op jit(solution)/shard_map/all_to_all | solution.py:254
  91.5 0.9 shard_map.44
  92.4 0.5 shard_map.46
  92.9 13.4 %collective-permute-start.1 = (f32[184,512]{1,0:T(8,128)S(1)}, f32[184,512]{1,0:T(8,128)S(1)}, u32[]{:S(2)}, u32[]{:S(2)}) collective-permute-start(f32[184,512]{1,0:T(8,128)S(1)} %shard_map.46), channel_id=1, source_target_pairs={{0,16},{16,32},{32,48},{48,64},{64,80},{80,96},{96,112},{112,128},... | collective-permute-start | bytes 1130504 | tf_op jit(solution)/shard_map/ppermute | solution.py:261
  106.3 0.5 shard_map.45.part_ref
  106.8 0.0 collective-permute-done.2.next_ref
  106.8 4.0 %collective-permute-done.1.came_ref = f32[184,512]{1,0:T(8,128)S(1)} collective-permute-done((f32[184,512]{1,0:T(8,128)S(1)}, f32[184,512]{1,0:T(8,128)S(1)}, u32[]{:S(2)}, u32[]{:S(2)}) %collective-permute-start.1) | collective-permute-done | bytes 376864 | tf_op jit(solution)/shard_map/ppermute | solution.py:261
  110.8 0.5 shard_map.47.v_ref.b_ref
  111.3 0.5 shard_map.49
  111.8 4.4 %collective-permute-start.3 = (f32[184,512]{1,0:T(8,128)S(1)}, f32[184,512]{1,0:T(8,128)S(1)}, u32[]{:S(2)}, u32[]{:S(2)}) collective-permute-start(f32[184,512]{1,0:T(8,128)S(1)} %shard_map.49), channel_id=1, source_target_pairs={{0,16},{16,32},{32,48},{48,64},{64,80},{80,96},{96,112},{112,128},... | collective-permute-start | bytes 1130504 | tf_op jit(solution)/shard_map/ppermute | solution.py:261
  116.2 1.9 %collective-permute-start.4 = (f32[184,512]{1,0:T(8,128)S(1)}, f32[184,512]{1,0:T(8,128)S(1)}, u32[]{:S(2)}, u32[]{:S(2)}) collective-permute-start(f32[184,512]{1,0:T(8,128)S(1)} %shard_map.47.v_ref.b_ref), channel_id=1, source_target_pairs={{16,0},{32,16},{48,32},{64,48},{80,64},{96,80},{112,96},{128,112},... | collective-permute-start | bytes 1130504 | tf_op jit(solution)/shard_map/ppermute | solution.py:266
  118.2 0.5 shard_map.48.part_ref
  118.6 2.1 %collective-permute-done.3.came_ref = f32[184,512]{1,0:T(8,128)S(1)} collective-permute-done((f32[184,512]{1,0:T(8,128)S(1)}, f32[184,512]{1,0:T(8,128)S(1)}, u32[]{:S(2)}, u32[]{:S(2)}) %collective-permute-start.3) | collective-permute-done | bytes 376864 | tf_op jit(solution)/shard_map/ppermute | solution.py:261
  120.8 7.6 %collective-permute-done.4.next_ref = f32[184,512]{1,0:T(8,128)S(1)} collective-permute-done((f32[184,512]{1,0:T(8,128)S(1)}, f32[184,512]{1,0:T(8,128)S(1)}, u32[]{:S(2)}, u32[]{:S(2)}) %collective-permute-start.4) | collective-permute-done | bytes 376864 | tf_op jit(solution)/shard_map/ppermute | solution.py:266
  128.4 0.5 shard_map.50.v_ref.c_ref
  128.9 0.5 shard_map.52
  129.4 1.9 %collective-permute-start.5 = (f32[184,512]{1,0:T(8,128)S(1)}, f32[184,512]{1,0:T(8,128)S(1)}, u32[]{:S(2)}, u32[]{:S(2)}) collective-permute-start(f32[184,512]{1,0:T(8,128)S(1)} %shard_map.52), channel_id=1, source_target_pairs={{0,16},{16,32},{32,48},{48,64},{64,80},{80,96},{96,112},{112,128},... | collective-permute-start | bytes 1130504 | tf_op jit(solution)/shard_map/ppermute | solution.py:261
  131.3 2.4 %collective-permute-start.6 = (f32[184,512]{1,0:T(8,128)S(1)}, f32[184,512]{1,0:T(8,128)S(1)}, u32[]{:S(2)}, u32[]{:S(2)}) collective-permute-start(f32[184,512]{1,0:T(8,128)S(1)} %shard_map.50.v_ref.c_ref), channel_id=1, source_target_pairs={{16,0},{32,16},{48,32},{64,48},{80,64},{96,80},{112,96},{128,112},... | collective-permute-start | bytes 1130504 | tf_op jit(solution)/shard_map/ppermute | solution.py:269
  133.7 0.5 shard_map.51.part_ref
  134.2 0.2 shard_map.53.early_ref
  134.5 1.4 collective-permute-done.5.came_ref
  135.8 7.1 %collective-permute-done.6.next_ref = f32[184,512]{1,0:T(8,128)S(1)} collective-permute-done((f32[184,512]{1,0:T(8,128)S(1)}, f32[184,512]{1,0:T(8,128)S(1)}, u32[]{:S(2)}, u32[]{:S(2)}) %collective-permute-start.6) | collective-permute-done | bytes 376864 | tf_op jit(solution)/shard_map/ppermute | solution.py:269
  142.9 0.6 shard_map.54
  143.5 18.0 %all_to_all.21.moments_ref = f32[32,8,256]{2,1,0:T(8,128)S(1)} all-to-all(f32[32,8,256]{2,1,0:T(8,128)S(1)} %get-tuple-element.30), channel_id=1, replica_groups=mesh['genome'=32,'cols'=16] {'genome'}, dimensions={0} | all-to-all | bytes 524288 | tf_op jit(solution)/shard_map/all_to_all | solution.py:275
  161.6 1.4 shard_map.55
Async XLA Ops:
  3.3 37.7 %collective-permute-start = (bf16[1920,512]{1,0:T(8,128)(2,1)S(1)}, bf16[1920,512]{1,0:T(8,128)(2,1)S(1)}, u32[]{:S(2)}, u32[]{:S(2)}) collective-permute-start(bf16[1920,512]{1,0:T(8,128)(2,1)S(1)} %convert_element_type.3.x_ref), channel_id=1, source_target_pairs={{16,0},{32,16},{48,32},{64,48},{80,64},{96,80},{112,96},{128,112},... | collective-permute-start | bytes 5898248 | tf_op jit(solution)/shard_map/ppermute | solution.py:242
  43.5 30.7 %copy-start = (f32[512,184]{0,1:T(8,128)S(1)}, f32[512,184]{0,1:T(8,128)}, u32[]{:S(2)}) copy-start(f32[512,184]{0,1:T(8,128)} %param.3) | copy-start | bytes 1130500
  43.5 25.7 %all-to-all-start.1 = ((s16[16,96,128]{2,1,0:T(8,128)(2,1)}), s16[16,96,128]{2,1,0:T(8,128)(2,1)S(1)}, u32[]{:S(2)}, u32[]{:S(2)}) async-start(s16[16,96,128]{2,1,0:T(8,128)(2,1)} %shard_map.42), calls=%async_computation.1 | async-start | bytes 786432 | tf_op jit(solution)/shard_map/all_to_all | solution.py:251
  70.2 21.3 %all-to-all-start.2 = ((s16[16,160,128]{2,1,0:T(8,128)(2,1)}), s16[16,160,128]{2,1,0:T(8,128)(2,1)S(1)}, u32[]{:S(2)}, u32[]{:S(2)}) async-start(s16[16,160,128]{2,1,0:T(8,128)(2,1)} %shard_map.43), calls=%async_computation.2 | async-start | bytes 1310720 | tf_op jit(solution)/shard_map/all_to_all | solution.py:254
  74.1 32.7 %collective-permute-start.2 = (f32[184,512]{1,0:T(8,128)S(1)}, f32[184,512]{1,0:T(8,128)S(1)}, u32[]{:S(2)}, u32[]{:S(2)}) collective-permute-start(f32[184,512]{1,0:T(8,128)S(1)} %bitcast.4), channel_id=1, source_target_pairs={{16,0},{32,16},{48,32},{64,48},{80,64},{96,80},{112,96},{128,112},... | collective-permute-start | bytes 1130504 | tf_op jit(solution)/shard_map/ppermute | solution.py:250
  92.9 17.9 %collective-permute-start.1 = (f32[184,512]{1,0:T(8,128)S(1)}, f32[184,512]{1,0:T(8,128)S(1)}, u32[]{:S(2)}, u32[]{:S(2)}) collective-permute-start(f32[184,512]{1,0:T(8,128)S(1)} %shard_map.46), channel_id=1, source_target_pairs={{0,16},{16,32},{32,48},{48,64},{64,80},{80,96},{96,112},{112,128},... | collective-permute-start | bytes 1130504 | tf_op jit(solution)/shard_map/ppermute | solution.py:261
  111.8 8.9 %collective-permute-start.3 = (f32[184,512]{1,0:T(8,128)S(1)}, f32[184,512]{1,0:T(8,128)S(1)}, u32[]{:S(2)}, u32[]{:S(2)}) collective-permute-start(f32[184,512]{1,0:T(8,128)S(1)} %shard_map.49), channel_id=1, source_target_pairs={{0,16},{16,32},{32,48},{48,64},{64,80},{80,96},{96,112},{112,128},... | collective-permute-start | bytes 1130504 | tf_op jit(solution)/shard_map/ppermute | solution.py:261
  116.2 12.2 %collective-permute-start.4 = (f32[184,512]{1,0:T(8,128)S(1)}, f32[184,512]{1,0:T(8,128)S(1)}, u32[]{:S(2)}, u32[]{:S(2)}) collective-permute-start(f32[184,512]{1,0:T(8,128)S(1)} %shard_map.47.v_ref.b_ref), channel_id=1, source_target_pairs={{16,0},{32,16},{48,32},{64,48},{80,64},{96,80},{112,96},{128,112},... | collective-permute-start | bytes 1130504 | tf_op jit(solution)/shard_map/ppermute | solution.py:266
  129.4 6.5 %collective-permute-start.5 = (f32[184,512]{1,0:T(8,128)S(1)}, f32[184,512]{1,0:T(8,128)S(1)}, u32[]{:S(2)}, u32[]{:S(2)}) collective-permute-start(f32[184,512]{1,0:T(8,128)S(1)} %shard_map.52), channel_id=1, source_target_pairs={{0,16},{16,32},{32,48},{48,64},{64,80},{80,96},{96,112},{112,128},... | collective-permute-start | bytes 1130504 | tf_op jit(solution)/shard_map/ppermute | solution.py:261
  131.3 11.6 %collective-permute-start.6 = (f32[184,512]{1,0:T(8,128)S(1)}, f32[184,512]{1,0:T(8,128)S(1)}, u32[]{:S(2)}, u32[]{:S(2)}) collective-permute-start(f32[184,512]{1,0:T(8,128)S(1)} %shard_map.50.v_ref.c_ref), channel_id=1, source_target_pairs={{16,0},{32,16},{48,32},{64,48},{80,64},{96,80},{112,96},{128,112},... | collective-permute-start | bytes 1130504 | tf_op jit(solution)/shard_map/ppermute | solution.py:269

commit v2 on v1

--- a/solution.py
+++ b/solution.py
@@ -15,6 +15,7 @@
 TILES = tuple((p, q) for p in range(SIDE) for q in range(p + 1))
 NT = len(TILES)
 CODE = 32000.0
+HALF = 32768
 f32, bf16, i16, i32 = jnp.float32, jnp.bfloat16, jnp.int16, jnp.int32
 
 
@@ -43,8 +44,7 @@
     return pltpu.VMEM(dims, dtype)
 
 
-def pack_products(gram, block, out_ref):
-    peers = out_ref.shape[0]
+def pack_products(gram, block, put, peers):
     rows = TILE // peers
     pieces = [
         gram[p * TILE : (p + 1) * TILE, q * TILE : (q + 1) * TILE].reshape(peers, rows, TILE) for p, q in TILES
@@ -56,40 +56,63 @@
     stats = jnp.concatenate(stats + [jnp.zeros((8, TILE), f32)], axis=0)
     for u in range(NT // 2):
         pair = jnp.concatenate(pieces[2 * u : 2 * u + 2], axis=1)
-        out_ref[:, 2 * rows * u : 2 * rows * (u + 1), :] = pair.astype(i32).astype(i16)
-    stats = stats.astype(i32).astype(i16)
-    for k in range(peers):
-        out_ref[k, NT * rows : NT * rows + 16, :] = stats
+        put(2 * rows * u, pair.astype(i32).astype(i16))
+    stats = jnp.broadcast_to(stats.astype(i32).astype(i16)[None], (peers, *stats.shape))
+    put(NT * rows, stats)
 
 
 def own_products(x_ref, out_ref, turned_ref):
     block = x_ref[...]
     turned = block.T
     turned_ref[...] = turned
-    pack_products(dot(turned, block), block, out_ref)
+    near, depth = out_ref.shape[0], out_ref.shape[1] // 2
+
+    def put(at, value):
+        for far in range(2):
+            lo = far * depth + at
+            out_ref[:, lo : lo + value.shape[1], :] = value[far * near : (far + 1) * near]
+
+    pack_products(dot(turned, block), block, put, 2 * near)
 
 
 def next_products(turned_ref, x_ref, out_ref):
     block = x_ref[...]
-    pack_products(dot(turned_ref[...], block), block, out_ref)
-
-
-def correlate(samples, me_ref, own_ref, next_ref, out_ref):
-    peers = own_ref.shape[0]
+
+    def put(at, value):
+        out_ref[:, at : at + value.shape[1], :] = value
+
+    pack_products(dot(turned_ref[...], block), block, put, out_ref.shape[0])
+
+
+def fold(me_ref, came_ref, keep_ref, send_ref):
+    near, depth = came_ref.shape[0], came_ref.shape[1] // 2
+    far = me_ref[0] // near
+
+    def total(side):
+        rows = pl.ds(pl.multiple_of(side * depth, depth), depth)
+        acc = came_ref[0, rows, :].astype(i32)
+        for k in range(1, near):
+            acc = acc + came_ref[k, rows, :].astype(i32)
+        return acc
+
+    keep_ref[...] = total(far)
+    send_ref[...] = (total(1 - far) - HALF).astype(i16)
+
+
+def correlate(samples, me_ref, keep_ref, far_ref, next_ref, out_ref):
+    peers = next_ref.shape[0]
     rows = TILE // peers
-
-    def total(ref):
-        acc = ref[0].astype(i32)
-        for k in range(1, peers):
-            acc = acc + ref[k].astype(i32)
-        return acc.astype(f32) / samples
 
     def stats(means):
         mean = means[NT * rows : NT * rows + SIDE]
         square = means[NT * rows + SIDE : NT * rows + 2 * SIDE]
         return mean, 1.0 / jnp.sqrt(jnp.maximum(square - mean * mean, FLOOR))
 
-    own, nxt = total(own_ref), total(next_ref)
+    own = keep_ref[...] + far_ref[...].astype(i32) + HALF
+    nxt = next_ref[0].astype(i32)
+    for k in range(1, peers):
+        nxt = nxt + next_ref[k].astype(i32)
+    own, nxt = own.astype(f32) / samples, nxt.astype(f32) / samples
     own_stats, next_stats = stats(own), stats(nxt)
     lane = lax.broadcasted_iota(i32, (rows, TILE), 1)
     row = lax.broadcasted_iota(i32, (rows, TILE), 0) + me_ref[0] * rows
@@ -154,40 +177,71 @@
     return dot(high, high_ref[...]) + dot(low, high_ref[...]) + dot(high, low_ref[...])
 
 
+def diagonal(rows):
+    return lax.broadcasted_iota(i32, (rows, 256), 0) == lax.broadcasted_iota(i32, (rows, 256), 1)
+
+
+def encode(v, out_ref):
+    rows = v.shape[0]
+    top = jnp.max(jnp.abs(v), axis=1, keepdims=True)
+    power = jnp.ceil(jnp.log2(jnp.maximum(top, 1e-30)) + 0.01)
+    code = jnp.round(v * (jnp.exp2(-power) * CODE))
+    turned = jnp.sum(jnp.where(diagonal(rows), power, 0.0), axis=0, keepdims=True)
+    tail = jnp.broadcast_to(jnp.concatenate([turned, turned], axis=1), (out_ref.shape[0] - rows, v.shape[1]))
+    out_ref[...] = jnp.concatenate([code, tail], axis=0).astype(i32).astype(i16)
+
+
+def decode(code_ref, rows):
+    code = code_ref[...].astype(i32).astype(f32)
+    power = jnp.sum(jnp.where(diagonal(rows), code[rows : rows + 1, :256], 0.0), axis=1, keepdims=True)
+    return code[:rows] * (jnp.exp2(power) * (1.0 / CODE))
+
+
+def start_code(v_ref, out_ref):
+    encode(v_ref[...], out_ref)
+
+
 def outward(v_ref, high_ref, low_ref, out_ref):
-    out_ref[...] = product(v_ref[...], high_ref, low_ref)
+    encode(product(v_ref[...], high_ref, low_ref), out_ref)
 
 
 def inward(v_ref, high_ref, low_ref, out_ref):
     out_ref[...] = product(v_ref[...], high_ref, low_ref) + RIDGE * v_ref[...]
 
 
-def gather_in(part_ref, came_ref, next_ref, high_ref, low_ref, out_ref):
-    out_ref[...] = part_ref[...] + came_ref[...] + product(next_ref[...], high_ref, low_ref)
+def gather(part_ref, came_ref, next_ref, high_ref, low_ref):
+    rows = part_ref.shape[0]
+    return part_ref[...] + decode(came_ref, rows) + product(decode(next_ref, rows), high_ref, low_ref)
+
+
+def gather_in(part_ref, came_ref, next_ref, back_h, back_l, next_h, next_l, out_ref, left_ref, right_ref):
+    w = gather(part_ref, came_ref, next_ref, back_h, back_l)
+    out_ref[...] = w
+    encode(w, left_ref)
+    encode(product(w, next_h, next_l), right_ref)
 
 
 def along(a, b):
     return jnp.sum(a * b, axis=1, keepdims=True)
 
 
+def turn(moment):
+    return jnp.sum(jnp.where(diagonal(moment.shape[0]), moment, 0.0), axis=0, keepdims=True)
+
+
 def early_moments(a_ref, b_ref, c_ref, out_ref):
     a, b, c = a_ref[...], b_ref[...], c_ref[...]
-    lane = lax.broadcasted_iota(i32, out_ref.shape, 1)
-    total = jnp.zeros(out_ref.shape, f32)
-    for k, m in enumerate((along(a, a), along(a, b), along(b, b), along(b, c), along(c, c))):
-        total = jnp.where(lane == k, m, total)
-    out_ref[...] = total
-
-
-def last_vector(part_ref, came_ref, next_ref, high_ref, low_ref, c_ref, early_ref, out_ref, moments_ref):
-    w = part_ref[...] + came_ref[...] + product(next_ref[...], high_ref, low_ref)
+    rows = [turn(m) for m in (along(a, a), along(a, b), along(b, b), along(b, c), along(c, c))]
+    out_ref[...] = jnp.concatenate(rows + [jnp.zeros((3, 256), f32)], axis=0)
+
+
+def last_vector(part_ref, came_ref, next_ref, back_h, back_l, c_ref, early_ref, out_ref, moments_ref):
+    w = gather(part_ref, came_ref, next_ref, back_h, back_l)
     out_ref[...] = w
-    lane = lax.broadcasted_iota(i32, early_ref.shape, 1)
-    total = jnp.where(lane == 5, along(c_ref[...], w), early_ref[...])
-    fill = moments_ref.shape[2] - total.shape[0]
-    turned = jnp.concatenate([total, jnp.zeros((fill, TILE), f32)], axis=0).T[:8]
+    row = lax.broadcasted_iota(i32, early_ref.shape, 0)
+    moments = jnp.where(row == 5, turn(along(c_ref[...], w)), early_ref[...])
     for k in range(moments_ref.shape[0]):
-        moments_ref[k] = turned
+        moments_ref[k] = moments
 
 
 def combine(moments_ref, a_ref, b_ref, c_ref, d_ref, effects_ref, residual_ref):
@@ -238,39 +292,52 @@
     to_right = [(k, k + 1) for k in range(blocks - 1)]
     rows = TILE // peers
 
+    near = peers // 2
+    depth = NT * rows + 16
+    cols = range(peers)
+    sides = [list(cols[:near]), list(cols[near:])]
+
     dosage = genotypes.astype(bf16)
     next_dosage = lax.ppermute(dosage, "genome", to_left)
-    packed = shape(peers, NT * rows + 16, TILE, dtype=i16)
-    own, turned = call(own_products, (packed, shape(variants, local_samples, dtype=bf16)), dosage)
-    own = lax.all_to_all(own, "cols", 0, 0)
-    own, next_dosage = lax.optimization_barrier((own, next_dosage))
-    nxt = call(next_products, packed, turned, next_dosage)
+    own, turned = call(
+        own_products,
+        (shape(near, 2 * depth, TILE, dtype=i16), shape(variants, local_samples, dtype=bf16)),
+        dosage,
+    )
+    own = lax.all_to_all(own, "cols", 0, 0, axis_index_groups=sides)
+    me = lax.axis_index("cols").astype(i32).reshape(1)
+    keep, far = call(fold, (shape(depth, TILE, dtype=i32), shape(depth, TILE, dtype=i16)), me, own)
+    far = lax.ppermute(far, "cols", [(k, (k + near) % peers) for k in cols])
     z = z_scores.T
-    z, nxt = lax.optimization_barrier((z, nxt))
-    z_next = lax.ppermute(z, "genome", to_left)
+    vector = shape(*z.shape)
+    code = shape(z.shape[0] // 16 * 16 + 16, z.shape[1], dtype=i16)
+    z_code = call(start_code, code, z)
+    far, next_dosage, z_code = lax.optimization_barrier((far, next_dosage, z_code))
+    nxt = call(next_products, shape(peers, depth, TILE, dtype=i16), turned, next_dosage)
+    z_code, nxt = lax.optimization_barrier((z_code, nxt))
     nxt = lax.all_to_all(nxt, "cols", 0, 0)
-    me = lax.axis_index("cols").astype(i32).reshape(1)
-    codes = call(functools.partial(correlate, samples), shape(peers, 2 * NT * rows, TILE, dtype=i16), me, own, nxt)
+    z_next = lax.ppermute(z_code, "genome", to_left)
+    codes = call(
+        functools.partial(correlate, samples), shape(peers, 2 * NT * rows, TILE, dtype=i16), me, keep, far, nxt
+    )
     codes = lax.all_to_all(codes, "cols", 0, 0)
     square = shape(W, W, dtype=bf16)
     near_h, near_l, next_h, next_l, back_h, back_l = call(unpack, (square,) * 6, codes)
 
-    vector = shape(*z.shape)
-
-    def spread(v):
-        came = lax.ppermute(call(outward, vector, v, next_h, next_l), "genome", to_right)
-        return came, call(inward, vector, v, near_h, near_l)
-
-    came, part = spread(z)
-    one = call(gather_in, vector, part, came, z_next, back_h, back_l)
-    one_next = lax.ppermute(one, "genome", to_left)
-    came, part = spread(one)
-    two = call(gather_in, vector, part, came, one_next, back_h, back_l)
-    two_next = lax.ppermute(two, "genome", to_left)
-    came, part = spread(two)
-    early = call(early_moments, shape(z.shape[0], TILE), z, one, two)
+    def step(part, came, nxt):
+        w, left, right = call(
+            gather_in, (vector, code, code), part, came, nxt, back_h, back_l, next_h, next_l
+        )
+        came = lax.ppermute(right, "genome", to_right)
+        nxt = lax.ppermute(left, "genome", to_left)
+        return w, came, nxt, call(inward, vector, w, near_h, near_l)
+
+    came = lax.ppermute(call(outward, code, z, next_h, next_l), "genome", to_right)
+    one, came, nxt, part = step(call(inward, vector, z, near_h, near_l), came, z_next)
+    two, came, nxt, part = step(part, came, nxt)
+    early = call(early_moments, shape(8, 256), z, one, two)
     three, moments = call(
-        last_vector, (vector, shape(blocks, 8, 256)), part, came, two_next, back_h, back_l, two, early
+        last_vector, (vector, shape(blocks, 8, 256)), part, came, nxt, back_h, back_l, two, early
     )
     moments = lax.all_to_all(moments, "genome", 0, 0)
     effects, residual = call(combine, (jax.ShapeDtypeStruct(z.shape, f32),) * 2, moments, z, one, two, three)

time: 164 us -> 155 us (0.945)
  starting transfers between devices: 51.2 us -> 46.2 us
  waiting for transfers between devices: 50.8 us -> 46.2 us
  blocking collectives: 45.2 us -> 41.5 us
  local copies, waits for them, and re-layouts: 0.01 us -> 2.81 us
  Pallas kernels: 12.3 us -> 14.4 us
    all_to_all x1, starting transfers between devices: 12.5 us -> 3.45 us  [shards(): own = lax.all_to_all(own, 'cols', 0, 0, axis_index_groups=sides)]
    ppermute x6 -> x7, waiting for transfers between devices: 22.2 us -> 14.6 us  [the longest x2 11.2 us: step(): nxt = lax.ppermute(left, 'genome', to_left)]
    all_to_all x1, blocking collectives: 27.2 us -> 21.7 us  [shards(): nxt = lax.all_to_all(nxt, 'cols', 0, 0)]
    unnamed x2 -> x6, local copies, waits for them, and re-layouts: 0.01 us -> 2.81 us
    ppermute x6 -> x7, starting transfers between devices: 26 us -> 28.5 us  [the longest x1 8.95 us: shards(): far = lax.ppermute(far, 'cols', [(k, (k + near) % peers) for k in cols])]
    pallas_call x15, Pallas kernels: 12.3 us -> 14.4 us  [call(): pl.pallas_call(kernel, out_shape=outs, in_specs=[pl.BlockSpec(memory_spac...]
    all_to_all x1, blocking collectives: 18 us -> 19.9 us  [shards(): moments = lax.all_to_all(moments, 'genome', 0, 0)]
    all_to_all x1, waiting for transfers between devices: 13.2 us -> 15 us  [shards(): own = lax.all_to_all(own, 'cols', 0, 0, axis_index_groups=sides)]
  transfers between devices with their start and end apart: 9 -> 10, of which waited for: 7 -> 7; matrix products, arithmetic and copies ran while one was open for 0% -> 0% of each run, Pallas kernels for 3% -> 4%
where the time goes in v2:
time: 155 us
  starting transfers between devices  46.2 us (30%)
  waiting for transfers between devices  46.2 us (30%)
  blocking collectives  41.5 us (27%)
  Pallas kernels  14.4 us (9%)
  local copies, waits for them, and re-layouts  2.81 us (2%)
  other arithmetic  2.65 us (2%)
    all_to_all x1, blocking collectives, shards(): nxt = lax.all_to_all(nxt, 'cols', 0, 0)  21.7 us
    all_to_all x1, blocking collectives, shards(): moments = lax.all_to_all(moments, 'genome', 0, 0)  19.9 us
    all_to_all x1, waiting for transfers between devices, shards(): codes = lax.all_to_all(codes, 'cols', 0, 0)  16.6 us
    all_to_all x1, waiting for transfers between devices, shards(): own = lax.all_to_all(own, 'cols', 0, 0, axis_index_groups=sides)  15 us
    pallas_call x15, Pallas kernels, call(): pl.pallas_call(kernel, out_shape=outs, in_specs=[pl.BlockSpec(memory_spac...  14.4 us
    ppermute x2, waiting for transfers between devices, step(): nxt = lax.ppermute(left, 'genome', to_left)  11.2 us
    ppermute x1, starting transfers between devices, shards(): far = lax.ppermute(far, 'cols', [(k, (k + near) % peers) for k in cols])  8.95 us
    ppermute x1, starting transfers between devices, shards(): next_dosage = lax.ppermute(dosage, 'genome', to_left)  8.88 us
  transfers between devices with their start and end apart: 10, of which 7 were waited for; matrix products, arithmetic and copies ran while one was open for 0% of the time, Pallas kernels for 4%

profile of v2, /device:TPU:1, one launch (start us, length us, event | category | flops | bytes accessed | tf_op | source)
XLA Modules:
  0.0 154.6 jit_solution(10769859405996935438)
XLA Ops:
  0.6 2.6 %convert_element_type.3.x_ref = bf16[1920,512]{1,0:T(8,128)(2,1)S(1)} convert(s32[1920,512]{1,0:T(8,128)} %param.2) | non-fusion elementwise | flops 983040 | bytes 5898240 | tf_op jit(solution)/shard_map/convert_element_type | solution.py:300
  3.3 0.0 copy-start
  3.3 8.9 %collective-permute-start.1 = (bf16[1920,512]{1,0:T(8,128)(2,1)S(1)}, bf16[1920,512]{1,0:T(8,128)(2,1)}, u32[]{:S(2)}, u32[]{:S(2)}) collective-permute-start(bf16[1920,512]{1,0:T(8,128)(2,1)S(1)} %convert_element_type.3.x_ref), channel_id=1, source_target_pairs={{16,0},{32,16},{48,32},{64,48},{80,64},{96,80},{112,96},{128,112},... | collective-permute-start | bytes 5898248 | tf_op jit(solution)/shard_map/ppermute | solution.py:301
  12.2 2.5 %shard_map.41 = (s16[8,192,128]{2,1,0:T(8,128)(2,1)}, bf16[512,1920]{1,0:T(8,128)(2,1)S(1)}) custom-call(bf16[1920,512]{1,0:T(8,128)(2,1)S(1)} %convert_element_type.3.x_ref), custom_call_target="tpu_custom_call" | custom-call | tf_op jit(solution)/shard_map/pallas_call | solution.py:34
  14.7 0.0 copy-start.1
  14.7 1.3 copy-done.1
  16.0 3.5 %all-to-all-start = ((s16[8,192,128]{2,1,0:T(8,128)(2,1)}), s16[8,192,128]{2,1,0:T(8,128)(2,1)S(1)}, u32[]{:S(2)}, u32[]{:S(2)}) async-start(s16[8,192,128]{2,1,0:T(8,128)(2,1)} %get-tuple-element.27), calls=%async_computation | async-start | bytes 786432 | tf_op jit(solution)/shard_map/all_to_all | solution.py:307
  19.4 15.0 %all-to-all-done.came_ref = s16[8,192,128]{2,1,0:T(8,128)(2,1)S(1)} async-done(((s16[8,192,128]{2,1,0:T(8,128)(2,1)}), s16[8,192,128]{2,1,0:T(8,128)(2,1)S(1)}, u32[]{:S(2)}, u32[]{:S(2)}) %all-to-all-start) | async-done | bytes 393248 | tf_op jit(solution)/shard_map/all_to_all | solution.py:307
  34.4 0.1 shard_map.42
  34.5 8.9 %collective-permute-start = (s16[96,128]{1,0:T(8,128)(2,1)S(1)}, s16[96,128]{1,0:T(8,128)(2,1)S(1)}, u32[]{:S(2)}, u32[]{:S(2)}) collective-permute-start(s16[96,128]{1,0:T(8,128)(2,1)S(1)} %get-tuple-element.29), channel_id=1, source_target_pairs={{0,8},{1,9},{2,10},{3,11},{4,12},{5,13},{6,14},{7,15},{8,0},{9,1},... | collective-permute-start | bytes 73736 | tf_op jit(solution)/shard_map/ppermute | solution.py:310
  43.4 0.0 copy-done
  43.4 0.2 shard_map.43
  43.6 1.1 collective-permute-done.far_ref
  44.7 0.0 collective-permute-done.1.x_ref
  44.7 0.0 copy-start.2
  44.7 1.5 copy-done.2
  46.3 3.3 %shard_map.44 = s16[16,96,128]{2,1,0:T(8,128)(2,1)S(1)} custom-call(bf16[512,1920]{1,0:T(8,128)(2,1)S(1)} %copy-done.2, bf16[1920,512]{1,0:T(8,128)(2,1)} %collective-permute-done.1.x_ref), custom_call_target="tpu_custom_call" | custom-call | tf_op jit(solution)/shard_map/pallas_call | solution.py:34
  49.6 21.7 %all_to_all.20.next_ref = s16[16,96,128]{2,1,0:T(8,128)(2,1)S(1)} all-to-all(s16[16,96,128]{2,1,0:T(8,128)(2,1)S(1)} %shard_map.44), channel_id=1, replica_groups=mesh['genome'=32,'cols'=16] {'cols'}, dimensions={0} | all-to-all | bytes 786432 | tf_op jit(solution)/shard_map/all_to_all | solution.py:318
  71.2 1.0 shard_map.45
  72.3 5.4 %all-to-all-start.2 = ((s16[16,160,128]{2,1,0:T(8,128)(2,1)}), s16[16,160,128]{2,1,0:T(8,128)(2,1)S(1)}, u32[]{:S(2)}, u32[]{:S(2)}) async-start(s16[16,160,128]{2,1,0:T(8,128)(2,1)} %shard_map.45), calls=%async_computation.2 | async-start | bytes 1310720 | tf_op jit(solution)/shard_map/all_to_all | solution.py:323
  77.7 3.7 %collective-permute-start.3 = (s16[192,512]{1,0:T(8,128)(2,1)S(1)}, s16[192,512]{1,0:T(8,128)(2,1)S(1)}, u32[]{:S(2)}, u32[]{:S(2)}) collective-permute-start(s16[192,512]{1,0:T(8,128)(2,1)S(1)} %shard_map.43), channel_id=1, source_target_pairs={{16,0},{32,16},{48,32},{64,48},{80,64},{96,80},{112,96},{128,112},... | collective-permute-start | bytes 589832 | tf_op jit(solution)/shard_map/ppermute | solution.py:319
  81.4 16.6 %all-to-all-done.2.codes_ref = s16[16,160,128]{2,1,0:T(8,128)(2,1)S(1)} async-done(((s16[16,160,128]{2,1,0:T(8,128)(2,1)}), s16[16,160,128]{2,1,0:T(8,128)(2,1)S(1)}, u32[]{:S(2)}, u32[]{:S(2)}) %all-to-all-start.2) | async-done | bytes 655392 | tf_op jit(solution)/shard_map/all_to_all | solution.py:323
  98.0 0.9 shard_map.46
  98.9 0.6 shard_map.48
  99.6 5.2 %collective-permute-start.2 = (s16[192,512]{1,0:T(8,128)(2,1)S(1)}, s16[192,512]{1,0:T(8,128)(2,1)S(1)}, u32[]{:S(2)}, u32[]{:S(2)}) collective-permute-start(s16[192,512]{1,0:T(8,128)(2,1)S(1)} %shard_map.48), channel_id=1, source_target_pairs={{0,16},{16,32},{32,48},{48,64},{64,80},{80,96},{96,112},{112,128},... | collective-permute-start | bytes 589832 | tf_op jit(solution)/shard_map/ppermute | solution.py:335
  104.8 0.5 shard_map.47.part_ref
  105.3 0.0 collective-permute-done.3.next_ref
  105.3 2.1 %collective-permute-done.2.came_ref = s16[192,512]{1,0:T(8,128)(2,1)S(1)} collective-permute-done((s16[192,512]{1,0:T(8,128)(2,1)S(1)}, s16[192,512]{1,0:T(8,128)(2,1)S(1)}, u32[]{:S(2)}, u32[]{:S(2)}) %collective-permute-start.2) | collective-permute-done | bytes 196640 | tf_op jit(solution)/shard_map/ppermute | solution.py:335
  107.4 1.1 shard_map.49
  108.4 4.4 %collective-permute-start.4 = (s16[192,512]{1,0:T(8,128)(2,1)S(1)}, s16[192,512]{1,0:T(8,128)(2,1)S(1)}, u32[]{:S(2)}, u32[]{:S(2)}) collective-permute-start(s16[192,512]{1,0:T(8,128)(2,1)S(1)} %get-tuple-element.43), channel_id=1, source_target_pairs={{0,16},{16,32},{32,48},{48,64},{64,80},{80,96},{96,112},{112,128},... | collective-permute-start | bytes 589832 | tf_op jit(solution)/shard_map/ppermute | solution.py:331
  112.8 1.9 %collective-permute-start.5 = (s16[192,512]{1,0:T(8,128)(2,1)S(1)}, s16[192,512]{1,0:T(8,128)(2,1)S(1)}, u32[]{:S(2)}, u32[]{:S(2)}) collective-permute-start(s16[192,512]{1,0:T(8,128)(2,1)S(1)} %get-tuple-element.44), channel_id=1, source_target_pairs={{16,0},{32,16},{48,32},{64,48},{80,64},{96,80},{112,96},{128,112},... | collective-permute-start | bytes 589832 | tf_op jit(solution)/shard_map/ppermute | solution.py:332
  114.8 0.5 shard_map.50.part_ref
  115.3 0.2 collective-permute-done.4.came_ref
  115.4 4.6 %collective-permute-done.5.next_ref = s16[192,512]{1,0:T(8,128)(2,1)S(1)} collective-permute-done((s16[192,512]{1,0:T(8,128)(2,1)S(1)}, s16[192,512]{1,0:T(8,128)(2,1)S(1)}, u32[]{:S(2)}, u32[]{:S(2)}) %collective-permute-start.5) | collective-permute-done | bytes 196640 | tf_op jit(solution)/shard_map/ppermute | solution.py:332
  120.1 1.1 shard_map.51
  121.1 1.9 %collective-permute-start.6 = (s16[192,512]{1,0:T(8,128)(2,1)S(1)}, s16[192,512]{1,0:T(8,128)(2,1)S(1)}, u32[]{:S(2)}, u32[]{:S(2)}) collective-permute-start(s16[192,512]{1,0:T(8,128)(2,1)S(1)} %get-tuple-element.46), channel_id=1, source_target_pairs={{0,16},{16,32},{32,48},{48,64},{64,80},{80,96},{96,112},{112,128},... | collective-permute-start | bytes 589832 | tf_op jit(solution)/shard_map/ppermute | solution.py:331
  123.1 2.4 %collective-permute-start.7 = (s16[192,512]{1,0:T(8,128)(2,1)S(1)}, s16[192,512]{1,0:T(8,128)(2,1)S(1)}, u32[]{:S(2)}, u32[]{:S(2)}) collective-permute-start(s16[192,512]{1,0:T(8,128)(2,1)S(1)} %get-tuple-element.47), channel_id=1, source_target_pairs={{16,0},{32,16},{48,32},{64,48},{80,64},{96,80},{112,96},{128,112},... | collective-permute-start | bytes 589832 | tf_op jit(solution)/shard_map/ppermute | solution.py:332
  125.5 0.5 shard_map.52.part_ref
  126.0 0.2 shard_map.53.early_ref
  126.2 0.0 collective-permute-done.6.came_ref
  126.2 6.5 %collective-permute-done.7.next_ref = s16[192,512]{1,0:T(8,128)(2,1)S(1)} collective-permute-done((s16[192,512]{1,0:T(8,128)(2,1)S(1)}, s16[192,512]{1,0:T(8,128)(2,1)S(1)}, u32[]{:S(2)}, u32[]{:S(2)}) %collective-permute-start.7) | collective-permute-done | bytes 196640 | tf_op jit(solution)/shard_map/ppermute | solution.py:332
  132.7 0.6 shard_map.54
  133.4 19.9 %all_to_all.21.moments_ref = f32[32,8,256]{2,1,0:T(8,128)S(1)} all-to-all(f32[32,8,256]{2,1,0:T(8,128)S(1)} %get-tuple-element.48), channel_id=1, replica_groups=mesh['genome'=32,'cols'=16] {'genome'}, dimensions={0} | all-to-all | bytes 524288 | tf_op jit(solution)/shard_map/all_to_all | solution.py:342
  153.2 1.4 shard_map.55
Async XLA Ops:
  3.3 40.1 %copy-start = (f32[512,184]{0,1:T(8,128)S(1)}, f32[512,184]{0,1:T(8,128)}, u32[]{:S(2)}) copy-start(f32[512,184]{0,1:T(8,128)} %param.3) | copy-start | bytes 1130500
  3.3 41.4 %collective-permute-start.1 = (bf16[1920,512]{1,0:T(8,128)(2,1)S(1)}, bf16[1920,512]{1,0:T(8,128)(2,1)}, u32[]{:S(2)}, u32[]{:S(2)}) collective-permute-start(bf16[1920,512]{1,0:T(8,128)(2,1)S(1)} %convert_element_type.3.x_ref), channel_id=1, source_target_pairs={{16,0},{32,16},{48,32},{64,48},{80,64},{96,80},{112,96},{128,112},... | collective-permute-start | bytes 5898248 | tf_op jit(solution)/shard_map/ppermute | solution.py:301
  14.7 1.3 copy-start.1
  16.0 18.4 %all-to-all-start = ((s16[8,192,128]{2,1,0:T(8,128)(2,1)}), s16[8,192,128]{2,1,0:T(8,128)(2,1)S(1)}, u32[]{:S(2)}, u32[]{:S(2)}) async-start(s16[8,192,128]{2,1,0:T(8,128)(2,1)} %get-tuple-element.27), calls=%async_computation | async-start | bytes 786432 | tf_op jit(solution)/shard_map/all_to_all | solution.py:307
  34.5 10.3 %collective-permute-start = (s16[96,128]{1,0:T(8,128)(2,1)S(1)}, s16[96,128]{1,0:T(8,128)(2,1)S(1)}, u32[]{:S(2)}, u32[]{:S(2)}) collective-permute-start(s16[96,128]{1,0:T(8,128)(2,1)S(1)} %get-tuple-element.29), channel_id=1, source_target_pairs={{0,8},{1,9},{2,10},{3,11},{4,12},{5,13},{6,14},{7,15},{8,0},{9,1},... | collective-permute-start | bytes 73736 | tf_op jit(solution)/shard_map/ppermute | solution.py:310
  44.7 1.5 %copy-start.2 = (bf16[512,1920]{1,0:T(8,128)(2,1)S(1)}, bf16[512,1920]{1,0:T(8,128)(2,1)}, u32[]{:S(2)}) copy-start(bf16[512,1920]{1,0:T(8,128)(2,1)} %copy-done.1) | copy-start | bytes 5898244
  72.3 25.8 %all-to-all-start.2 = ((s16[16,160,128]{2,1,0:T(8,128)(2,1)}), s16[16,160,128]{2,1,0:T(8,128)(2,1)S(1)}, u32[]{:S(2)}, u32[]{:S(2)}) async-start(s16[16,160,128]{2,1,0:T(8,128)(2,1)} %shard_map.45), calls=%async_computation.2 | async-start | bytes 1310720 | tf_op jit(solution)/shard_map/all_to_all | solution.py:323
  77.7 27.5 %collective-permute-start.3 = (s16[192,512]{1,0:T(8,128)(2,1)S(1)}, s16[192,512]{1,0:T(8,128)(2,1)S(1)}, u32[]{:S(2)}, u32[]{:S(2)}) collective-permute-start(s16[192,512]{1,0:T(8,128)(2,1)S(1)} %shard_map.43), channel_id=1, source_target_pairs={{16,0},{32,16},{48,32},{64,48},{80,64},{96,80},{112,96},{128,112},... | collective-permute-start | bytes 589832 | tf_op jit(solution)/shard_map/ppermute | solution.py:319
  99.6 7.8 %collective-permute-start.2 = (s16[192,512]{1,0:T(8,128)(2,1)S(1)}, s16[192,512]{1,0:T(8,128)(2,1)S(1)}, u32[]{:S(2)}, u32[]{:S(2)}) collective-permute-start(s16[192,512]{1,0:T(8,128)(2,1)S(1)} %shard_map.48), channel_id=1, source_target_pairs={{0,16},{16,32},{32,48},{48,64},{64,80},{80,96},{96,112},{112,128},... | collective-permute-start | bytes 589832 | tf_op jit(solution)/shard_map/ppermute | solution.py:335
  108.4 7.0 %collective-permute-start.4 = (s16[192,512]{1,0:T(8,128)(2,1)S(1)}, s16[192,512]{1,0:T(8,128)(2,1)S(1)}, u32[]{:S(2)}, u32[]{:S(2)}) collective-permute-start(s16[192,512]{1,0:T(8,128)(2,1)S(1)} %get-tuple-element.43), channel_id=1, source_target_pairs={{0,16},{16,32},{32,48},{48,64},{64,80},{80,96},{96,112},{112,128},... | collective-permute-start | bytes 589832 | tf_op jit(solution)/shard_map/ppermute | solution.py:331
  112.8 7.2 %collective-permute-start.5 = (s16[192,512]{1,0:T(8,128)(2,1)S(1)}, s16[192,512]{1,0:T(8,128)(2,1)S(1)}, u32[]{:S(2)}, u32[]{:S(2)}) collective-permute-start(s16[192,512]{1,0:T(8,128)(2,1)S(1)} %get-tuple-element.44), channel_id=1, source_target_pairs={{16,0},{32,16},{48,32},{64,48},{80,64},{96,80},{112,96},{128,112},... | collective-permute-start | bytes 589832 | tf_op jit(solution)/shard_map/ppermute | solution.py:332
  121.1 5.1 %collective-permute-start.6 = (s16[192,512]{1,0:T(8,128)(2,1)S(1)}, s16[192,512]{1,0:T(8,128)(2,1)S(1)}, u32[]{:S(2)}, u32[]{:S(2)}) collective-permute-start(s16[192,512]{1,0:T(8,128)(2,1)S(1)} %get-tuple-element.46), channel_id=1, source_target_pairs={{0,16},{16,32},{32,48},{48,64},{64,80},{80,96},{96,112},{112,128},... | collective-permute-start | bytes 589832 | tf_op jit(solution)/shard_map/ppermute | solution.py:331
  123.1 9.7 %collective-permute-start.7 = (s16[192,512]{1,0:T(8,128)(2,1)S(1)}, s16[192,512]{1,0:T(8,128)(2,1)S(1)}, u32[]{:S(2)}, u32[]{:S(2)}) collective-permute-start(s16[192,512]{1,0:T(8,128)(2,1)S(1)} %get-tuple-element.47), channel_id=1, source_target_pairs={{16,0},{32,16},{48,32},{64,48},{80,64},{96,80},{112,96},{128,112},... | collective-permute-start | bytes 589832 | tf_op jit(solution)/shard_map/ppermute | solution.py:332

commit v3 on v2

--- a/solution.py
+++ b/solution.py
@@ -12,8 +12,9 @@
 FLOOR = 0.02
 TILE = 128
 SIDE = W // TILE
-TILES = tuple((p, q) for p in range(SIDE) for q in range(p + 1))
-NT = len(TILES)
+UPPER = tuple((p, q) for p in range(SIDE) for q in range(p, SIDE))
+LOWER = tuple((p, q) for p in range(SIDE) for q in range(p + 1))
+NT = len(UPPER)
 CODE = 32000.0
 HALF = 32768
 f32, bf16, i16, i32 = jnp.float32, jnp.bfloat16, jnp.int16, jnp.int32
@@ -44,44 +45,51 @@
     return pltpu.VMEM(dims, dtype)
 
 
-def pack_products(gram, block, put, peers):
+def tile_of(matrix, p, q):
+    return matrix[p * TILE : (p + 1) * TILE, q * TILE : (q + 1) * TILE]
+
+
+def pack_tiles(gram, tiles, put, peers):
     rows = TILE // peers
-    pieces = [
-        gram[p * TILE : (p + 1) * TILE, q * TILE : (q + 1) * TILE].reshape(peers, rows, TILE) for p, q in TILES
-    ]
-    ones = jnp.ones((8, block.shape[0]), bf16)
-    sums = dot(ones, block)[:1]
-    squares = dot(ones, block * block)[:1]
-    stats = [v[:, q * TILE : (q + 1) * TILE] for v in (sums, squares) for q in range(SIDE)]
-    stats = jnp.concatenate(stats + [jnp.zeros((8, TILE), f32)], axis=0)
-    for u in range(NT // 2):
+    pieces = [tile_of(gram, p, q).reshape(peers, rows, TILE) for p, q in tiles]
+    for u in range(len(tiles) // 2):
         pair = jnp.concatenate(pieces[2 * u : 2 * u + 2], axis=1)
         put(2 * rows * u, pair.astype(i32).astype(i16))
-    stats = jnp.broadcast_to(stats.astype(i32).astype(i16)[None], (peers, *stats.shape))
-    put(NT * rows, stats)
-
-
-def own_products(x_ref, out_ref, turned_ref):
+
+
+def products(left, right):
+    return lax.dot_general(left, right, (((0,), (0,)), ((), ())), preferred_element_type=f32)
+
+
+def on_diagonal():
+    return lax.broadcasted_iota(i32, (TILE, TILE), 0) == lax.broadcasted_iota(i32, (TILE, TILE), 1)
+
+
+def own_products(x_ref, out_ref):
     block = x_ref[...]
-    turned = block.T
-    turned_ref[...] = turned
     near, depth = out_ref.shape[0], out_ref.shape[1] // 2
+    peers = 2 * near
 
     def put(at, value):
         for far in range(2):
             lo = far * depth + at
             out_ref[:, lo : lo + value.shape[1], :] = value[far * near : (far + 1) * near]
 
-    pack_products(dot(turned, block), block, put, 2 * near)
-
-
-def next_products(turned_ref, x_ref, out_ref):
-    block = x_ref[...]
-
+    gram = products(block, block)
+    pack_tiles(gram, UPPER, put, peers)
+    sums = dot(jnp.ones((8, block.shape[0]), bf16), block)[:1]
+    here = on_diagonal()
+    stats = [sums[:, q * TILE : (q + 1) * TILE] for q in range(SIDE)]
+    stats += [jnp.sum(jnp.where(here, tile_of(gram, q, q), 0.0), axis=0, keepdims=True) for q in range(SIDE)]
+    stats = jnp.concatenate(stats + [jnp.zeros((8, TILE), f32)], axis=0)
+    put(NT * TILE // peers, jnp.broadcast_to(stats.astype(i32).astype(i16)[None], (peers, 16, TILE)))
+
+
+def next_products(x_ref, next_ref, out_ref):
     def put(at, value):
         out_ref[:, at : at + value.shape[1], :] = value
 
-    pack_products(dot(turned_ref[...], block), block, put, out_ref.shape[0])
+    pack_tiles(products(x_ref[...], next_ref[...]), LOWER, put, out_ref.shape[0])
 
 
 def fold(me_ref, came_ref, keep_ref, send_ref):
@@ -99,39 +107,48 @@
     send_ref[...] = (total(1 - far) - HALF).astype(i16)
 
 
-def correlate(samples, me_ref, keep_ref, far_ref, next_ref, out_ref):
+def correlate(samples, me_ref, keep_ref, far_ref, stats_ref, next_ref, out_ref, diagonal_ref):
     peers = next_ref.shape[0]
     rows = TILE // peers
-
-    def stats(means):
-        mean = means[NT * rows : NT * rows + SIDE]
-        square = means[NT * rows + SIDE : NT * rows + 2 * SIDE]
-        return mean, 1.0 / jnp.sqrt(jnp.maximum(square - mean * mean, FLOOR))
-
     own = keep_ref[...] + far_ref[...].astype(i32) + HALF
     nxt = next_ref[0].astype(i32)
     for k in range(1, peers):
         nxt = nxt + next_ref[k].astype(i32)
     own, nxt = own.astype(f32) / samples, nxt.astype(f32) / samples
-    own_stats, next_stats = stats(own), stats(nxt)
+
+    def stats(means):
+        mean, square = means[:SIDE], means[SIDE : 2 * SIDE]
+        variance = square - mean * mean
+        return mean, variance, 1.0 / jnp.sqrt(jnp.maximum(variance, FLOOR))
+
+    mean, variance, scale = stats(own[NT * rows :])
+    next_mean, _, next_scale = stats(stats_ref[...].astype(f32) / samples)
+    diagonal_ref[...] = jnp.concatenate([variance * scale * scale, jnp.zeros((8 - SIDE, TILE), f32)], axis=0)
     lane = lax.broadcasted_iota(i32, (rows, TILE), 1)
     row = lax.broadcasted_iota(i32, (rows, TILE), 0) + me_ref[0] * rows
 
     def at_rows(vector, p):
         return jnp.sum(jnp.where(lane == row, vector[p : p + 1], 0.0), axis=1, keepdims=True)
 
-    row_mean = [at_rows(own_stats[0], p) for p in range(SIDE)]
-    row_scale = [at_rows(own_stats[1], p) * CODE for p in range(SIDE)]
-    base = 0
-    for means, (mean, scale) in ((own, own_stats), (nxt, next_stats)):
-        codes = []
-        for t, (p, q) in enumerate(TILES):
-            cov = means[t * rows : (t + 1) * rows] - row_mean[p] * mean[q : q + 1]
-            codes.append(jnp.round(cov * row_scale[p] * scale[q : q + 1]))
-        codes = jnp.concatenate(codes, axis=0).astype(i32).astype(i16)
-        for k in range(peers):
-            out_ref[k, base : base + NT * rows, :] = codes
-        base += NT * rows
+    row_mean = [at_rows(mean, p) for p in range(SIDE)]
+    row_scale = [at_rows(scale, p) * CODE for p in range(SIDE)]
+
+    def code(means, t, p, q, col_mean, col_scale):
+        cov = means[t * rows : (t + 1) * rows] - row_mean[p] * col_mean[q : q + 1]
+        return jnp.round(cov * row_scale[p] * col_scale[q : q + 1])
+
+    upper = {(p, q): code(own, t, p, q, mean, scale) for t, (p, q) in enumerate(UPPER)}
+    lower = {(p, q): code(nxt, t, p, q, next_mean, next_scale) for t, (p, q) in enumerate(LOWER)}
+    codes = []
+    for p in range(SIDE):
+        for q in range(SIDE):
+            if p == q:
+                codes.append(jnp.where(lane > row, upper[p, q], lower[p, q]))
+            else:
+                codes.append(upper[p, q] if p < q else lower[p, q])
+    codes = jnp.concatenate(codes, axis=0).astype(i32).astype(i16)
+    for k in range(peers):
+        out_ref[k] = codes
 
 
 def taper(p, q, shift):
@@ -141,35 +158,45 @@
     return jnp.maximum(1.0 - reach / (W + 1), 0.0)
 
 
-def unpack(codes_ref, near_high, near_low, next_high, next_low, back_high, back_low):
+def unpack(codes_ref, diagonal_ref, near_high, near_low, next_high, next_low, back_high, back_low):
     peers = codes_ref.shape[0]
     rows = TILE // peers
-
-    def tiles(base):
-        for u in range(NT // 2):
-            lo = base + 2 * rows * u
-            pair = codes_ref[:, lo : lo + 2 * rows, :].astype(i32).astype(f32)
-            yield TILES[2 * u], pair[:, :rows].reshape(TILE, TILE)
-            yield TILES[2 * u + 1], pair[:, rows:].reshape(TILE, TILE)
 
     def put(high_ref, low_ref, p, q, value):
         high, low = halves(value)
         high_ref[p * TILE : (p + 1) * TILE, q * TILE : (q + 1) * TILE] = high
         low_ref[p * TILE : (p + 1) * TILE, q * TILE : (q + 1) * TILE] = low
 
-    for (p, q), code in tiles(0):
+    def put_near(p, q, code):
         value = code * (taper(p, q, 0) * (1.0 / CODE))
-        put(near_high, near_low, p, q, value)
-        if p != q:
+        if p == q:
+            value = value + value.T
+            value = jnp.where(on_diagonal(), diagonal_ref[p : p + 1, :], value)
+            put(near_high, near_low, p, q, value)
+        else:
+            put(near_high, near_low, p, q, value)
             put(near_high, near_low, q, p, value.T)
-    zero = jnp.zeros((TILE, TILE), f32)
-    for (p, q), code in tiles(NT * rows):
+
+    def put_next(p, q, code):
         value = code * (taper(p, q, W) * (1.0 / CODE))
         put(next_high, next_low, p, q, value)
         put(back_high, back_low, q, p, value.T)
-        if p != q:
-            put(next_high, next_low, q, p, zero)
-            put(back_high, back_low, p, q, zero)
+
+    strict = lax.broadcasted_iota(i32, (TILE, TILE), 0) < lax.broadcasted_iota(i32, (TILE, TILE), 1)
+    zero = jnp.zeros((TILE, TILE), f32)
+    for p in range(SIDE):
+        for u in range(SIDE // 2):
+            lo = 2 * rows * (p * SIDE // 2 + u)
+            pair = codes_ref[:, lo : lo + 2 * rows, :].astype(i32).astype(f32)
+            for q, code in ((2 * u, pair[:, :rows]), (2 * u + 1, pair[:, rows:])):
+                code = code.reshape(TILE, TILE)
+                if p <= q:
+                    put_near(p, q, jnp.where(strict, code, 0.0) if p == q else code)
+                if p >= q:
+                    put_next(p, q, code)
+                else:
+                    put(next_high, next_low, p, q, zero)
+                    put(back_high, back_low, q, p, zero)
 
 
 def product(v, high_ref, low_ref):
@@ -299,30 +326,34 @@
 
     dosage = genotypes.astype(bf16)
     next_dosage = lax.ppermute(dosage, "genome", to_left)
-    own, turned = call(
-        own_products,
-        (shape(near, 2 * depth, TILE, dtype=i16), shape(variants, local_samples, dtype=bf16)),
-        dosage,
-    )
+    own = call(own_products, shape(near, 2 * depth, TILE, dtype=i16), dosage)
     own = lax.all_to_all(own, "cols", 0, 0, axis_index_groups=sides)
     me = lax.axis_index("cols").astype(i32).reshape(1)
     keep, far = call(fold, (shape(depth, TILE, dtype=i32), shape(depth, TILE, dtype=i16)), me, own)
-    far = lax.ppermute(far, "cols", [(k, (k + near) % peers) for k in cols])
     z = z_scores.T
     vector = shape(*z.shape)
     code = shape(z.shape[0] // 16 * 16 + 16, z.shape[1], dtype=i16)
     z_code = call(start_code, code, z)
-    far, next_dosage, z_code = lax.optimization_barrier((far, next_dosage, z_code))
-    nxt = call(next_products, shape(peers, depth, TILE, dtype=i16), turned, next_dosage)
-    z_code, nxt = lax.optimization_barrier((z_code, nxt))
+    keep, next_dosage = lax.optimization_barrier((keep, next_dosage))
+    nxt = call(next_products, shape(peers, NT * rows, TILE, dtype=i16), dosage, next_dosage)
+    far, z_code, nxt = lax.optimization_barrier((far, z_code, nxt))
     nxt = lax.all_to_all(nxt, "cols", 0, 0)
+    far = lax.ppermute(far, "cols", [(k, (k + near) % peers) for k in cols])
+    stats = keep[NT * rows : NT * rows + 8] + far[NT * rows : NT * rows + 8].astype(i32) + HALF
+    next_stats = lax.ppermute(stats, "genome", to_left)
     z_next = lax.ppermute(z_code, "genome", to_left)
-    codes = call(
-        functools.partial(correlate, samples), shape(peers, 2 * NT * rows, TILE, dtype=i16), me, keep, far, nxt
+    codes, diagonal_row = call(
+        functools.partial(correlate, samples),
+        (shape(peers, SIDE * SIDE * rows, TILE, dtype=i16), shape(8, TILE)),
+        me,
+        keep,
+        far,
+        next_stats,
+        nxt,
     )
     codes = lax.all_to_all(codes, "cols", 0, 0)
     square = shape(W, W, dtype=bf16)
-    near_h, near_l, next_h, next_l, back_h, back_l = call(unpack, (square,) * 6, codes)
+    near_h, near_l, next_h, next_l, back_h, back_l = call(unpack, (square,) * 6, codes, diagonal_row)
 
     def step(part, came, nxt):
         w, left, right = call(

time: 155 us -> 158 us (1.019)
  starting transfers between devices: 46.2 us -> 61.4 us
  blocking collectives: 41.5 us -> 29.7 us
  local copies, waits for them, and re-layouts: 2.81 us -> 0.01 us
  waiting for transfers between devices: 46.2 us -> 47.8 us
    all_to_all x1 -> x0, blocking collectives: 21.7 us -> none  [shards(): nxt = lax.all_to_all(nxt, 'cols', 0, 0)]
    all_to_all x0 -> x1, starting transfers between devices: none -> 12.7 us  [shards(): nxt = lax.all_to_all(nxt, 'cols', 0, 0)]
    all_to_all x1, blocking collectives: 19.9 us -> 29.7 us  [shards(): moments = lax.all_to_all(moments, 'genome', 0, 0)]
    all_to_all x1, starting transfers between devices: 5.43 us -> 11.1 us  [shards(): codes = lax.all_to_all(codes, 'cols', 0, 0)]
    ppermute x0 -> x1, waiting for transfers between devices: none -> 3 us  [shards(): next_stats = lax.ppermute(stats, 'genome', to_left)]
    unnamed x6 -> x2, local copies, waits for them, and re-layouts: 2.81 us -> 0.01 us
    ppermute x2, waiting for transfers between devices: 11.2 us -> 8.93 us  [step(): nxt = lax.ppermute(left, 'genome', to_left)]
    ppermute x0 -> x1, starting transfers between devices: none -> 1.91 us  [shards(): next_stats = lax.ppermute(stats, 'genome', to_left)]
  transfers between devices with their start and end apart: 10 -> 12, of which waited for: 7 -> 8; matrix products, arithmetic and copies ran while one was open for 0% -> 0% of each run, Pallas kernels for 4% -> 4%
where the time goes in v3:
time: 158 us; the launch traced here: 157 us
  starting transfers between devices  61.4 us (39%)
  waiting for transfers between devices  47.8 us (30%)
  blocking collectives  29.7 us (19%)
  Pallas kernels  14.5 us (9%)
  other arithmetic  2.65 us (2%)
    all_to_all x1, blocking collectives, shards(): moments = lax.all_to_all(moments, 'genome', 0, 0)  29.7 us
    all_to_all x1, waiting for transfers between devices, shards(): codes = lax.all_to_all(codes, 'cols', 0, 0)  16.4 us
    all_to_all x1, waiting for transfers between devices, shards(): own = lax.all_to_all(own, 'cols', 0, 0, axis_index_groups=sides)  14.8 us
    pallas_call x15, Pallas kernels, call(): pl.pallas_call(kernel, out_shape=outs, in_specs=[pl.BlockSpec(memory_spac...  14.5 us
    all_to_all x1, starting transfers between devices, shards(): nxt = lax.all_to_all(nxt, 'cols', 0, 0)  12.7 us
    all_to_all x1, starting transfers between devices, shards(): codes = lax.all_to_all(codes, 'cols', 0, 0)  11.1 us
    ppermute x2, waiting for transfers between devices, step(): nxt = lax.ppermute(left, 'genome', to_left)  8.93 us
    ppermute x1, starting transfers between devices, shards(): next_dosage = lax.ppermute(dosage, 'genome', to_left)  8.88 us
  transfers between devices with their start and end apart: 12, of which 8 were waited for; matrix products, arithmetic and copies ran while one was open for 0% of the time, Pallas kernels for 4%

profile of v3, /device:TPU:1, one launch (start us, length us, event | category | flops | bytes accessed | tf_op | source)
XLA Modules:
  0.0 156.8 jit_solution(17492855689437368132)
XLA Ops:
  0.6 2.6 %convert_element_type.6.x_ref = bf16[1920,512]{1,0:T(8,128)(2,1)S(1)} convert(s32[1920,512]{1,0:T(8,128)} %param.2) | non-fusion elementwise | flops 983040 | bytes 5898240 | tf_op jit(solution)/shard_map/convert_element_type | solution.py:327
  3.3 0.0 copy-start
  3.3 8.9 %collective-permute-start = (bf16[1920,512]{1,0:T(8,128)(2,1)S(1)}, bf16[1920,512]{1,0:T(8,128)(2,1)}, u32[]{:S(2)}, u32[]{:S(2)}) collective-permute-start(bf16[1920,512]{1,0:T(8,128)(2,1)S(1)} %convert_element_type.6.x_ref), channel_id=1, source_target_pairs={{16,0},{32,16},{48,32},{64,48},{80,64},{96,80},{112,96},{128,112},... | collective-permute-start | bytes 5898248 | tf_op jit(solution)/shard_map/ppermute | solution.py:328
  12.2 2.3 %shard_map.41 = s16[8,192,128]{2,1,0:T(8,128)(2,1)} custom-call(bf16[1920,512]{1,0:T(8,128)(2,1)S(1)} %convert_element_type.6.x_ref), custom_call_target="tpu_custom_call" | custom-call | tf_op jit(solution)/shard_map/pallas_call | solution.py:35
  14.4 3.5 %all-to-all-start = ((s16[8,192,128]{2,1,0:T(8,128)(2,1)}), s16[8,192,128]{2,1,0:T(8,128)(2,1)S(1)}, u32[]{:S(2)}, u32[]{:S(2)}) async-start(s16[8,192,128]{2,1,0:T(8,128)(2,1)} %shard_map.41), calls=%async_computation | async-start | bytes 786432 | tf_op jit(solution)/shard_map/all_to_all | solution.py:330
  17.9 0.0 copy-done
  17.9 0.2 shard_map.43
  18.1 14.8 %all-to-all-done.came_ref = s16[8,192,128]{2,1,0:T(8,128)(2,1)S(1)} async-done(((s16[8,192,128]{2,1,0:T(8,128)(2,1)}), s16[8,192,128]{2,1,0:T(8,128)(2,1)S(1)}, u32[]{:S(2)}, u32[]{:S(2)}) %all-to-all-start) | async-done | bytes 393248 | tf_op jit(solution)/shard_map/all_to_all | solution.py:330
  32.9 0.1 shard_map.42
  33.0 0.0 collective-permute-done.next_ref
  33.0 3.6 %shard_map.44 = s16[16,80,128]{2,1,0:T(8,128)(2,1)} custom-call(bf16[1920,512]{1,0:T(8,128)(2,1)S(1)} %convert_element_type.6.x_ref, bf16[1920,512]{1,0:T(8,128)(2,1)} %collective-permute-done.next_ref), custom_call_target="tpu_custom_call" | custom-call | tf_op jit(solution)/shard_map/pallas_call | solution.py:35
  36.5 12.7 %all-to-all-start.1 = ((s16[16,80,128]{2,1,0:T(8,128)(2,1)}), s16[16,80,128]{2,1,0:T(8,128)(2,1)S(1)}, u32[]{:S(2)}, u32[]{:S(2)}) async-start(s16[16,80,128]{2,1,0:T(8,128)(2,1)} %shard_map.44), calls=%async_computation.1 | async-start | bytes 655360 | tf_op jit(solution)/shard_map/all_to_all | solution.py:340
  49.2 7.2 %collective-permute-start.1 = (s16[96,128]{1,0:T(8,128)(2,1)S(1)}, s16[96,128]{1,0:T(8,128)(2,1)S(1)}, u32[]{:S(2)}, u32[]{:S(2)}) collective-permute-start(s16[96,128]{1,0:T(8,128)(2,1)S(1)} %get-tuple-element.31), channel_id=1, source_target_pairs={{0,8},{1,9},{2,10},{3,11},{4,12},{5,13},{6,14},{7,15},{8,0},{9,1},... | collective-permute-start | bytes 73736 | tf_op jit(solution)/shard_map/ppermute | solution.py:341
  56.4 2.4 %collective-permute-done.1.far_ref = s16[96,128]{1,0:T(8,128)(2,1)S(1)} collective-permute-done((s16[96,128]{1,0:T(8,128)(2,1)S(1)}, s16[96,128]{1,0:T(8,128)(2,1)S(1)}, u32[]{:S(2)}, u32[]{:S(2)}) %collective-permute-start.1) | collective-permute-done | bytes 24608 | tf_op jit(solution)/shard_map/ppermute | solution.py:341
  58.9 1.9 %collective-permute-start.2 = (s32[8,128]{1,0:T(8,128)S(1)}, s32[8,128]{1,0:T(8,128)S(1)}, u32[]{:S(2)}, u32[]{:S(2)}) collective-permute-start(s32[8,128]{1,0:T(8,128)S(1)} %add_add_fusion), channel_id=1, source_target_pairs={{16,0},{32,16},{48,32},{64,48},{80,64},{96,80},{112,96},{128,112},... | collective-permute-start | bytes 12296 | tf_op jit(solution)/shard_map/ppermute | solution.py:343
  60.8 3.0 %collective-permute-done.2.stats_ref = s32[8,128]{1,0:T(8,128)S(1)} collective-permute-done((s32[8,128]{1,0:T(8,128)S(1)}, s32[8,128]{1,0:T(8,128)S(1)}, u32[]{:S(2)}, u32[]{:S(2)}) %collective-permute-start.2) | collective-permute-done | bytes 4128 | tf_op jit(solution)/shard_map/ppermute | solution.py:343
  63.8 0.0 all-to-all-done.1.next_ref
  63.8 1.0 shard_map.45
  64.8 11.1 %all-to-all-start.2 = ((s16[16,128,128]{2,1,0:T(8,128)(2,1)}), s16[16,128,128]{2,1,0:T(8,128)(2,1)S(1)}, u32[]{:S(2)}, u32[]{:S(2)}) async-start(s16[16,128,128]{2,1,0:T(8,128)(2,1)} %get-tuple-element.33), calls=%async_computation.2 | async-start | bytes 1048576 | tf_op jit(solution)/shard_map/all_to_all | solution.py:354
  75.8 1.9 %collective-permute-start.4 = (s16[192,512]{1,0:T(8,128)(2,1)S(1)}, s16[192,512]{1,0:T(8,128)(2,1)S(1)}, u32[]{:S(2)}, u32[]{:S(2)}) collective-permute-start(s16[192,512]{1,0:T(8,128)(2,1)S(1)} %shard_map.43), channel_id=1, source_target_pairs={{16,0},{32,16},{48,32},{64,48},{80,64},{96,80},{112,96},{128,112},... | collective-permute-start | bytes 589832 | tf_op jit(solution)/shard_map/ppermute | solution.py:344
  77.8 16.4 %all-to-all-done.2.codes_ref = s16[16,128,128]{2,1,0:T(8,128)(2,1)S(1)} async-done(((s16[16,128,128]{2,1,0:T(8,128)(2,1)}), s16[16,128,128]{2,1,0:T(8,128)(2,1)S(1)}, u32[]{:S(2)}, u32[]{:S(2)}) %all-to-all-start.2) | async-done | bytes 524320 | tf_op jit(solution)/shard_map/all_to_all | solution.py:354
  94.1 0.9 shard_map.46
  95.1 0.6 shard_map.48
  95.7 3.6 %collective-permute-start.3 = (s16[192,512]{1,0:T(8,128)(2,1)S(1)}, s16[192,512]{1,0:T(8,128)(2,1)S(1)}, u32[]{:S(2)}, u32[]{:S(2)}) collective-permute-start(s16[192,512]{1,0:T(8,128)(2,1)S(1)} %shard_map.48), channel_id=1, source_target_pairs={{0,16},{16,32},{32,48},{48,64},{64,80},{80,96},{96,112},{112,128},... | collective-permute-start | bytes 589832 | tf_op jit(solution)/shard_map/ppermute | solution.py:366
  99.3 0.5 shard_map.47.part_ref
  99.8 0.0 collective-permute-done.4.next_ref
  99.8 2.1 %collective-permute-done.3.came_ref = s16[192,512]{1,0:T(8,128)(2,1)S(1)} collective-permute-done((s16[192,512]{1,0:T(8,128)(2,1)S(1)}, s16[192,512]{1,0:T(8,128)(2,1)S(1)}, u32[]{:S(2)}, u32[]{:S(2)}) %collective-permute-start.3) | collective-permute-done | bytes 196640 | tf_op jit(solution)/shard_map/ppermute | solution.py:366
  101.9 1.1 shard_map.49
  103.0 4.4 %collective-permute-start.5 = (s16[192,512]{1,0:T(8,128)(2,1)S(1)}, s16[192,512]{1,0:T(8,128)(2,1)S(1)}, u32[]{:S(2)}, u32[]{:S(2)}) collective-permute-start(s16[192,512]{1,0:T(8,128)(2,1)S(1)} %get-tuple-element.43), channel_id=1, source_target_pairs={{0,16},{16,32},{32,48},{48,64},{64,80},{80,96},{96,112},{112,128},... | collective-permute-start | bytes 589832 | tf_op jit(solution)/shard_map/ppermute | solution.py:362
  107.4 1.9 %collective-permute-start.6 = (s16[192,512]{1,0:T(8,128)(2,1)S(1)}, s16[192,512]{1,0:T(8,128)(2,1)S(1)}, u32[]{:S(2)}, u32[]{:S(2)}) collective-permute-start(s16[192,512]{1,0:T(8,128)(2,1)S(1)} %get-tuple-element.44), channel_id=1, source_target_pairs={{16,0},{32,16},{48,32},{64,48},{80,64},{96,80},{112,96},{128,112},... | collective-permute-start | bytes 589832 | tf_op jit(solution)/shard_map/ppermute | solution.py:363
  109.3 0.5 shard_map.50.part_ref
  109.8 0.2 collective-permute-done.5.came_ref
  110.0 4.4 %collective-permute-done.6.next_ref = s16[192,512]{1,0:T(8,128)(2,1)S(1)} collective-permute-done((s16[192,512]{1,0:T(8,128)(2,1)S(1)}, s16[192,512]{1,0:T(8,128)(2,1)S(1)}, u32[]{:S(2)}, u32[]{:S(2)}) %collective-permute-start.6) | collective-permute-done | bytes 196640 | tf_op jit(solution)/shard_map/ppermute | solution.py:363
  114.4 1.1 shard_map.51
  115.5 1.9 %collective-permute-start.7 = (s16[192,512]{1,0:T(8,128)(2,1)S(1)}, s16[192,512]{1,0:T(8,128)(2,1)S(1)}, u32[]{:S(2)}, u32[]{:S(2)}) collective-permute-start(s16[192,512]{1,0:T(8,128)(2,1)S(1)} %get-tuple-element.46), channel_id=1, source_target_pairs={{0,16},{16,32},{32,48},{48,64},{64,80},{80,96},{96,112},{112,128},... | collective-permute-start | bytes 589832 | tf_op jit(solution)/shard_map/ppermute | solution.py:362
  117.4 2.4 %collective-permute-start.8 = (s16[192,512]{1,0:T(8,128)(2,1)S(1)}, s16[192,512]{1,0:T(8,128)(2,1)S(1)}, u32[]{:S(2)}, u32[]{:S(2)}) collective-permute-start(s16[192,512]{1,0:T(8,128)(2,1)S(1)} %get-tuple-element.47), channel_id=1, source_target_pairs={{16,0},{32,16},{48,32},{64,48},{80,64},{96,80},{112,96},{128,112},... | collective-permute-start | bytes 589832 | tf_op jit(solution)/shard_map/ppermute | solution.py:363
  119.9 0.5 shard_map.52.part_ref
  120.4 0.2 shard_map.53.early_ref
  120.6 0.0 collective-permute-done.7.came_ref
  120.6 4.5 %collective-permute-done.8.next_ref = s16[192,512]{1,0:T(8,128)(2,1)S(1)} collective-permute-done((s16[192,512]{1,0:T(8,128)(2,1)S(1)}, s16[192,512]{1,0:T(8,128)(2,1)S(1)}, u32[]{:S(2)}, u32[]{:S(2)}) %collective-permute-start.8) | collective-permute-done | bytes 196640 | tf_op jit(solution)/shard_map/ppermute | solution.py:363
  125.1 0.7 shard_map.54
  125.8 29.7 %all_to_all.20.moments_ref = f32[32,8,256]{2,1,0:T(8,128)S(1)} all-to-all(f32[32,8,256]{2,1,0:T(8,128)S(1)} %get-tuple-element.48), channel_id=1, replica_groups=mesh['genome'=32,'cols'=16] {'genome'}, dimensions={0} | all-to-all | bytes 524288 | tf_op jit(solution)/shard_map/all_to_all | solution.py:373
  155.4 1.4 shard_map.55
  (1 shorter events, 0.0 us)
Async XLA Ops:
  3.3 14.6 %copy-start = (f32[512,184]{0,1:T(8,128)S(1)}, f32[512,184]{0,1:T(8,128)}, u32[]{:S(2)}) copy-start(f32[512,184]{0,1:T(8,128)} %param.3) | copy-start | bytes 1130500
  3.3 29.7 %collective-permute-start = (bf16[1920,512]{1,0:T(8,128)(2,1)S(1)}, bf16[1920,512]{1,0:T(8,128)(2,1)}, u32[]{:S(2)}, u32[]{:S(2)}) collective-permute-start(bf16[1920,512]{1,0:T(8,128)(2,1)S(1)} %convert_element_type.6.x_ref), channel_id=1, source_target_pairs={{16,0},{32,16},{48,32},{64,48},{80,64},{96,80},{112,96},{128,112},... | collective-permute-start | bytes 5898248 | tf_op jit(solution)/shard_map/ppermute | solution.py:328
  14.4 18.5 %all-to-all-start = ((s16[8,192,128]{2,1,0:T(8,128)(2,1)}), s16[8,192,128]{2,1,0:T(8,128)(2,1)S(1)}, u32[]{:S(2)}, u32[]{:S(2)}) async-start(s16[8,192,128]{2,1,0:T(8,128)(2,1)} %shard_map.41), calls=%async_computation | async-start | bytes 786432 | tf_op jit(solution)/shard_map/all_to_all | solution.py:330
  36.5 27.3 %all-to-all-start.1 = ((s16[16,80,128]{2,1,0:T(8,128)(2,1)}), s16[16,80,128]{2,1,0:T(8,128)(2,1)S(1)}, u32[]{:S(2)}, u32[]{:S(2)}) async-start(s16[16,80,128]{2,1,0:T(8,128)(2,1)} %shard_map.44), calls=%async_computation.1 | async-start | bytes 655360 | tf_op jit(solution)/shard_map/all_to_all | solution.py:340
  49.2 9.6 %collective-permute-start.1 = (s16[96,128]{1,0:T(8,128)(2,1)S(1)}, s16[96,128]{1,0:T(8,128)(2,1)S(1)}, u32[]{:S(2)}, u32[]{:S(2)}) collective-permute-start(s16[96,128]{1,0:T(8,128)(2,1)S(1)} %get-tuple-element.31), channel_id=1, source_target_pairs={{0,8},{1,9},{2,10},{3,11},{4,12},{5,13},{6,14},{7,15},{8,0},{9,1},... | collective-permute-start | bytes 73736 | tf_op jit(solution)/shard_map/ppermute | solution.py:341
  58.9 4.9 %collective-permute-start.2 = (s32[8,128]{1,0:T(8,128)S(1)}, s32[8,128]{1,0:T(8,128)S(1)}, u32[]{:S(2)}, u32[]{:S(2)}) collective-permute-start(s32[8,128]{1,0:T(8,128)S(1)} %add_add_fusion), channel_id=1, source_target_pairs={{16,0},{32,16},{48,32},{64,48},{80,64},{96,80},{112,96},{128,112},... | collective-permute-start | bytes 12296 | tf_op jit(solution)/shard_map/ppermute | solution.py:343
  64.8 29.4 %all-to-all-start.2 = ((s16[16,128,128]{2,1,0:T(8,128)(2,1)}), s16[16,128,128]{2,1,0:T(8,128)(2,1)S(1)}, u32[]{:S(2)}, u32[]{:S(2)}) async-start(s16[16,128,128]{2,1,0:T(8,128)(2,1)} %get-tuple-element.33), calls=%async_computation.2 | async-start | bytes 1048576 | tf_op jit(solution)/shard_map/all_to_all | solution.py:354
  75.8 24.0 %collective-permute-start.4 = (s16[192,512]{1,0:T(8,128)(2,1)S(1)}, s16[192,512]{1,0:T(8,128)(2,1)S(1)}, u32[]{:S(2)}, u32[]{:S(2)}) collective-permute-start(s16[192,512]{1,0:T(8,128)(2,1)S(1)} %shard_map.43), channel_id=1, source_target_pairs={{16,0},{32,16},{48,32},{64,48},{80,64},{96,80},{112,96},{128,112},... | collective-permute-start | bytes 589832 | tf_op jit(solution)/shard_map/ppermute | solution.py:344
  95.7 6.2 %collective-permute-start.3 = (s16[192,512]{1,0:T(8,128)(2,1)S(1)}, s16[192,512]{1,0:T(8,128)(2,1)S(1)}, u32[]{:S(2)}, u32[]{:S(2)}) collective-permute-start(s16[192,512]{1,0:T(8,128)(2,1)S(1)} %shard_map.48), channel_id=1, source_target_pairs={{0,16},{16,32},{32,48},{48,64},{64,80},{80,96},{96,112},{112,128},... | collective-permute-start | bytes 589832 | tf_op jit(solution)/shard_map/ppermute | solution.py:366
  103.0 7.0 %collective-permute-start.5 = (s16[192,512]{1,0:T(8,128)(2,1)S(1)}, s16[192,512]{1,0:T(8,128)(2,1)S(1)}, u32[]{:S(2)}, u32[]{:S(2)}) collective-permute-start(s16[192,512]{1,0:T(8,128)(2,1)S(1)} %get-tuple-element.43), channel_id=1, source_target_pairs={{0,16},{16,32},{32,48},{48,64},{64,80},{80,96},{96,112},{112,128},... | collective-permute-start | bytes 589832 | tf_op jit(solution)/shard_map/ppermute | solution.py:362
  107.4 7.0 %collective-permute-start.6 = (s16[192,512]{1,0:T(8,128)(2,1)S(1)}, s16[192,512]{1,0:T(8,128)(2,1)S(1)}, u32[]{:S(2)}, u32[]{:S(2)}) collective-permute-start(s16[192,512]{1,0:T(8,128)(2,1)S(1)} %get-tuple-element.44), channel_id=1, source_target_pairs={{16,0},{32,16},{48,32},{64,48},{80,64},{96,80},{112,96},{128,112},... | collective-permute-start | bytes 589832 | tf_op jit(solution)/shard_map/ppermute | solution.py:363
  115.5 5.1 %collective-permute-start.7 = (s16[192,512]{1,0:T(8,128)(2,1)S(1)}, s16[192,512]{1,0:T(8,128)(2,1)S(1)}, u32[]{:S(2)}, u32[]{:S(2)}) collective-permute-start(s16[192,512]{1,0:T(8,128)(2,1)S(1)} %get-tuple-element.46), channel_id=1, source_target_pairs={{0,16},{16,32},{32,48},{48,64},{64,80},{80,96},{96,112},{112,128},... | collective-permute-start | bytes 589832 | tf_op jit(solution)/shard_map/ppermute | solution.py:362
  117.4 7.7 %collective-permute-start.8 = (s16[192,512]{1,0:T(8,128)(2,1)S(1)}, s16[192,512]{1,0:T(8,128)(2,1)S(1)}, u32[]{:S(2)}, u32[]{:S(2)}) collective-permute-start(s16[192,512]{1,0:T(8,128)(2,1)S(1)} %get-tuple-element.47), channel_id=1, source_target_pairs={{16,0},{32,16},{48,32},{64,48},{80,64},{96,80},{112,96},{128,112},... | collective-permute-start | bytes 589832 | tf_op jit(solution)/shard_map/ppermute | solution.py:363

commit v4 on v3

--- a/solution.py
+++ b/solution.py
@@ -6,6 +6,7 @@
 from jax.experimental import pallas as pl
 from jax.experimental.pallas import tpu as pltpu
 from jax.sharding import PartitionSpec as P
+
 
 W = 512
 RIDGE = 0.1
@@ -57,12 +58,16 @@
         put(2 * rows * u, pair.astype(i32).astype(i16))
 
 
-def products(left, right):
-    return lax.dot_general(left, right, (((0,), (0,)), ((), ())), preferred_element_type=f32)
-
-
 def on_diagonal():
     return lax.broadcasted_iota(i32, (TILE, TILE), 0) == lax.broadcasted_iota(i32, (TILE, TILE), 1)
+
+
+def sums(block, peers):
+    ones = jnp.ones((8, block.shape[0]), bf16)
+    both = (dot(ones, block)[:1], dot(ones, block * block)[:1])
+    stats = [v[:, q * TILE : (q + 1) * TILE] for v in both for q in range(SIDE)]
+    stats = jnp.concatenate(stats + [jnp.zeros((8, TILE), f32)], axis=0)
+    return jnp.broadcast_to(stats.astype(i32).astype(i16)[None], (peers, 16, TILE))
 
 
 def own_products(x_ref, out_ref):
@@ -75,21 +80,19 @@
             lo = far * depth + at
             out_ref[:, lo : lo + value.shape[1], :] = value[far * near : (far + 1) * near]
 
-    gram = products(block, block)
-    pack_tiles(gram, UPPER, put, peers)
-    sums = dot(jnp.ones((8, block.shape[0]), bf16), block)[:1]
-    here = on_diagonal()
-    stats = [sums[:, q * TILE : (q + 1) * TILE] for q in range(SIDE)]
-    stats += [jnp.sum(jnp.where(here, tile_of(gram, q, q), 0.0), axis=0, keepdims=True) for q in range(SIDE)]
-    stats = jnp.concatenate(stats + [jnp.zeros((8, TILE), f32)], axis=0)
-    put(NT * TILE // peers, jnp.broadcast_to(stats.astype(i32).astype(i16)[None], (peers, 16, TILE)))
+    pack_tiles(dot(block.T, block), UPPER, put, peers)
+    put(NT * TILE // peers, sums(block, peers))
 
 
 def next_products(x_ref, next_ref, out_ref):
+    block = next_ref[...]
+    peers = out_ref.shape[0]
+
     def put(at, value):
         out_ref[:, at : at + value.shape[1], :] = value
 
-    pack_tiles(products(x_ref[...], next_ref[...]), LOWER, put, out_ref.shape[0])
+    pack_tiles(dot(x_ref[...].T, block), LOWER, put, peers)
+    put(NT * TILE // peers, sums(block, peers))
 
 
 def fold(me_ref, came_ref, keep_ref, send_ref):
@@ -107,7 +110,7 @@
     send_ref[...] = (total(1 - far) - HALF).astype(i16)
 
 
-def correlate(samples, me_ref, keep_ref, far_ref, stats_ref, next_ref, out_ref, diagonal_ref):
+def correlate(samples, me_ref, keep_ref, far_ref, next_ref, out_ref, diagonal_ref):
     peers = next_ref.shape[0]
     rows = TILE // peers
     own = keep_ref[...] + far_ref[...].astype(i32) + HALF
@@ -122,7 +125,7 @@
         return mean, variance, 1.0 / jnp.sqrt(jnp.maximum(variance, FLOOR))
 
     mean, variance, scale = stats(own[NT * rows :])
-    next_mean, _, next_scale = stats(stats_ref[...].astype(f32) / samples)
+    next_mean, _, next_scale = stats(nxt[NT * rows :])
     diagonal_ref[...] = jnp.concatenate([variance * scale * scale, jnp.zeros((8 - SIDE, TILE), f32)], axis=0)
     lane = lax.broadcasted_iota(i32, (rows, TILE), 1)
     row = lax.broadcasted_iota(i32, (rows, TILE), 0) + me_ref[0] * rows
@@ -311,7 +314,7 @@
 
 
 def shards(genotypes, z_scores):
-    local_samples, variants = genotypes.shape
+    local_samples, _ = genotypes.shape
     blocks = lax.axis_size("genome")
     peers = lax.axis_size("cols")
     samples = local_samples * peers
@@ -334,13 +337,11 @@
     vector = shape(*z.shape)
     code = shape(z.shape[0] // 16 * 16 + 16, z.shape[1], dtype=i16)
     z_code = call(start_code, code, z)
-    keep, next_dosage = lax.optimization_barrier((keep, next_dosage))
-    nxt = call(next_products, shape(peers, NT * rows, TILE, dtype=i16), dosage, next_dosage)
-    far, z_code, nxt = lax.optimization_barrier((far, z_code, nxt))
+    far, next_dosage = lax.optimization_barrier((far, next_dosage))
+    far = lax.ppermute(far, "cols", [(k, (k + near) % peers) for k in cols])
+    nxt = call(next_products, shape(peers, depth, TILE, dtype=i16), dosage, next_dosage)
+    z_code, nxt = lax.optimization_barrier((z_code, nxt))
     nxt = lax.all_to_all(nxt, "cols", 0, 0)
-    far = lax.ppermute(far, "cols", [(k, (k + near) % peers) for k in cols])
-    stats = keep[NT * rows : NT * rows + 8] + far[NT * rows : NT * rows + 8].astype(i32) + HALF
-    next_stats = lax.ppermute(stats, "genome", to_left)
     z_next = lax.ppermute(z_code, "genome", to_left)
     codes, diagonal_row = call(
         functools.partial(correlate, samples),
@@ -348,7 +349,6 @@
         me,
         keep,
         far,
-        next_stats,
         nxt,
     )
     codes = lax.all_to_all(codes, "cols", 0, 0)

time: 158 us -> 152 us (0.962)
  blocking collectives: 29.7 us -> 22.4 us
  waiting for transfers between devices: 47.8 us -> 52.9 us
  starting transfers between devices: 61.4 us -> 57.6 us
    all_to_all x1, blocking collectives: 29.7 us -> 22.4 us  [shards(): moments = lax.all_to_all(moments, 'genome', 0, 0)]
    all_to_all x1, starting transfers between devices: 11.1 us -> 6.79 us  [shards(): codes = lax.all_to_all(codes, 'cols', 0, 0)]
    all_to_all x1, waiting for transfers between devices: 0.01 us -> 3.86 us  [shards(): nxt = lax.all_to_all(nxt, 'cols', 0, 0)]
    ppermute x2, waiting for transfers between devices: 8.93 us -> 12.2 us  [step(): nxt = lax.ppermute(left, 'genome', to_left)]
    ppermute x1 -> x0, waiting for transfers between devices: 3 us -> none  [shards(): next_stats = lax.ppermute(stats, 'genome', to_left)]
    ppermute x1, starting transfers between devices: 3.65 us -> 6.29 us  [shards(): lax.ppermute(call(outward, code, z, next_h, next_l), 'genome', to_right)]
    ppermute x1 -> x0, starting transfers between devices: 1.91 us -> none  [shards(): next_stats = lax.ppermute(stats, 'genome', to_left)]
  transfers between devices with their start and end apart: 12 -> 11, of which waited for: 8 -> 8; matrix products, arithmetic and copies ran while one was open for 0% -> 0% of each run, Pallas kernels for 4% -> 4%
where the time goes in v4:
time: 152 us
  starting transfers between devices  57.6 us (38%)
  waiting for transfers between devices  52.9 us (35%)
  blocking collectives  22.4 us (15%)
  Pallas kernels  15.2 us (10%)
  other arithmetic  2.65 us (2%)
    all_to_all x1, blocking collectives, shards(): moments = lax.all_to_all(moments, 'genome', 0, 0)  22.4 us
    all_to_all x1, waiting for transfers between devices, shards(): codes = lax.all_to_all(codes, 'cols', 0, 0)  16.9 us
    pallas_call x15, Pallas kernels, call(): pl.pallas_call(kernel, out_shape=outs, in_specs=[pl.BlockSpec(memory_spac...  15.2 us
    all_to_all x1, waiting for transfers between devices, shards(): own = lax.all_to_all(own, 'cols', 0, 0, axis_index_groups=sides)  14.8 us
    all_to_all x1, starting transfers between devices, shards(): nxt = lax.all_to_all(nxt, 'cols', 0, 0)  12.5 us
    ppermute x2, waiting for transfers between devices, step(): nxt = lax.ppermute(left, 'genome', to_left)  12.2 us
    ppermute x1, starting transfers between devices, shards(): next_dosage = lax.ppermute(dosage, 'genome', to_left)  8.88 us
    ppermute x1, starting transfers between devices, shards(): far = lax.ppermute(far, 'cols', [(k, (k + near) % peers) for k in cols])  7.17 us
  transfers between devices with their start and end apart: 11, of which 8 were waited for; matrix products, arithmetic and copies ran while one was open for 0% of the time, Pallas kernels for 4%

profile of v4, /device:TPU:1, one launch (start us, length us, event | category | flops | bytes accessed | tf_op | source)
XLA Modules:
  0.0 151.6 jit_solution(10620345448428974124)
XLA Ops:
  0.6 2.6 %convert_element_type.3.x_ref = bf16[1920,512]{1,0:T(8,128)(2,1)S(1)} convert(s32[1920,512]{1,0:T(8,128)} %param.2) | non-fusion elementwise | flops 983040 | bytes 5898240 | tf_op jit(solution)/shard_map/convert_element_type | solution.py:330
  3.3 0.0 copy-start
  3.3 8.9 %collective-permute-start = (bf16[1920,512]{1,0:T(8,128)(2,1)S(1)}, bf16[1920,512]{1,0:T(8,128)(2,1)}, u32[]{:S(2)}, u32[]{:S(2)}) collective-permute-start(bf16[1920,512]{1,0:T(8,128)(2,1)S(1)} %convert_element_type.3.x_ref), channel_id=1, source_target_pairs={{16,0},{32,16},{48,32},{64,48},{80,64},{96,80},{112,96},{128,112},... | collective-permute-start | bytes 5898248 | tf_op jit(solution)/shard_map/ppermute | solution.py:331
  12.2 2.5 %shard_map.41 = s16[8,192,128]{2,1,0:T(8,128)(2,1)} custom-call(bf16[1920,512]{1,0:T(8,128)(2,1)S(1)} %convert_element_type.3.x_ref), custom_call_target="tpu_custom_call" | custom-call | tf_op jit(solution)/shard_map/pallas_call | solution.py:36
  14.7 3.5 %all-to-all-start = ((s16[8,192,128]{2,1,0:T(8,128)(2,1)}), s16[8,192,128]{2,1,0:T(8,128)(2,1)S(1)}, u32[]{:S(2)}, u32[]{:S(2)}) async-start(s16[8,192,128]{2,1,0:T(8,128)(2,1)} %shard_map.41), calls=%async_computation | async-start | bytes 786432 | tf_op jit(solution)/shard_map/all_to_all | solution.py:333
  18.2 0.0 copy-done
  18.2 0.2 shard_map.43
  18.3 14.8 %all-to-all-done.came_ref = s16[8,192,128]{2,1,0:T(8,128)(2,1)S(1)} async-done(((s16[8,192,128]{2,1,0:T(8,128)(2,1)}), s16[8,192,128]{2,1,0:T(8,128)(2,1)S(1)}, u32[]{:S(2)}, u32[]{:S(2)}) %all-to-all-start) | async-done | bytes 393248 | tf_op jit(solution)/shard_map/all_to_all | solution.py:333
  33.1 0.1 shard_map.42
  33.2 0.0 collective-permute-done.next_ref
  33.2 4.1 %shard_map.44 = s16[16,96,128]{2,1,0:T(8,128)(2,1)} custom-call(bf16[1920,512]{1,0:T(8,128)(2,1)S(1)} %convert_element_type.3.x_ref, bf16[1920,512]{1,0:T(8,128)(2,1)} %collective-permute-done.next_ref), custom_call_target="tpu_custom_call" | custom-call | tf_op jit(solution)/shard_map/pallas_call | solution.py:36
  37.3 12.5 %all-to-all-start.1 = ((s16[16,96,128]{2,1,0:T(8,128)(2,1)}), s16[16,96,128]{2,1,0:T(8,128)(2,1)S(1)}, u32[]{:S(2)}, u32[]{:S(2)}) async-start(s16[16,96,128]{2,1,0:T(8,128)(2,1)} %shard_map.44), calls=%async_computation.1 | async-start | bytes 786432 | tf_op jit(solution)/shard_map/all_to_all | solution.py:344
  49.8 7.2 %collective-permute-start.1 = (s16[96,128]{1,0:T(8,128)(2,1)S(1)}, s16[96,128]{1,0:T(8,128)(2,1)S(1)}, u32[]{:S(2)}, u32[]{:S(2)}) collective-permute-start(s16[96,128]{1,0:T(8,128)(2,1)S(1)} %get-tuple-element.28), channel_id=1, source_target_pairs={{0,8},{1,9},{2,10},{3,11},{4,12},{5,13},{6,14},{7,15},{8,0},{9,1},... | collective-permute-start | bytes 73736 | tf_op jit(solution)/shard_map/ppermute | solution.py:341
  56.9 2.8 %collective-permute-done.1.far_ref = s16[96,128]{1,0:T(8,128)(2,1)S(1)} collective-permute-done((s16[96,128]{1,0:T(8,128)(2,1)S(1)}, s16[96,128]{1,0:T(8,128)(2,1)S(1)}, u32[]{:S(2)}, u32[]{:S(2)}) %collective-permute-start.1) | collective-permute-done | bytes 24608 | tf_op jit(solution)/shard_map/ppermute | solution.py:341
  59.8 3.9 %all-to-all-done.1.next_ref = s16[16,96,128]{2,1,0:T(8,128)(2,1)S(1)} async-done(((s16[16,96,128]{2,1,0:T(8,128)(2,1)}), s16[16,96,128]{2,1,0:T(8,128)(2,1)S(1)}, u32[]{:S(2)}, u32[]{:S(2)}) %all-to-all-start.1) | async-done | bytes 393248 | tf_op jit(solution)/shard_map/all_to_all | solution.py:344
  63.6 1.0 shard_map.45
  64.6 6.8 %all-to-all-start.2 = ((s16[16,128,128]{2,1,0:T(8,128)(2,1)}), s16[16,128,128]{2,1,0:T(8,128)(2,1)S(1)}, u32[]{:S(2)}, u32[]{:S(2)}) async-start(s16[16,128,128]{2,1,0:T(8,128)(2,1)} %get-tuple-element.31), calls=%async_computation.2 | async-start | bytes 1048576 | tf_op jit(solution)/shard_map/all_to_all | solution.py:354
  71.4 1.9 %collective-permute-start.3 = (s16[192,512]{1,0:T(8,128)(2,1)S(1)}, s16[192,512]{1,0:T(8,128)(2,1)S(1)}, u32[]{:S(2)}, u32[]{:S(2)}) collective-permute-start(s16[192,512]{1,0:T(8,128)(2,1)S(1)} %shard_map.43), channel_id=1, source_target_pairs={{16,0},{32,16},{48,32},{64,48},{80,64},{96,80},{112,96},{128,112},... | collective-permute-start | bytes 589832 | tf_op jit(solution)/shard_map/ppermute | solution.py:345
  73.4 16.9 %all-to-all-done.2.codes_ref = s16[16,128,128]{2,1,0:T(8,128)(2,1)S(1)} async-done(((s16[16,128,128]{2,1,0:T(8,128)(2,1)}), s16[16,128,128]{2,1,0:T(8,128)(2,1)S(1)}, u32[]{:S(2)}, u32[]{:S(2)}) %all-to-all-start.2) | async-done | bytes 524320 | tf_op jit(solution)/shard_map/all_to_all | solution.py:354
  90.3 0.9 shard_map.46
  91.2 0.6 shard_map.48
  91.8 6.3 %collective-permute-start.2 = (s16[192,512]{1,0:T(8,128)(2,1)S(1)}, s16[192,512]{1,0:T(8,128)(2,1)S(1)}, u32[]{:S(2)}, u32[]{:S(2)}) collective-permute-start(s16[192,512]{1,0:T(8,128)(2,1)S(1)} %shard_map.48), channel_id=1, source_target_pairs={{0,16},{16,32},{32,48},{48,64},{64,80},{80,96},{96,112},{112,128},... | collective-permute-start | bytes 589832 | tf_op jit(solution)/shard_map/ppermute | solution.py:366
  98.1 0.5 shard_map.47.part_ref
  98.6 0.0 collective-permute-done.3.next_ref
  98.6 2.1 %collective-permute-done.2.came_ref = s16[192,512]{1,0:T(8,128)(2,1)S(1)} collective-permute-done((s16[192,512]{1,0:T(8,128)(2,1)S(1)}, s16[192,512]{1,0:T(8,128)(2,1)S(1)}, u32[]{:S(2)}, u32[]{:S(2)}) %collective-permute-start.2) | collective-permute-done | bytes 196640 | tf_op jit(solution)/shard_map/ppermute | solution.py:366
  100.7 1.1 shard_map.49
  101.8 4.4 %collective-permute-start.4 = (s16[192,512]{1,0:T(8,128)(2,1)S(1)}, s16[192,512]{1,0:T(8,128)(2,1)S(1)}, u32[]{:S(2)}, u32[]{:S(2)}) collective-permute-start(s16[192,512]{1,0:T(8,128)(2,1)S(1)} %get-tuple-element.41), channel_id=1, source_target_pairs={{0,16},{16,32},{32,48},{48,64},{64,80},{80,96},{96,112},{112,128},... | collective-permute-start | bytes 589832 | tf_op jit(solution)/shard_map/ppermute | solution.py:362
  106.2 1.9 %collective-permute-start.5 = (s16[192,512]{1,0:T(8,128)(2,1)S(1)}, s16[192,512]{1,0:T(8,128)(2,1)S(1)}, u32[]{:S(2)}, u32[]{:S(2)}) collective-permute-start(s16[192,512]{1,0:T(8,128)(2,1)S(1)} %get-tuple-element.42), channel_id=1, source_target_pairs={{16,0},{32,16},{48,32},{64,48},{80,64},{96,80},{112,96},{128,112},... | collective-permute-start | bytes 589832 | tf_op jit(solution)/shard_map/ppermute | solution.py:363
  108.1 0.5 shard_map.50.part_ref
  108.6 0.2 collective-permute-done.4.came_ref
  108.8 6.3 %collective-permute-done.5.next_ref = s16[192,512]{1,0:T(8,128)(2,1)S(1)} collective-permute-done((s16[192,512]{1,0:T(8,128)(2,1)S(1)}, s16[192,512]{1,0:T(8,128)(2,1)S(1)}, u32[]{:S(2)}, u32[]{:S(2)}) %collective-permute-start.5) | collective-permute-done | bytes 196640 | tf_op jit(solution)/shard_map/ppermute | solution.py:363
  115.1 1.1 shard_map.51
  116.2 1.9 %collective-permute-start.6 = (s16[192,512]{1,0:T(8,128)(2,1)S(1)}, s16[192,512]{1,0:T(8,128)(2,1)S(1)}, u32[]{:S(2)}, u32[]{:S(2)}) collective-permute-start(s16[192,512]{1,0:T(8,128)(2,1)S(1)} %get-tuple-element.44), channel_id=1, source_target_pairs={{0,16},{16,32},{32,48},{48,64},{64,80},{80,96},{96,112},{112,128},... | collective-permute-start | bytes 589832 | tf_op jit(solution)/shard_map/ppermute | solution.py:362
  118.1 2.4 %collective-permute-start.7 = (s16[192,512]{1,0:T(8,128)(2,1)S(1)}, s16[192,512]{1,0:T(8,128)(2,1)S(1)}, u32[]{:S(2)}, u32[]{:S(2)}) collective-permute-start(s16[192,512]{1,0:T(8,128)(2,1)S(1)} %get-tuple-element.45), channel_id=1, source_target_pairs={{16,0},{32,16},{48,32},{64,48},{80,64},{96,80},{112,96},{128,112},... | collective-permute-start | bytes 589832 | tf_op jit(solution)/shard_map/ppermute | solution.py:363
  120.5 0.5 shard_map.52.part_ref
  121.0 0.2 shard_map.53.early_ref
  121.2 0.0 collective-permute-done.6.came_ref
  121.3 5.9 %collective-permute-done.7.next_ref = s16[192,512]{1,0:T(8,128)(2,1)S(1)} collective-permute-done((s16[192,512]{1,0:T(8,128)(2,1)S(1)}, s16[192,512]{1,0:T(8,128)(2,1)S(1)}, u32[]{:S(2)}, u32[]{:S(2)}) %collective-permute-start.7) | collective-permute-done | bytes 196640 | tf_op jit(solution)/shard_map/ppermute | solution.py:363
  127.2 0.6 shard_map.54
  127.8 22.4 %all_to_all.20.moments_ref = f32[32,8,256]{2,1,0:T(8,128)S(1)} all-to-all(f32[32,8,256]{2,1,0:T(8,128)S(1)} %get-tuple-element.46), channel_id=1, replica_groups=mesh['genome'=32,'cols'=16] {'genome'}, dimensions={0} | all-to-all | bytes 524288 | tf_op jit(solution)/shard_map/all_to_all | solution.py:373
  150.2 1.4 shard_map.55
Async XLA Ops:
  3.3 14.9 %copy-start = (f32[512,184]{0,1:T(8,128)S(1)}, f32[512,184]{0,1:T(8,128)}, u32[]{:S(2)}) copy-start(f32[512,184]{0,1:T(8,128)} %param.3) | copy-start | bytes 1130500
  3.3 29.9 %collective-permute-start = (bf16[1920,512]{1,0:T(8,128)(2,1)S(1)}, bf16[1920,512]{1,0:T(8,128)(2,1)}, u32[]{:S(2)}, u32[]{:S(2)}) collective-permute-start(bf16[1920,512]{1,0:T(8,128)(2,1)S(1)} %convert_element_type.3.x_ref), channel_id=1, source_target_pairs={{16,0},{32,16},{48,32},{64,48},{80,64},{96,80},{112,96},{128,112},... | collective-permute-start | bytes 5898248 | tf_op jit(solution)/shard_map/ppermute | solution.py:331
  14.7 18.4 %all-to-all-start = ((s16[8,192,128]{2,1,0:T(8,128)(2,1)}), s16[8,192,128]{2,1,0:T(8,128)(2,1)S(1)}, u32[]{:S(2)}, u32[]{:S(2)}) async-start(s16[8,192,128]{2,1,0:T(8,128)(2,1)} %shard_map.41), calls=%async_computation | async-start | bytes 786432 | tf_op jit(solution)/shard_map/all_to_all | solution.py:333
  37.3 26.4 %all-to-all-start.1 = ((s16[16,96,128]{2,1,0:T(8,128)(2,1)}), s16[16,96,128]{2,1,0:T(8,128)(2,1)S(1)}, u32[]{:S(2)}, u32[]{:S(2)}) async-start(s16[16,96,128]{2,1,0:T(8,128)(2,1)} %shard_map.44), calls=%async_computation.1 | async-start | bytes 786432 | tf_op jit(solution)/shard_map/all_to_all | solution.py:344
  49.8 10.0 %collective-permute-start.1 = (s16[96,128]{1,0:T(8,128)(2,1)S(1)}, s16[96,128]{1,0:T(8,128)(2,1)S(1)}, u32[]{:S(2)}, u32[]{:S(2)}) collective-permute-start(s16[96,128]{1,0:T(8,128)(2,1)S(1)} %get-tuple-element.28), channel_id=1, source_target_pairs={{0,8},{1,9},{2,10},{3,11},{4,12},{5,13},{6,14},{7,15},{8,0},{9,1},... | collective-permute-start | bytes 73736 | tf_op jit(solution)/shard_map/ppermute | solution.py:341
  64.6 25.6 %all-to-all-start.2 = ((s16[16,128,128]{2,1,0:T(8,128)(2,1)}), s16[16,128,128]{2,1,0:T(8,128)(2,1)S(1)}, u32[]{:S(2)}, u32[]{:S(2)}) async-start(s16[16,128,128]{2,1,0:T(8,128)(2,1)} %get-tuple-element.31), calls=%async_computation.2 | async-start | bytes 1048576 | tf_op jit(solution)/shard_map/all_to_all | solution.py:354
  71.4 27.2 %collective-permute-start.3 = (s16[192,512]{1,0:T(8,128)(2,1)S(1)}, s16[192,512]{1,0:T(8,128)(2,1)S(1)}, u32[]{:S(2)}, u32[]{:S(2)}) collective-permute-start(s16[192,512]{1,0:T(8,128)(2,1)S(1)} %shard_map.43), channel_id=1, source_target_pairs={{16,0},{32,16},{48,32},{64,48},{80,64},{96,80},{112,96},{128,112},... | collective-permute-start | bytes 589832 | tf_op jit(solution)/shard_map/ppermute | solution.py:345
  91.8 8.9 %collective-permute-start.2 = (s16[192,512]{1,0:T(8,128)(2,1)S(1)}, s16[192,512]{1,0:T(8,128)(2,1)S(1)}, u32[]{:S(2)}, u32[]{:S(2)}) collective-permute-start(s16[192,512]{1,0:T(8,128)(2,1)S(1)} %shard_map.48), channel_id=1, source_target_pairs={{0,16},{16,32},{32,48},{48,64},{64,80},{80,96},{96,112},{112,128},... | collective-permute-start | bytes 589832 | tf_op jit(solution)/shard_map/ppermute | solution.py:366
  101.8 7.0 %collective-permute-start.4 = (s16[192,512]{1,0:T(8,128)(2,1)S(1)}, s16[192,512]{1,0:T(8,128)(2,1)S(1)}, u32[]{:S(2)}, u32[]{:S(2)}) collective-permute-start(s16[192,512]{1,0:T(8,128)(2,1)S(1)} %get-tuple-element.41), channel_id=1, source_target_pairs={{0,16},{16,32},{32,48},{48,64},{64,80},{80,96},{96,112},{112,128},... | collective-permute-start | bytes 589832 | tf_op jit(solution)/shard_map/ppermute | solution.py:362
  106.2 8.8 %collective-permute-start.5 = (s16[192,512]{1,0:T(8,128)(2,1)S(1)}, s16[192,512]{1,0:T(8,128)(2,1)S(1)}, u32[]{:S(2)}, u32[]{:S(2)}) collective-permute-start(s16[192,512]{1,0:T(8,128)(2,1)S(1)} %get-tuple-element.42), channel_id=1, source_target_pairs={{16,0},{32,16},{48,32},{64,48},{80,64},{96,80},{112,96},{128,112},... | collective-permute-start | bytes 589832 | tf_op jit(solution)/shard_map/ppermute | solution.py:363
  116.2 5.1 %collective-permute-start.6 = (s16[192,512]{1,0:T(8,128)(2,1)S(1)}, s16[192,512]{1,0:T(8,128)(2,1)S(1)}, u32[]{:S(2)}, u32[]{:S(2)}) collective-permute-start(s16[192,512]{1,0:T(8,128)(2,1)S(1)} %get-tuple-element.44), channel_id=1, source_target_pairs={{0,16},{16,32},{32,48},{48,64},{64,80},{80,96},{96,112},{112,128},... | collective-permute-start | bytes 589832 | tf_op jit(solution)/shard_map/ppermute | solution.py:362
  118.1 9.1 %collective-permute-start.7 = (s16[192,512]{1,0:T(8,128)(2,1)S(1)}, s16[192,512]{1,0:T(8,128)(2,1)S(1)}, u32[]{:S(2)}, u32[]{:S(2)}) collective-permute-start(s16[192,512]{1,0:T(8,128)(2,1)S(1)} %get-tuple-element.45), channel_id=1, source_target_pairs={{16,0},{32,16},{48,32},{64,48},{80,64},{96,80},{112,96},{128,112},... | collective-permute-start | bytes 589832 | tf_op jit(solution)/shard_map/ppermute | solution.py:363

commit v5 on v4

--- a/solution.py
+++ b/solution.py
@@ -30,16 +30,16 @@
     return high, (a - high.astype(f32)).astype(bf16)
 
 
-def call(kernel, outs, *args):
+def call(kernel, outs, *args, far=(), scratch=()):
     spec = pl.BlockSpec(memory_space=pltpu.VMEM)
-    scalars = [a.dtype == i32 and a.ndim == 1 for a in args]
     return pl.pallas_call(
         kernel,
         out_shape=outs,
-        in_specs=[pl.BlockSpec(memory_space=pltpu.SMEM) if s else spec for s in scalars],
+        in_specs=[pl.BlockSpec(memory_space=pl.ANY) if k in far else spec for k in range(len(args))],
+        scratch_shapes=scratch,
         out_specs=jax.tree.map(lambda _: spec, outs, is_leaf=lambda o: not isinstance(o, tuple)),
         compiler_params=pltpu.CompilerParams(vmem_limit_bytes=16 << 20),
-    )(*(a if s else pltpu.with_memory_space_constraint(a, pltpu.VMEM) for a, s in zip(args, scalars)))
+    )(*(a if k in far else pltpu.with_memory_space_constraint(a, pltpu.VMEM) for k, a in enumerate(args)))
 
 
 def shape(*dims, dtype=f32):
@@ -63,8 +63,15 @@
 
 
 def sums(block, peers):
-    ones = jnp.ones((8, block.shape[0]), bf16)
-    both = (dot(ones, block)[:1], dot(ones, block * block)[:1])
+    high = 0.0, 0.0
+    step = 16
+    for lo in range(0, block.shape[0], 60 * step):
+        near = square = None
+        for at in range(lo, min(lo + 60 * step, block.shape[0]), step):
+            x = block[at : at + step]
+            near, square = (x, x * x) if near is None else (near + x, square + x * x)
+        high = high[0] + near.astype(f32), high[1] + square.astype(f32)
+    both = [jnp.sum(v, axis=0, keepdims=True) for v in high]
     stats = [v[:, q * TILE : (q + 1) * TILE] for v in both for q in range(SIDE)]
     stats = jnp.concatenate(stats + [jnp.zeros((8, TILE), f32)], axis=0)
     return jnp.broadcast_to(stats.astype(i32).astype(i16)[None], (peers, 16, TILE))
@@ -84,20 +91,33 @@
     put(NT * TILE // peers, sums(block, peers))
 
 
-def next_products(x_ref, next_ref, out_ref):
-    block = next_ref[...]
+def next_products(x_ref, next_ref, out_ref, block_ref, sem):
     peers = out_ref.shape[0]
+    parts = sem.shape[0]
+    length = block_ref.shape[0] // parts
+    spans = [pl.ds(k * length, length) for k in range(parts)]
+    copies = [
+        pltpu.make_async_copy(next_ref.at[span], block_ref.at[span], sem.at[k]) for k, span in enumerate(spans)
+    ]
+    for copy in copies:
+        copy.start()
+    gram = None
+    for copy, span in zip(copies, spans):
+        turned = x_ref[span].T
+        copy.wait()
+        more = dot(turned, block_ref[span])
+        gram = more if gram is None else gram + more
 
     def put(at, value):
         out_ref[:, at : at + value.shape[1], :] = value
 
-    pack_tiles(dot(x_ref[...].T, block), LOWER, put, peers)
-    put(NT * TILE // peers, sums(block, peers))
-
-
-def fold(me_ref, came_ref, keep_ref, send_ref):
+    pack_tiles(gram, LOWER, put, peers)
+    put(NT * TILE // peers, sums(block_ref[...], peers))
+
+
+def fold(came_ref, keep_ref, send_ref):
     near, depth = came_ref.shape[0], came_ref.shape[1] // 2
-    far = me_ref[0] // near
+    far = lax.axis_index("cols") // near
 
     def total(side):
         rows = pl.ds(pl.multiple_of(side * depth, depth), depth)
@@ -110,7 +130,7 @@
     send_ref[...] = (total(1 - far) - HALF).astype(i16)
 
 
-def correlate(samples, me_ref, keep_ref, far_ref, next_ref, out_ref, diagonal_ref):
+def correlate(samples, keep_ref, far_ref, next_ref, out_ref, diagonal_ref):
     peers = next_ref.shape[0]
     rows = TILE // peers
     own = keep_ref[...] + far_ref[...].astype(i32) + HALF
@@ -128,7 +148,7 @@
     next_mean, _, next_scale = stats(nxt[NT * rows :])
     diagonal_ref[...] = jnp.concatenate([variance * scale * scale, jnp.zeros((8 - SIDE, TILE), f32)], axis=0)
     lane = lax.broadcasted_iota(i32, (rows, TILE), 1)
-    row = lax.broadcasted_iota(i32, (rows, TILE), 0) + me_ref[0] * rows
+    row = lax.broadcasted_iota(i32, (rows, TILE), 0) + lax.axis_index("cols") * rows
 
     def at_rows(vector, p):
         return jnp.sum(jnp.where(lane == row, vector[p : p + 1], 0.0), axis=1, keepdims=True)
@@ -221,8 +241,8 @@
     out_ref[...] = jnp.concatenate([code, tail], axis=0).astype(i32).astype(i16)
 
 
-def decode(code_ref, rows):
-    code = code_ref[...].astype(i32).astype(f32)
+def decode(code, rows):
+    code = code.astype(i32).astype(f32)
     power = jnp.sum(jnp.where(diagonal(rows), code[rows : rows + 1, :256], 0.0), axis=1, keepdims=True)
     return code[:rows] * (jnp.exp2(power) * (1.0 / CODE))
 
@@ -239,16 +259,43 @@
     out_ref[...] = product(v_ref[...], high_ref, low_ref) + RIDGE * v_ref[...]
 
 
-def gather(part_ref, came_ref, next_ref, high_ref, low_ref):
+def gather(part_ref, came, nxt, back_h, back_l):
     rows = part_ref.shape[0]
-    return part_ref[...] + decode(came_ref, rows) + product(decode(next_ref, rows), high_ref, low_ref)
-
-
-def gather_in(part_ref, came_ref, next_ref, back_h, back_l, next_h, next_l, out_ref, left_ref, right_ref):
-    w = gather(part_ref, came_ref, next_ref, back_h, back_l)
+    return part_ref[...] + decode(came, rows) + product(decode(nxt, rows), back_h, back_l)
+
+
+def first_gather(part_ref, came_ref, next_ref, back_h, back_l, next_h, next_l, out_ref, across_ref, inside_ref):
+    w = gather(part_ref, came_ref[...], next_ref[...], back_h, back_l)
+    hand_on(w, next_h, next_l, out_ref, across_ref, inside_ref)
+
+
+def next_gather(part_ref, across_in, inside_in, back_h, back_l, next_h, next_l, out_ref, across_ref, inside_ref):
+    w = gather(part_ref, *arrived(across_in, inside_in), back_h, back_l)
+    hand_on(w, next_h, next_l, out_ref, across_ref, inside_ref)
+
+
+def odd():
+    return lax.rem(lax.axis_index("genome"), 2)
+
+
+def hand_on(w, next_h, next_l, out_ref, across_ref, inside_ref):
     out_ref[...] = w
-    encode(w, left_ref)
-    encode(product(w, next_h, next_l), right_ref)
+
+    @pl.when(odd() == 0)
+    def _():
+        encode(w, across_ref)
+        encode(product(w, next_h, next_l), inside_ref)
+
+    @pl.when(odd() == 1)
+    def _():
+        encode(product(w, next_h, next_l), across_ref)
+        encode(w, inside_ref)
+
+
+def arrived(across_in, inside_in):
+    even = odd() == 0
+    across, inside = across_in[...].astype(i32), inside_in[...].astype(i32)
+    return jnp.where(even, across, inside), jnp.where(even, inside, across)
 
 
 def along(a, b):
@@ -265,8 +312,8 @@
     out_ref[...] = jnp.concatenate(rows + [jnp.zeros((3, 256), f32)], axis=0)
 
 
-def last_vector(part_ref, came_ref, next_ref, back_h, back_l, c_ref, early_ref, out_ref, moments_ref):
-    w = gather(part_ref, came_ref, next_ref, back_h, back_l)
+def last_vector(part_ref, across_in, inside_in, back_h, back_l, c_ref, early_ref, out_ref, moments_ref):
+    w = gather(part_ref, *arrived(across_in, inside_in), back_h, back_l)
     out_ref[...] = w
     row = lax.broadcasted_iota(i32, early_ref.shape, 0)
     moments = jnp.where(row == 5, turn(along(c_ref[...], w)), early_ref[...])
@@ -331,22 +378,27 @@
     next_dosage = lax.ppermute(dosage, "genome", to_left)
     own = call(own_products, shape(near, 2 * depth, TILE, dtype=i16), dosage)
     own = lax.all_to_all(own, "cols", 0, 0, axis_index_groups=sides)
-    me = lax.axis_index("cols").astype(i32).reshape(1)
-    keep, far = call(fold, (shape(depth, TILE, dtype=i32), shape(depth, TILE, dtype=i16)), me, own)
+    keep, far = call(fold, (shape(depth, TILE, dtype=i32), shape(depth, TILE, dtype=i16)), own)
     z = z_scores.T
     vector = shape(*z.shape)
     code = shape(z.shape[0] // 16 * 16 + 16, z.shape[1], dtype=i16)
     z_code = call(start_code, code, z)
     far, next_dosage = lax.optimization_barrier((far, next_dosage))
     far = lax.ppermute(far, "cols", [(k, (k + near) % peers) for k in cols])
-    nxt = call(next_products, shape(peers, depth, TILE, dtype=i16), dosage, next_dosage)
+    nxt = call(
+        next_products,
+        shape(peers, depth, TILE, dtype=i16),
+        dosage,
+        next_dosage,
+        far=(1,),
+        scratch=(pltpu.VMEM(dosage.shape, bf16), pltpu.SemaphoreType.DMA((5,))),
+    )
     z_code, nxt = lax.optimization_barrier((z_code, nxt))
     nxt = lax.all_to_all(nxt, "cols", 0, 0)
     z_next = lax.ppermute(z_code, "genome", to_left)
     codes, diagonal_row = call(
         functools.partial(correlate, samples),
         (shape(peers, SIDE * SIDE * rows, TILE, dtype=i16), shape(8, TILE)),
-        me,
         keep,
         far,
         nxt,
@@ -355,20 +407,23 @@
     square = shape(W, W, dtype=bf16)
     near_h, near_l, next_h, next_l, back_h, back_l = call(unpack, (square,) * 6, codes, diagonal_row)
 
-    def step(part, came, nxt):
-        w, left, right = call(
-            gather_in, (vector, code, code), part, came, nxt, back_h, back_l, next_h, next_l
+    inside = [(k, k ^ 1) for k in range(blocks)]
+    across = [(k, ((k + 1) ^ 1) - 1) for k in range(1, blocks - 1)]
+
+    def step(kernel, part, *came):
+        w, out, inn = call(
+            kernel, (vector, code, code), part, *came, back_h, back_l, next_h, next_l
         )
-        came = lax.ppermute(right, "genome", to_right)
-        nxt = lax.ppermute(left, "genome", to_left)
-        return w, came, nxt, call(inward, vector, w, near_h, near_l)
+        out = lax.ppermute(out, "genome", across)
+        inn = lax.ppermute(inn, "genome", inside)
+        return w, call(inward, vector, w, near_h, near_l), out, inn
 
     came = lax.ppermute(call(outward, code, z, next_h, next_l), "genome", to_right)
-    one, came, nxt, part = step(call(inward, vector, z, near_h, near_l), came, z_next)
-    two, came, nxt, part = step(part, came, nxt)
+    one, *rest = step(first_gather, call(inward, vector, z, near_h, near_l), came, z_next)
+    two, part, out, inn = step(next_gather, *rest)
     early = call(early_moments, shape(8, 256), z, one, two)
     three, moments = call(
-        last_vector, (vector, shape(blocks, 8, 256)), part, came, nxt, back_h, back_l, two, early
+        last_vector, (vector, shape(blocks, 8, 256)), part, out, inn, back_h, back_l, two, early
     )
     moments = lax.all_to_all(moments, "genome", 0, 0)
     effects, residual = call(combine, (jax.ShapeDtypeStruct(z.shape, f32),) * 2, moments, z, one, two, three)

time: 152 us -> 144 us (0.947)
  waiting for transfers between devices: 52.9 us -> 42 us
  starting transfers between devices: 57.6 us -> 59.4 us
    ppermute x4, waiting for transfers between devices: 12.4 us -> 1.64 us  [the longest x2 1.63 us: step(): out = lax.ppermute(out, 'genome', across)]
  transfers between devices with their start and end apart: 11 -> 11, of which waited for: 8 -> 7; matrix products, arithmetic and copies ran while one was open for 0% -> 0% of each run, Pallas kernels for 4% -> 4%
where the time goes in v5:
time: 144 us; the launch traced here: 143 us
  starting transfers between devices  59.4 us (41%)
  waiting for transfers between devices  42 us (29%)
  blocking collectives  23.5 us (16%)
  Pallas kernels  15 us (10%)
  other arithmetic  2.65 us (2%)
    all_to_all x1, blocking collectives, shards(): moments = lax.all_to_all(moments, 'genome', 0, 0)  23.5 us
    all_to_all x1, waiting for transfers between devices, shards(): codes = lax.all_to_all(codes, 'cols', 0, 0)  16.5 us
    pallas_call x15, Pallas kernels, call(): pl.pallas_call(kernel, out_shape=outs, in_specs=[pl.BlockSpec(memory_spac...  15 us
    all_to_all x1, waiting for transfers between devices, shards(): own = lax.all_to_all(own, 'cols', 0, 0, axis_index_groups=sides)  14.8 us
    all_to_all x1, starting transfers between devices, shards(): nxt = lax.all_to_all(nxt, 'cols', 0, 0)  13 us
    ppermute x1, starting transfers between devices, shards(): next_dosage = lax.ppermute(dosage, 'genome', to_left)  8.88 us
    ppermute x2, starting transfers between devices, step(): out = lax.ppermute(out, 'genome', across)  7.95 us
    ppermute x1, starting transfers between devices, shards(): far = lax.ppermute(far, 'cols', [(k, (k + near) % peers) for k in cols])  7.17 us
  transfers between devices with their start and end apart: 11, of which 7 were waited for; matrix products, arithmetic and copies ran while one was open for 0% of the time, Pallas kernels for 4%

profile of v5, /device:TPU:1, one launch (start us, length us, event | category | flops | bytes accessed | tf_op | source)
XLA Modules:
  0.0 143.4 jit_solution(13112296720589353679)
XLA Ops:
  0.6 2.6 %convert_element_type.3.x_ref = bf16[1920,512]{1,0:T(8,128)(2,1)S(1)} convert(s32[1920,512]{1,0:T(8,128)} %param.2) | non-fusion elementwise | flops 983040 | bytes 5898240 | tf_op jit(solution)/shard_map/convert_element_type | solution.py:377
  3.3 0.0 copy-start
  3.3 8.9 %collective-permute-start = (bf16[1920,512]{1,0:T(8,128)(2,1)S(1)}, bf16[1920,512]{1,0:T(8,128)(2,1)}, u32[]{:S(2)}, u32[]{:S(2)}) collective-permute-start(bf16[1920,512]{1,0:T(8,128)(2,1)S(1)} %convert_element_type.3.x_ref), channel_id=1, source_target_pairs={{16,0},{32,16},{48,32},{64,48},{80,64},{96,80},{112,96},{128,112},... | collective-permute-start | bytes 5898248 | tf_op jit(solution)/shard_map/ppermute | solution.py:378
  12.2 2.0 %shard_map.41 = s16[8,192,128]{2,1,0:T(8,128)(2,1)} custom-call(bf16[1920,512]{1,0:T(8,128)(2,1)S(1)} %convert_element_type.3.x_ref), custom_call_target="tpu_custom_call" | custom-call | tf_op jit(solution)/shard_map/pallas_call | solution.py:35
  14.2 3.5 %all-to-all-start = ((s16[8,192,128]{2,1,0:T(8,128)(2,1)}), s16[8,192,128]{2,1,0:T(8,128)(2,1)S(1)}, u32[]{:S(2)}, u32[]{:S(2)}) async-start(s16[8,192,128]{2,1,0:T(8,128)(2,1)} %shard_map.41), calls=%async_computation | async-start | bytes 786432 | tf_op jit(solution)/shard_map/all_to_all | solution.py:380
  17.7 0.0 copy-done
  17.7 0.2 shard_map.43
  17.8 14.8 %all-to-all-done.came_ref = s16[8,192,128]{2,1,0:T(8,128)(2,1)S(1)} async-done(((s16[8,192,128]{2,1,0:T(8,128)(2,1)}), s16[8,192,128]{2,1,0:T(8,128)(2,1)S(1)}, u32[]{:S(2)}, u32[]{:S(2)}) %all-to-all-start) | async-done | bytes 393248 | tf_op jit(solution)/shard_map/all_to_all | solution.py:380
  32.7 0.1 shard_map.42
  32.7 0.0 collective-permute-done.next_ref
  32.7 3.9 %shard_map.44 = s16[16,96,128]{2,1,0:T(8,128)(2,1)} custom-call(bf16[1920,512]{1,0:T(8,128)(2,1)S(1)} %convert_element_type.3.x_ref, bf16[1920,512]{1,0:T(8,128)(2,1)} %collective-permute-done.next_ref), custom_call_target="tpu_custom_call" | custom-call | tf_op jit(solution)/shard_map/pallas_call | solution.py:35
  36.7 13.0 %all-to-all-start.1 = ((s16[16,96,128]{2,1,0:T(8,128)(2,1)}), s16[16,96,128]{2,1,0:T(8,128)(2,1)S(1)}, u32[]{:S(2)}, u32[]{:S(2)}) async-start(s16[16,96,128]{2,1,0:T(8,128)(2,1)} %shard_map.44), calls=%async_computation.1 | async-start | bytes 786432 | tf_op jit(solution)/shard_map/all_to_all | solution.py:397
  49.7 7.2 %collective-permute-start.1 = (s16[96,128]{1,0:T(8,128)(2,1)S(1)}, s16[96,128]{1,0:T(8,128)(2,1)S(1)}, u32[]{:S(2)}, u32[]{:S(2)}) collective-permute-start(s16[96,128]{1,0:T(8,128)(2,1)S(1)} %get-tuple-element.28), channel_id=1, source_target_pairs={{0,8},{1,9},{2,10},{3,11},{4,12},{5,13},{6,14},{7,15},{8,0},{9,1},... | collective-permute-start | bytes 73736 | tf_op jit(solution)/shard_map/ppermute | solution.py:387
  56.8 2.6 %collective-permute-done.1.far_ref = s16[96,128]{1,0:T(8,128)(2,1)S(1)} collective-permute-done((s16[96,128]{1,0:T(8,128)(2,1)S(1)}, s16[96,128]{1,0:T(8,128)(2,1)S(1)}, u32[]{:S(2)}, u32[]{:S(2)}) %collective-permute-start.1) | collective-permute-done | bytes 24608 | tf_op jit(solution)/shard_map/ppermute | solution.py:387
  59.4 4.4 %all-to-all-done.1.next_ref = s16[16,96,128]{2,1,0:T(8,128)(2,1)S(1)} async-done(((s16[16,96,128]{2,1,0:T(8,128)(2,1)}), s16[16,96,128]{2,1,0:T(8,128)(2,1)S(1)}, u32[]{:S(2)}, u32[]{:S(2)}) %all-to-all-start.1) | async-done | bytes 393248 | tf_op jit(solution)/shard_map/all_to_all | solution.py:397
  63.8 1.0 shard_map.45
  64.8 6.4 %all-to-all-start.2 = ((s16[16,128,128]{2,1,0:T(8,128)(2,1)}), s16[16,128,128]{2,1,0:T(8,128)(2,1)S(1)}, u32[]{:S(2)}, u32[]{:S(2)}) async-start(s16[16,128,128]{2,1,0:T(8,128)(2,1)} %get-tuple-element.31), calls=%async_computation.2 | async-start | bytes 1048576 | tf_op jit(solution)/shard_map/all_to_all | solution.py:406
  71.2 1.9 %collective-permute-start.3 = (s16[192,512]{1,0:T(8,128)(2,1)S(1)}, s16[192,512]{1,0:T(8,128)(2,1)S(1)}, u32[]{:S(2)}, u32[]{:S(2)}) collective-permute-start(s16[192,512]{1,0:T(8,128)(2,1)S(1)} %shard_map.43), channel_id=1, source_target_pairs={{16,0},{32,16},{48,32},{64,48},{80,64},{96,80},{112,96},{128,112},... | collective-permute-start | bytes 589832 | tf_op jit(solution)/shard_map/ppermute | solution.py:398
  73.1 16.5 %all-to-all-done.2.codes_ref = s16[16,128,128]{2,1,0:T(8,128)(2,1)S(1)} async-done(((s16[16,128,128]{2,1,0:T(8,128)(2,1)}), s16[16,128,128]{2,1,0:T(8,128)(2,1)S(1)}, u32[]{:S(2)}, u32[]{:S(2)}) %all-to-all-start.2) | async-done | bytes 524320 | tf_op jit(solution)/shard_map/all_to_all | solution.py:406
  89.7 0.9 shard_map.46
  90.6 0.6 shard_map.48
  91.2 6.8 %collective-permute-start.2 = (s16[192,512]{1,0:T(8,128)(2,1)S(1)}, s16[192,512]{1,0:T(8,128)(2,1)S(1)}, u32[]{:S(2)}, u32[]{:S(2)}) collective-permute-start(s16[192,512]{1,0:T(8,128)(2,1)S(1)} %shard_map.48), channel_id=1, source_target_pairs={{0,16},{16,32},{32,48},{48,64},{64,80},{80,96},{96,112},{112,128},... | collective-permute-start | bytes 589832 | tf_op jit(solution)/shard_map/ppermute | solution.py:421
  98.0 0.5 shard_map.47.part_ref
  98.5 0.0 collective-permute-done.3.next_ref
  98.5 2.1 %collective-permute-done.2.came_ref = s16[192,512]{1,0:T(8,128)(2,1)S(1)} collective-permute-done((s16[192,512]{1,0:T(8,128)(2,1)S(1)}, s16[192,512]{1,0:T(8,128)(2,1)S(1)}, u32[]{:S(2)}, u32[]{:S(2)}) %collective-permute-start.2) | collective-permute-done | bytes 196640 | tf_op jit(solution)/shard_map/ppermute | solution.py:421
  100.6 1.2 shard_map.49
  101.8 4.3 %collective-permute-start.4 = (s16[192,512]{1,0:T(8,128)(2,1)S(1)}, s16[192,512]{1,0:T(8,128)(2,1)S(1)}, u32[]{:S(2)}, u32[]{:S(2)}) collective-permute-start(s16[192,512]{1,0:T(8,128)(2,1)S(1)} %get-tuple-element.41), channel_id=1, source_target_pairs={{16,32},{32,16},{48,64},{64,48},{80,96},{96,80},{112,128},{128,112... | collective-permute-start | bytes 589832 | tf_op jit(solution)/shard_map/ppermute | solution.py:417
  106.2 1.9 %collective-permute-start.5 = (s16[192,512]{1,0:T(8,128)(2,1)S(1)}, s16[192,512]{1,0:T(8,128)(2,1)S(1)}, u32[]{:S(2)}, u32[]{:S(2)}) collective-permute-start(s16[192,512]{1,0:T(8,128)(2,1)S(1)} %get-tuple-element.42), channel_id=1, source_target_pairs={{0,16},{16,0},{32,48},{48,32},{64,80},{80,64},{96,112},{112,96},{1... | collective-permute-start | bytes 589832 | tf_op jit(solution)/shard_map/ppermute | solution.py:418
  108.1 0.5 shard_map.50.part_ref
  108.6 0.9 collective-permute-done.4.across_in
  109.5 0.0 collective-permute-done.5.inside_in
  109.5 1.3 shard_map.51
  110.8 3.6 %collective-permute-start.6 = (s16[192,512]{1,0:T(8,128)(2,1)S(1)}, s16[192,512]{1,0:T(8,128)(2,1)S(1)}, u32[]{:S(2)}, u32[]{:S(2)}) collective-permute-start(s16[192,512]{1,0:T(8,128)(2,1)S(1)} %get-tuple-element.44), channel_id=1, source_target_pairs={{16,32},{32,16},{48,64},{64,48},{80,96},{96,80},{112,128},{128,112... | collective-permute-start | bytes 589832 | tf_op jit(solution)/shard_map/ppermute | solution.py:417
  114.4 1.9 %collective-permute-start.7 = (s16[192,512]{1,0:T(8,128)(2,1)S(1)}, s16[192,512]{1,0:T(8,128)(2,1)S(1)}, u32[]{:S(2)}, u32[]{:S(2)}) collective-permute-start(s16[192,512]{1,0:T(8,128)(2,1)S(1)} %get-tuple-element.45), channel_id=1, source_target_pairs={{0,16},{16,0},{32,48},{48,32},{64,80},{80,64},{96,112},{112,96},{1... | collective-permute-start | bytes 589832 | tf_op jit(solution)/shard_map/ppermute | solution.py:418
  116.3 0.5 shard_map.52.part_ref
  116.8 0.2 shard_map.53.early_ref
  117.1 0.7 collective-permute-done.6.across_in
  117.8 0.0 collective-permute-done.7.inside_in
  117.8 0.7 shard_map.54
  118.5 23.5 %all_to_all.20.moments_ref = f32[32,8,256]{2,1,0:T(8,128)S(1)} all-to-all(f32[32,8,256]{2,1,0:T(8,128)S(1)} %get-tuple-element.46), channel_id=1, replica_groups=mesh['genome'=32,'cols'=16] {'genome'}, dimensions={0} | all-to-all | bytes 524288 | tf_op jit(solution)/shard_map/all_to_all | solution.py:428
  142.0 1.4 shard_map.55
Async XLA Ops:
  3.3 14.4 %copy-start = (f32[512,184]{0,1:T(8,128)S(1)}, f32[512,184]{0,1:T(8,128)}, u32[]{:S(2)}) copy-start(f32[512,184]{0,1:T(8,128)} %param.3) | copy-start | bytes 1130500
  3.3 29.4 %collective-permute-start = (bf16[1920,512]{1,0:T(8,128)(2,1)S(1)}, bf16[1920,512]{1,0:T(8,128)(2,1)}, u32[]{:S(2)}, u32[]{:S(2)}) collective-permute-start(bf16[1920,512]{1,0:T(8,128)(2,1)S(1)} %convert_element_type.3.x_ref), channel_id=1, source_target_pairs={{16,0},{32,16},{48,32},{64,48},{80,64},{96,80},{112,96},{128,112},... | collective-permute-start | bytes 5898248 | tf_op jit(solution)/shard_map/ppermute | solution.py:378
  14.2 18.4 %all-to-all-start = ((s16[8,192,128]{2,1,0:T(8,128)(2,1)}), s16[8,192,128]{2,1,0:T(8,128)(2,1)S(1)}, u32[]{:S(2)}, u32[]{:S(2)}) async-start(s16[8,192,128]{2,1,0:T(8,128)(2,1)} %shard_map.41), calls=%async_computation | async-start | bytes 786432 | tf_op jit(solution)/shard_map/all_to_all | solution.py:380
  36.7 27.1 %all-to-all-start.1 = ((s16[16,96,128]{2,1,0:T(8,128)(2,1)}), s16[16,96,128]{2,1,0:T(8,128)(2,1)S(1)}, u32[]{:S(2)}, u32[]{:S(2)}) async-start(s16[16,96,128]{2,1,0:T(8,128)(2,1)} %shard_map.44), calls=%async_computation.1 | async-start | bytes 786432 | tf_op jit(solution)/shard_map/all_to_all | solution.py:397
  49.7 9.8 %collective-permute-start.1 = (s16[96,128]{1,0:T(8,128)(2,1)S(1)}, s16[96,128]{1,0:T(8,128)(2,1)S(1)}, u32[]{:S(2)}, u32[]{:S(2)}) collective-permute-start(s16[96,128]{1,0:T(8,128)(2,1)S(1)} %get-tuple-element.28), channel_id=1, source_target_pairs={{0,8},{1,9},{2,10},{3,11},{4,12},{5,13},{6,14},{7,15},{8,0},{9,1},... | collective-permute-start | bytes 73736 | tf_op jit(solution)/shard_map/ppermute | solution.py:387
  64.8 24.9 %all-to-all-start.2 = ((s16[16,128,128]{2,1,0:T(8,128)(2,1)}), s16[16,128,128]{2,1,0:T(8,128)(2,1)S(1)}, u32[]{:S(2)}, u32[]{:S(2)}) async-start(s16[16,128,128]{2,1,0:T(8,128)(2,1)} %get-tuple-element.31), calls=%async_computation.2 | async-start | bytes 1048576 | tf_op jit(solution)/shard_map/all_to_all | solution.py:406
  71.2 27.3 %collective-permute-start.3 = (s16[192,512]{1,0:T(8,128)(2,1)S(1)}, s16[192,512]{1,0:T(8,128)(2,1)S(1)}, u32[]{:S(2)}, u32[]{:S(2)}) collective-permute-start(s16[192,512]{1,0:T(8,128)(2,1)S(1)} %shard_map.43), channel_id=1, source_target_pairs={{16,0},{32,16},{48,32},{64,48},{80,64},{96,80},{112,96},{128,112},... | collective-permute-start | bytes 589832 | tf_op jit(solution)/shard_map/ppermute | solution.py:398
  91.2 9.4 %collective-permute-start.2 = (s16[192,512]{1,0:T(8,128)(2,1)S(1)}, s16[192,512]{1,0:T(8,128)(2,1)S(1)}, u32[]{:S(2)}, u32[]{:S(2)}) collective-permute-start(s16[192,512]{1,0:T(8,128)(2,1)S(1)} %shard_map.48), channel_id=1, source_target_pairs={{0,16},{16,32},{32,48},{48,64},{64,80},{80,96},{96,112},{112,128},... | collective-permute-start | bytes 589832 | tf_op jit(solution)/shard_map/ppermute | solution.py:421
  101.8 7.7 %collective-permute-start.4 = (s16[192,512]{1,0:T(8,128)(2,1)S(1)}, s16[192,512]{1,0:T(8,128)(2,1)S(1)}, u32[]{:S(2)}, u32[]{:S(2)}) collective-permute-start(s16[192,512]{1,0:T(8,128)(2,1)S(1)} %get-tuple-element.41), channel_id=1, source_target_pairs={{16,32},{32,16},{48,64},{64,48},{80,96},{96,80},{112,128},{128,112... | collective-permute-start | bytes 589832 | tf_op jit(solution)/shard_map/ppermute | solution.py:417
  106.2 3.3 %collective-permute-start.5 = (s16[192,512]{1,0:T(8,128)(2,1)S(1)}, s16[192,512]{1,0:T(8,128)(2,1)S(1)}, u32[]{:S(2)}, u32[]{:S(2)}) collective-permute-start(s16[192,512]{1,0:T(8,128)(2,1)S(1)} %get-tuple-element.42), channel_id=1, source_target_pairs={{0,16},{16,0},{32,48},{48,32},{64,80},{80,64},{96,112},{112,96},{1... | collective-permute-start | bytes 589832 | tf_op jit(solution)/shard_map/ppermute | solution.py:418
  110.8 7.0 %collective-permute-start.6 = (s16[192,512]{1,0:T(8,128)(2,1)S(1)}, s16[192,512]{1,0:T(8,128)(2,1)S(1)}, u32[]{:S(2)}, u32[]{:S(2)}) collective-permute-start(s16[192,512]{1,0:T(8,128)(2,1)S(1)} %get-tuple-element.44), channel_id=1, source_target_pairs={{16,32},{32,16},{48,64},{64,48},{80,96},{96,80},{112,128},{128,112... | collective-permute-start | bytes 589832 | tf_op jit(solution)/shard_map/ppermute | solution.py:417
  114.4 3.4 %collective-permute-start.7 = (s16[192,512]{1,0:T(8,128)(2,1)S(1)}, s16[192,512]{1,0:T(8,128)(2,1)S(1)}, u32[]{:S(2)}, u32[]{:S(2)}) collective-permute-start(s16[192,512]{1,0:T(8,128)(2,1)S(1)} %get-tuple-element.45), channel_id=1, source_target_pairs={{0,16},{16,0},{32,48},{48,32},{64,80},{80,64},{96,112},{112,96},{1... | collective-permute-start | bytes 589832 | tf_op jit(solution)/shard_map/ppermute | solution.py:418

commit v6 on v5

--- a/solution.py
+++ b/solution.py
@@ -14,7 +14,9 @@
 TILE = 128
 SIDE = W // TILE
 UPPER = tuple((p, q) for p in range(SIDE) for q in range(p, SIDE))
-LOWER = tuple((p, q) for p in range(SIDE) for q in range(p + 1))
+LOWER = tuple((p, q) for q in range(SIDE) for p in range(q, SIDE))
+HEAD = tuple(t for t in LOWER if t[1] < SIDE // 2)
+TAIL = tuple(t for t in LOWER if t[1] >= SIDE // 2)
 NT = len(UPPER)
 CODE = 32000.0
 HALF = 32768
@@ -30,16 +32,15 @@
     return high, (a - high.astype(f32)).astype(bf16)
 
 
-def call(kernel, outs, *args, far=(), scratch=()):
+def call(kernel, outs, *args):
     spec = pl.BlockSpec(memory_space=pltpu.VMEM)
     return pl.pallas_call(
         kernel,
         out_shape=outs,
-        in_specs=[pl.BlockSpec(memory_space=pl.ANY) if k in far else spec for k in range(len(args))],
-        scratch_shapes=scratch,
+        in_specs=[spec] * len(args),
         out_specs=jax.tree.map(lambda _: spec, outs, is_leaf=lambda o: not isinstance(o, tuple)),
         compiler_params=pltpu.CompilerParams(vmem_limit_bytes=16 << 20),
-    )(*(a if k in far else pltpu.with_memory_space_constraint(a, pltpu.VMEM) for k, a in enumerate(args)))
+    )(*(pltpu.with_memory_space_constraint(a, pltpu.VMEM) for a in args))
 
 
 def shape(*dims, dtype=f32):
@@ -50,10 +51,10 @@
     return matrix[p * TILE : (p + 1) * TILE, q * TILE : (q + 1) * TILE]
 
 
-def pack_tiles(gram, tiles, put, peers):
+def pack_tiles(tiles, block, peers, put):
     rows = TILE // peers
-    pieces = [tile_of(gram, p, q).reshape(peers, rows, TILE) for p, q in tiles]
-    for u in range(len(tiles) // 2):
+    pieces = [tile.reshape(peers, rows, TILE) for tile in tiles] + sums(block, peers, rows)
+    for u in range(len(pieces) // 2):
         pair = jnp.concatenate(pieces[2 * u : 2 * u + 2], axis=1)
         put(2 * rows * u, pair.astype(i32).astype(i16))
 
@@ -62,7 +63,7 @@
     return lax.broadcasted_iota(i32, (TILE, TILE), 0) == lax.broadcasted_iota(i32, (TILE, TILE), 1)
 
 
-def sums(block, peers):
+def sums(block, peers, rows):
     high = 0.0, 0.0
     step = 16
     for lo in range(0, block.shape[0], 60 * step):
@@ -72,13 +73,15 @@
             near, square = (x, x * x) if near is None else (near + x, square + x * x)
         high = high[0] + near.astype(f32), high[1] + square.astype(f32)
     both = [jnp.sum(v, axis=0, keepdims=True) for v in high]
-    stats = [v[:, q * TILE : (q + 1) * TILE] for v in both for q in range(SIDE)]
-    stats = jnp.concatenate(stats + [jnp.zeros((8, TILE), f32)], axis=0)
-    return jnp.broadcast_to(stats.astype(i32).astype(i16)[None], (peers, 16, TILE))
-
-
-def own_products(x_ref, out_ref):
-    block = x_ref[...]
+    stats = [v[:, at : at + TILE] for v in both for at in range(0, block.shape[1], TILE)]
+    if len(stats) < rows:
+        stats.append(jnp.zeros((rows - len(stats), TILE), f32))
+    stats = jnp.broadcast_to(jnp.concatenate(stats, axis=0)[None], (peers, rows, TILE))
+    return [stats, jnp.zeros_like(stats)] if block.shape[1] == W else [stats]
+
+
+def own_products(first_ref, second_ref, out_ref):
+    block = jnp.concatenate([first_ref[...], second_ref[...]], axis=1)
     near, depth = out_ref.shape[0], out_ref.shape[1] // 2
     peers = 2 * near
 
@@ -87,32 +90,32 @@
             lo = far * depth + at
             out_ref[:, lo : lo + value.shape[1], :] = value[far * near : (far + 1) * near]
 
-    pack_tiles(dot(block.T, block), UPPER, put, peers)
-    put(NT * TILE // peers, sums(block, peers))
-
-
-def next_products(x_ref, next_ref, out_ref, block_ref, sem):
-    peers = out_ref.shape[0]
-    parts = sem.shape[0]
-    length = block_ref.shape[0] // parts
-    spans = [pl.ds(k * length, length) for k in range(parts)]
-    copies = [
-        pltpu.make_async_copy(next_ref.at[span], block_ref.at[span], sem.at[k]) for k, span in enumerate(spans)
-    ]
-    for copy in copies:
-        copy.start()
-    gram = None
-    for copy, span in zip(copies, spans):
-        turned = x_ref[span].T
-        copy.wait()
-        more = dot(turned, block_ref[span])
-        gram = more if gram is None else gram + more
+    gram = dot(block.T, block)
+    pack_tiles([tile_of(gram, p, q) for p, q in UPPER], block, peers, put)
+
+
+def head_products(first_ref, second_ref, next_ref, out_ref):
+    block = next_ref[...]
+    grams = dot(first_ref[...].T, block), dot(second_ref[...].T, block)
 
     def put(at, value):
         out_ref[:, at : at + value.shape[1], :] = value
 
-    pack_tiles(gram, LOWER, put, peers)
-    put(NT * TILE // peers, sums(block_ref[...], peers))
+    half = SIDE // 2
+    pack_tiles([tile_of(grams[p // half], p % half, q) for p, q in HEAD], block, out_ref.shape[0], put)
+
+
+def tail_products(second_ref, next_ref, head_ref, out_ref):
+    block = next_ref[...]
+    gram = dot(second_ref[...].T, block)
+    done = head_ref.shape[1]
+    out_ref[:, :done, :] = head_ref[...]
+
+    def put(at, value):
+        out_ref[:, done + at : done + at + value.shape[1], :] = value
+
+    half = SIDE // 2
+    pack_tiles([tile_of(gram, p - half, q - half) for p, q in TAIL], block, out_ref.shape[0], put)
 
 
 def fold(came_ref, keep_ref, send_ref):
@@ -145,7 +148,10 @@
         return mean, variance, 1.0 / jnp.sqrt(jnp.maximum(variance, FLOOR))
 
     mean, variance, scale = stats(own[NT * rows :])
-    next_mean, _, next_scale = stats(nxt[NT * rows :])
+    slot = {tile: t for t, tile in enumerate(HEAD + ("head",) + TAIL + ("tail",))}
+    half = SIDE // 2
+    parts = [nxt[slot[name] * rows : slot[name] * rows + SIDE] for name in ("head", "tail")]
+    next_mean, _, next_scale = stats(jnp.concatenate([v[k : k + half] for k in (0, half) for v in parts], axis=0))
     diagonal_ref[...] = jnp.concatenate([variance * scale * scale, jnp.zeros((8 - SIDE, TILE), f32)], axis=0)
     lane = lax.broadcasted_iota(i32, (rows, TILE), 1)
     row = lax.broadcasted_iota(i32, (rows, TILE), 0) + lax.axis_index("cols") * rows
@@ -161,7 +167,7 @@
         return jnp.round(cov * row_scale[p] * col_scale[q : q + 1])
 
     upper = {(p, q): code(own, t, p, q, mean, scale) for t, (p, q) in enumerate(UPPER)}
-    lower = {(p, q): code(nxt, t, p, q, next_mean, next_scale) for t, (p, q) in enumerate(LOWER)}
+    lower = {(p, q): code(nxt, slot[p, q], p, q, next_mean, next_scale) for p, q in LOWER}
     codes = []
     for p in range(SIDE):
         for q in range(SIDE):
@@ -361,7 +367,7 @@
 
 
 def shards(genotypes, z_scores):
-    local_samples, _ = genotypes.shape
+    local_samples, variants = genotypes.shape
     blocks = lax.axis_size("genome")
     peers = lax.axis_size("cols")
     samples = local_samples * peers
@@ -374,25 +380,21 @@
     cols = range(peers)
     sides = [list(cols[:near]), list(cols[near:])]
 
-    dosage = genotypes.astype(bf16)
-    next_dosage = lax.ppermute(dosage, "genome", to_left)
-    own = call(own_products, shape(near, 2 * depth, TILE, dtype=i16), dosage)
+    half = variants // 2
+    first = genotypes[:, :half].astype(bf16)
+    next_first = lax.ppermute(first, "genome", to_left)
+    second = lax.optimization_barrier((genotypes, first))[0][:, half:].astype(bf16)
+    next_second = lax.ppermute(second, "genome", to_left)
+    own = call(own_products, shape(near, 2 * depth, TILE, dtype=i16), first, second)
     own = lax.all_to_all(own, "cols", 0, 0, axis_index_groups=sides)
+    head = call(head_products, shape(peers, 8 * rows, TILE, dtype=i16), first, second, next_first)
     keep, far = call(fold, (shape(depth, TILE, dtype=i32), shape(depth, TILE, dtype=i16)), own)
     z = z_scores.T
     vector = shape(*z.shape)
     code = shape(z.shape[0] // 16 * 16 + 16, z.shape[1], dtype=i16)
     z_code = call(start_code, code, z)
-    far, next_dosage = lax.optimization_barrier((far, next_dosage))
     far = lax.ppermute(far, "cols", [(k, (k + near) % peers) for k in cols])
-    nxt = call(
-        next_products,
-        shape(peers, depth, TILE, dtype=i16),
-        dosage,
-        next_dosage,
-        far=(1,),
-        scratch=(pltpu.VMEM(dosage.shape, bf16), pltpu.SemaphoreType.DMA((5,))),
-    )
+    nxt = call(tail_products, shape(peers, depth, TILE, dtype=i16), second, next_second, head)
     z_code, nxt = lax.optimization_barrier((z_code, nxt))
     nxt = lax.all_to_all(nxt, "cols", 0, 0)
     z_next = lax.ppermute(z_code, "genome", to_left)

time: 144 us -> 142 us (0.986)
  waiting for transfers between devices: 42 us -> 36.9 us
    all_to_all x1, waiting for transfers between devices: 14.8 us -> 1.88 us  [shards(): own = lax.all_to_all(own, 'cols', 0, 0, axis_index_groups=sides)]
    ppermute x1 -> x2, waiting for transfers between devices: 0.01 us -> 7.75 us  [the longest x1 7.75 us: shards(): next_second = lax.ppermute(second, 'genome', to_left)]
    another operation x0 -> x2, other arithmetic: none -> 3.46 us
    convert_element_type x1 -> x0, other arithmetic: 2.65 us -> none  [shards(): dosage = genotypes.astype(bf16)]
    ppermute x1 -> x2, starting transfers between devices: 8.88 us -> 10.7 us  [the longest x1 8.75 us: shards(): next_first = lax.ppermute(first, 'genome', to_left)]
    pallas_call x15 -> x16, Pallas kernels: 15 us -> 15.5 us  [call(): pl.pallas_call(kernel, out_shape=outs, in_specs=[spec] * len(args), out_s...]
  transfers between devices with their start and end apart: 11 -> 12, of which waited for: 7 -> 8; matrix products, arithmetic and copies ran while one was open for 0% -> 1% of each run, Pallas kernels for 4% -> 7%
where the time goes in v6:
time: 142 us; the launch traced here: 141 us
  starting transfers between devices  60.6 us (43%)
  waiting for transfers between devices  36.9 us (26%)
  blocking collectives  23.6 us (17%)
  Pallas kernels  15.5 us (11%)
  other arithmetic  3.46 us (2%)
    all_to_all x1, blocking collectives, shards(): moments = lax.all_to_all(moments, 'genome', 0, 0)  23.6 us
    all_to_all x1, waiting for transfers between devices, shards(): codes = lax.all_to_all(codes, 'cols', 0, 0)  16.9 us
    pallas_call x16, Pallas kernels, call(): pl.pallas_call(kernel, out_shape=outs, in_specs=[spec] * len(args), out_s...  15.5 us
    all_to_all x1, starting transfers between devices, shards(): nxt = lax.all_to_all(nxt, 'cols', 0, 0)  12.6 us
    ppermute x1, starting transfers between devices, shards(): next_first = lax.ppermute(first, 'genome', to_left)  8.75 us
    ppermute x2, starting transfers between devices, step(): out = lax.ppermute(out, 'genome', across)  7.95 us
    ppermute x1, waiting for transfers between devices, shards(): next_second = lax.ppermute(second, 'genome', to_left)  7.75 us
    ppermute x1, starting transfers between devices, shards(): far = lax.ppermute(far, 'cols', [(k, (k + near) % peers) for k in cols])  7.16 us
  transfers between devices with their start and end apart: 12, of which 8 were waited for; matrix products, arithmetic and copies ran while one was open for 1% of the time, Pallas kernels for 7%

profile of v6, /device:TPU:1, one launch (start us, length us, event | category | flops | bytes accessed | tf_op | source)
XLA Modules:
  0.0 140.9 jit_solution(9698178899475311386)
XLA Ops:
  0.6 0.0 copy-start
  0.6 1.8 %slice_convert_fusion.1.first_ref = bf16[1920,256]{1,0:T(8,128)(2,1)S(1)} fusion(s32[1920,512]{1,0:T(8,128)} %param.2), kind=kLoop, calls=%fused_computation.1 | loop fusion | flops 491520 | bytes 2949120 | tf_op jit(solution)/shard_map/convert.1
  2.4 8.7 %collective-permute-start.2 = (bf16[1920,256]{1,0:T(8,128)(2,1)S(1)}, bf16[1920,256]{1,0:T(8,128)(2,1)}, u32[]{:S(2)}, u32[]{:S(2)}) collective-permute-start(bf16[1920,256]{1,0:T(8,128)(2,1)S(1)} %slice_convert_fusion.1.first_ref), channel_id=1, source_target_pairs={{16,0},{32,16},{48,32},{64,48},{80,64},{96,80},{112,96},{128,112},... | collective-permute-start | bytes 2949128 | tf_op jit(solution)/shard_map/ppermute | solution.py:385
  11.2 1.7 %slice_convert_fusion.second_ref = bf16[1920,256]{1,0:T(8,128)(2,1)S(1)} fusion(s32[1920,512]{1,0:T(8,128)} %param.2), kind=kLoop, calls=%fused_computation | loop fusion | flops 491520 | bytes 2949120 | tf_op jit(solution)/shard_map/convert
  12.9 1.9 %collective-permute-start.1 = (bf16[1920,256]{1,0:T(8,128)(2,1)S(1)}, bf16[1920,256]{1,0:T(8,128)(2,1)}, u32[]{:S(2)}, u32[]{:S(2)}) collective-permute-start(bf16[1920,256]{1,0:T(8,128)(2,1)S(1)} %slice_convert_fusion.second_ref), channel_id=1, source_target_pairs={{16,0},{32,16},{48,32},{64,48},{80,64},{96,80},{112,96},{128,112},... | collective-permute-start | bytes 2949128 | tf_op jit(solution)/shard_map/ppermute | solution.py:387
  14.8 2.0 %shard_map.41 = s16[8,192,128]{2,1,0:T(8,128)(2,1)} custom-call(bf16[1920,256]{1,0:T(8,128)(2,1)S(1)} %slice_convert_fusion.1.first_ref, bf16[1920,256]{1,0:T(8,128)(2,1)S(1)} %slice_convert_fusion.second_ref), custom_call_target="tpu_custom_call" | custom-call | tf_op jit(solution)/shard_map/pallas_call | solution.py:37
  16.8 3.5 %all-to-all-start = ((s16[8,192,128]{2,1,0:T(8,128)(2,1)}), s16[8,192,128]{2,1,0:T(8,128)(2,1)S(1)}, u32[]{:S(2)}, u32[]{:S(2)}) async-start(s16[8,192,128]{2,1,0:T(8,128)(2,1)} %shard_map.41), calls=%async_computation | async-start | bytes 786432 | tf_op jit(solution)/shard_map/all_to_all | solution.py:389
  20.3 0.0 copy-done
  20.3 0.2 shard_map.43
  20.5 0.0 collective-permute-done.2.next_ref
  20.5 2.0 %shard_map.44.head_ref = s16[16,64,128]{2,1,0:T(8,128)(2,1)S(1)} custom-call(bf16[1920,256]{1,0:T(8,128)(2,1)S(1)} %slice_convert_fusion.1.first_ref, bf16[1920,256]{1,0:T(8,128)(2,1)S(1)} %slice_convert_fusion.second_ref, bf16[1920,256]{1,0:T(8,128)(2,1)} %collective-permute-done.2.next_ref), custom_call_target="tpu_custom_call" | custom-call | tf_op jit(solution)/shard_map/pallas_call | solution.py:37
  22.4 7.7 %collective-permute-done.1.next_ref = bf16[1920,256]{1,0:T(8,128)(2,1)} collective-permute-done((bf16[1920,256]{1,0:T(8,128)(2,1)S(1)}, bf16[1920,256]{1,0:T(8,128)(2,1)}, u32[]{:S(2)}, u32[]{:S(2)}) %collective-permute-start.1) | collective-permute-done | bytes 983072 | tf_op jit(solution)/shard_map/ppermute | solution.py:387
  30.2 2.5 %shard_map.45 = s16[16,96,128]{2,1,0:T(8,128)(2,1)} custom-call(bf16[1920,256]{1,0:T(8,128)(2,1)S(1)} %slice_convert_fusion.second_ref, bf16[1920,256]{1,0:T(8,128)(2,1)} %collective-permute-done.1.next_ref, s16[16,64,128]{2,1,0:T(8,128)(2,1)S(1)} %shard_map.44.head_ref), custom_call_target="tpu_custom_call" | custom-call | tf_op jit(solution)/shard_map/pallas_call | solution.py:37
  32.7 1.9 %all-to-all-done.came_ref = s16[8,192,128]{2,1,0:T(8,128)(2,1)S(1)} async-done(((s16[8,192,128]{2,1,0:T(8,128)(2,1)}), s16[8,192,128]{2,1,0:T(8,128)(2,1)S(1)}, u32[]{:S(2)}, u32[]{:S(2)}) %all-to-all-start) | async-done | bytes 393248 | tf_op jit(solution)/shard_map/all_to_all | solution.py:389
  34.5 12.6 %all-to-all-start.1 = ((s16[16,96,128]{2,1,0:T(8,128)(2,1)}), s16[16,96,128]{2,1,0:T(8,128)(2,1)S(1)}, u32[]{:S(2)}, u32[]{:S(2)}) async-start(s16[16,96,128]{2,1,0:T(8,128)(2,1)} %shard_map.45), calls=%async_computation.1 | async-start | bytes 786432 | tf_op jit(solution)/shard_map/all_to_all | solution.py:399
  47.1 0.1 shard_map.42
  47.2 7.2 %collective-permute-start = (s16[96,128]{1,0:T(8,128)(2,1)S(1)}, s16[96,128]{1,0:T(8,128)(2,1)S(1)}, u32[]{:S(2)}, u32[]{:S(2)}) collective-permute-start(s16[96,128]{1,0:T(8,128)(2,1)S(1)} %get-tuple-element.27), channel_id=1, source_target_pairs={{0,8},{1,9},{2,10},{3,11},{4,12},{5,13},{6,14},{7,15},{8,0},{9,1},... | collective-permute-start | bytes 73736 | tf_op jit(solution)/shard_map/ppermute | solution.py:396
  54.4 2.8 %collective-permute-done.far_ref = s16[96,128]{1,0:T(8,128)(2,1)S(1)} collective-permute-done((s16[96,128]{1,0:T(8,128)(2,1)S(1)}, s16[96,128]{1,0:T(8,128)(2,1)S(1)}, u32[]{:S(2)}, u32[]{:S(2)}) %collective-permute-start) | collective-permute-done | bytes 24608 | tf_op jit(solution)/shard_map/ppermute | solution.py:396
  57.2 3.9 %all-to-all-done.1.next_ref = s16[16,96,128]{2,1,0:T(8,128)(2,1)S(1)} async-done(((s16[16,96,128]{2,1,0:T(8,128)(2,1)}), s16[16,96,128]{2,1,0:T(8,128)(2,1)S(1)}, u32[]{:S(2)}, u32[]{:S(2)}) %all-to-all-start.1) | async-done | bytes 393248 | tf_op jit(solution)/shard_map/all_to_all | solution.py:399
  61.1 1.0 shard_map.46
  62.1 6.8 %all-to-all-start.2 = ((s16[16,128,128]{2,1,0:T(8,128)(2,1)}), s16[16,128,128]{2,1,0:T(8,128)(2,1)S(1)}, u32[]{:S(2)}, u32[]{:S(2)}) async-start(s16[16,128,128]{2,1,0:T(8,128)(2,1)} %get-tuple-element.29), calls=%async_computation.2 | async-start | bytes 1048576 | tf_op jit(solution)/shard_map/all_to_all | solution.py:408
  68.9 1.9 %collective-permute-start.4 = (s16[192,512]{1,0:T(8,128)(2,1)S(1)}, s16[192,512]{1,0:T(8,128)(2,1)S(1)}, u32[]{:S(2)}, u32[]{:S(2)}) collective-permute-start(s16[192,512]{1,0:T(8,128)(2,1)S(1)} %shard_map.43), channel_id=1, source_target_pairs={{16,0},{32,16},{48,32},{64,48},{80,64},{96,80},{112,96},{128,112},... | collective-permute-start | bytes 589832 | tf_op jit(solution)/shard_map/ppermute | solution.py:400
  70.8 16.9 %all-to-all-done.2.codes_ref = s16[16,128,128]{2,1,0:T(8,128)(2,1)S(1)} async-done(((s16[16,128,128]{2,1,0:T(8,128)(2,1)}), s16[16,128,128]{2,1,0:T(8,128)(2,1)S(1)}, u32[]{:S(2)}, u32[]{:S(2)}) %all-to-all-start.2) | async-done | bytes 524320 | tf_op jit(solution)/shard_map/all_to_all | solution.py:408
  87.8 0.9 shard_map.47
  88.7 0.6 shard_map.49
  89.3 6.2 %collective-permute-start.3 = (s16[192,512]{1,0:T(8,128)(2,1)S(1)}, s16[192,512]{1,0:T(8,128)(2,1)S(1)}, u32[]{:S(2)}, u32[]{:S(2)}) collective-permute-start(s16[192,512]{1,0:T(8,128)(2,1)S(1)} %shard_map.49), channel_id=1, source_target_pairs={{0,16},{16,32},{32,48},{48,64},{64,80},{80,96},{96,112},{112,128},... | collective-permute-start | bytes 589832 | tf_op jit(solution)/shard_map/ppermute | solution.py:423
  95.5 0.5 shard_map.48.part_ref
  96.0 0.0 collective-permute-done.4.next_ref
  96.0 2.1 %collective-permute-done.3.came_ref = s16[192,512]{1,0:T(8,128)(2,1)S(1)} collective-permute-done((s16[192,512]{1,0:T(8,128)(2,1)S(1)}, s16[192,512]{1,0:T(8,128)(2,1)S(1)}, u32[]{:S(2)}, u32[]{:S(2)}) %collective-permute-start.3) | collective-permute-done | bytes 196640 | tf_op jit(solution)/shard_map/ppermute | solution.py:423
  98.1 1.2 shard_map.50
  99.3 4.3 %collective-permute-start.5 = (s16[192,512]{1,0:T(8,128)(2,1)S(1)}, s16[192,512]{1,0:T(8,128)(2,1)S(1)}, u32[]{:S(2)}, u32[]{:S(2)}) collective-permute-start(s16[192,512]{1,0:T(8,128)(2,1)S(1)} %get-tuple-element.39), channel_id=1, source_target_pairs={{16,32},{32,16},{48,64},{64,48},{80,96},{96,80},{112,128},{128,112... | collective-permute-start | bytes 589832 | tf_op jit(solution)/shard_map/ppermute | solution.py:419
  103.7 1.9 %collective-permute-start.6 = (s16[192,512]{1,0:T(8,128)(2,1)S(1)}, s16[192,512]{1,0:T(8,128)(2,1)S(1)}, u32[]{:S(2)}, u32[]{:S(2)}) collective-permute-start(s16[192,512]{1,0:T(8,128)(2,1)S(1)} %get-tuple-element.40), channel_id=1, source_target_pairs={{0,16},{16,0},{32,48},{48,32},{64,80},{80,64},{96,112},{112,96},{1... | collective-permute-start | bytes 589832 | tf_op jit(solution)/shard_map/ppermute | solution.py:420
  105.6 0.5 shard_map.51.part_ref
  106.1 0.9 collective-permute-done.5.across_in
  107.0 0.0 collective-permute-done.6.inside_in
  107.0 1.3 shard_map.52
  108.3 3.6 %collective-permute-start.7 = (s16[192,512]{1,0:T(8,128)(2,1)S(1)}, s16[192,512]{1,0:T(8,128)(2,1)S(1)}, u32[]{:S(2)}, u32[]{:S(2)}) collective-permute-start(s16[192,512]{1,0:T(8,128)(2,1)S(1)} %get-tuple-element.42), channel_id=1, source_target_pairs={{16,32},{32,16},{48,64},{64,48},{80,96},{96,80},{112,128},{128,112... | collective-permute-start | bytes 589832 | tf_op jit(solution)/shard_map/ppermute | solution.py:419
  111.9 1.9 %collective-permute-start.8 = (s16[192,512]{1,0:T(8,128)(2,1)S(1)}, s16[192,512]{1,0:T(8,128)(2,1)S(1)}, u32[]{:S(2)}, u32[]{:S(2)}) collective-permute-start(s16[192,512]{1,0:T(8,128)(2,1)S(1)} %get-tuple-element.43), channel_id=1, source_target_pairs={{0,16},{16,0},{32,48},{48,32},{64,80},{80,64},{96,112},{112,96},{1... | collective-permute-start | bytes 589832 | tf_op jit(solution)/shard_map/ppermute | solution.py:420
  113.8 0.5 shard_map.53.part_ref
  114.3 0.2 shard_map.54.early_ref
  114.5 0.7 collective-permute-done.7.across_in
  115.2 0.0 collective-permute-done.8.inside_in
  115.3 0.7 shard_map.55
  116.0 23.6 %all_to_all.20.moments_ref = f32[32,8,256]{2,1,0:T(8,128)S(1)} all-to-all(f32[32,8,256]{2,1,0:T(8,128)S(1)} %get-tuple-element.44), channel_id=1, replica_groups=mesh['genome'=32,'cols'=16] {'genome'}, dimensions={0} | all-to-all | bytes 524288 | tf_op jit(solution)/shard_map/all_to_all | solution.py:430
  139.5 1.4 shard_map.56
Async XLA Ops:
  0.6 19.7 %copy-start = (f32[512,184]{0,1:T(8,128)S(1)}, f32[512,184]{0,1:T(8,128)}, u32[]{:S(2)}) copy-start(f32[512,184]{0,1:T(8,128)} %param.3) | copy-start | bytes 1130500
  2.4 18.1 %collective-permute-start.2 = (bf16[1920,256]{1,0:T(8,128)(2,1)S(1)}, bf16[1920,256]{1,0:T(8,128)(2,1)}, u32[]{:S(2)}, u32[]{:S(2)}) collective-permute-start(bf16[1920,256]{1,0:T(8,128)(2,1)S(1)} %slice_convert_fusion.1.first_ref), channel_id=1, source_target_pairs={{16,0},{32,16},{48,32},{64,48},{80,64},{96,80},{112,96},{128,112},... | collective-permute-start | bytes 2949128 | tf_op jit(solution)/shard_map/ppermute | solution.py:385
  12.9 17.3 %collective-permute-start.1 = (bf16[1920,256]{1,0:T(8,128)(2,1)S(1)}, bf16[1920,256]{1,0:T(8,128)(2,1)}, u32[]{:S(2)}, u32[]{:S(2)}) collective-permute-start(bf16[1920,256]{1,0:T(8,128)(2,1)S(1)} %slice_convert_fusion.second_ref), channel_id=1, source_target_pairs={{16,0},{32,16},{48,32},{64,48},{80,64},{96,80},{112,96},{128,112},... | collective-permute-start | bytes 2949128 | tf_op jit(solution)/shard_map/ppermute | solution.py:387
  16.8 17.7 %all-to-all-start = ((s16[8,192,128]{2,1,0:T(8,128)(2,1)}), s16[8,192,128]{2,1,0:T(8,128)(2,1)S(1)}, u32[]{:S(2)}, u32[]{:S(2)}) async-start(s16[8,192,128]{2,1,0:T(8,128)(2,1)} %shard_map.41), calls=%async_computation | async-start | bytes 786432 | tf_op jit(solution)/shard_map/all_to_all | solution.py:389
  34.5 26.5 %all-to-all-start.1 = ((s16[16,96,128]{2,1,0:T(8,128)(2,1)}), s16[16,96,128]{2,1,0:T(8,128)(2,1)S(1)}, u32[]{:S(2)}, u32[]{:S(2)}) async-start(s16[16,96,128]{2,1,0:T(8,128)(2,1)} %shard_map.45), calls=%async_computation.1 | async-start | bytes 786432 | tf_op jit(solution)/shard_map/all_to_all | solution.py:399
  47.2 9.9 %collective-permute-start = (s16[96,128]{1,0:T(8,128)(2,1)S(1)}, s16[96,128]{1,0:T(8,128)(2,1)S(1)}, u32[]{:S(2)}, u32[]{:S(2)}) collective-permute-start(s16[96,128]{1,0:T(8,128)(2,1)S(1)} %get-tuple-element.27), channel_id=1, source_target_pairs={{0,8},{1,9},{2,10},{3,11},{4,12},{5,13},{6,14},{7,15},{8,0},{9,1},... | collective-permute-start | bytes 73736 | tf_op jit(solution)/shard_map/ppermute | solution.py:396
  62.1 25.7 %all-to-all-start.2 = ((s16[16,128,128]{2,1,0:T(8,128)(2,1)}), s16[16,128,128]{2,1,0:T(8,128)(2,1)S(1)}, u32[]{:S(2)}, u32[]{:S(2)}) async-start(s16[16,128,128]{2,1,0:T(8,128)(2,1)} %get-tuple-element.29), calls=%async_computation.2 | async-start | bytes 1048576 | tf_op jit(solution)/shard_map/all_to_all | solution.py:408
  68.9 27.1 %collective-permute-start.4 = (s16[192,512]{1,0:T(8,128)(2,1)S(1)}, s16[192,512]{1,0:T(8,128)(2,1)S(1)}, u32[]{:S(2)}, u32[]{:S(2)}) collective-permute-start(s16[192,512]{1,0:T(8,128)(2,1)S(1)} %shard_map.43), channel_id=1, source_target_pairs={{16,0},{32,16},{48,32},{64,48},{80,64},{96,80},{112,96},{128,112},... | collective-permute-start | bytes 589832 | tf_op jit(solution)/shard_map/ppermute | solution.py:400
  89.3 8.8 %collective-permute-start.3 = (s16[192,512]{1,0:T(8,128)(2,1)S(1)}, s16[192,512]{1,0:T(8,128)(2,1)S(1)}, u32[]{:S(2)}, u32[]{:S(2)}) collective-permute-start(s16[192,512]{1,0:T(8,128)(2,1)S(1)} %shard_map.49), channel_id=1, source_target_pairs={{0,16},{16,32},{32,48},{48,64},{64,80},{80,96},{96,112},{112,128},... | collective-permute-start | bytes 589832 | tf_op jit(solution)/shard_map/ppermute | solution.py:423
  99.3 7.7 %collective-permute-start.5 = (s16[192,512]{1,0:T(8,128)(2,1)S(1)}, s16[192,512]{1,0:T(8,128)(2,1)S(1)}, u32[]{:S(2)}, u32[]{:S(2)}) collective-permute-start(s16[192,512]{1,0:T(8,128)(2,1)S(1)} %get-tuple-element.39), channel_id=1, source_target_pairs={{16,32},{32,16},{48,64},{64,48},{80,96},{96,80},{112,128},{128,112... | collective-permute-start | bytes 589832 | tf_op jit(solution)/shard_map/ppermute | solution.py:419
  103.7 3.3 %collective-permute-start.6 = (s16[192,512]{1,0:T(8,128)(2,1)S(1)}, s16[192,512]{1,0:T(8,128)(2,1)S(1)}, u32[]{:S(2)}, u32[]{:S(2)}) collective-permute-start(s16[192,512]{1,0:T(8,128)(2,1)S(1)} %get-tuple-element.40), channel_id=1, source_target_pairs={{0,16},{16,0},{32,48},{48,32},{64,80},{80,64},{96,112},{112,96},{1... | collective-permute-start | bytes 589832 | tf_op jit(solution)/shard_map/ppermute | solution.py:420
  108.3 7.0 %collective-permute-start.7 = (s16[192,512]{1,0:T(8,128)(2,1)S(1)}, s16[192,512]{1,0:T(8,128)(2,1)S(1)}, u32[]{:S(2)}, u32[]{:S(2)}) collective-permute-start(s16[192,512]{1,0:T(8,128)(2,1)S(1)} %get-tuple-element.42), channel_id=1, source_target_pairs={{16,32},{32,16},{48,64},{64,48},{80,96},{96,80},{112,128},{128,112... | collective-permute-start | bytes 589832 | tf_op jit(solution)/shard_map/ppermute | solution.py:419
  111.9 3.4 %collective-permute-start.8 = (s16[192,512]{1,0:T(8,128)(2,1)S(1)}, s16[192,512]{1,0:T(8,128)(2,1)S(1)}, u32[]{:S(2)}, u32[]{:S(2)}) collective-permute-start(s16[192,512]{1,0:T(8,128)(2,1)S(1)} %get-tuple-element.43), channel_id=1, source_target_pairs={{0,16},{16,0},{32,48},{48,32},{64,80},{80,64},{96,112},{112,96},{1... | collective-permute-start | bytes 589832 | tf_op jit(solution)/shard_map/ppermute | solution.py:420

commit v7 on v6

--- a/solution.py
+++ b/solution.py
@@ -80,8 +80,10 @@
     return [stats, jnp.zeros_like(stats)] if block.shape[1] == W else [stats]
 
 
-def own_products(first_ref, second_ref, out_ref):
+def own_products(first_ref, second_ref, out_ref, turned_ref):
     block = jnp.concatenate([first_ref[...], second_ref[...]], axis=1)
+    turned = block.T
+    turned_ref[...] = turned[turned_ref.shape[0] :]
     near, depth = out_ref.shape[0], out_ref.shape[1] // 2
     peers = 2 * near
 
@@ -90,13 +92,13 @@
             lo = far * depth + at
             out_ref[:, lo : lo + value.shape[1], :] = value[far * near : (far + 1) * near]
 
-    gram = dot(block.T, block)
+    gram = dot(turned, block)
     pack_tiles([tile_of(gram, p, q) for p, q in UPPER], block, peers, put)
 
 
-def head_products(first_ref, second_ref, next_ref, out_ref):
+def head_products(first_ref, turned_ref, next_ref, out_ref):
     block = next_ref[...]
-    grams = dot(first_ref[...].T, block), dot(second_ref[...].T, block)
+    grams = dot(first_ref[...].T, block), dot(turned_ref[...], block)
 
     def put(at, value):
         out_ref[:, at : at + value.shape[1], :] = value
@@ -105,9 +107,9 @@
     pack_tiles([tile_of(grams[p // half], p % half, q) for p, q in HEAD], block, out_ref.shape[0], put)
 
 
-def tail_products(second_ref, next_ref, head_ref, out_ref):
+def tail_products(turned_ref, next_ref, head_ref, out_ref):
     block = next_ref[...]
-    gram = dot(second_ref[...].T, block)
+    gram = dot(turned_ref[...], block)
     done = head_ref.shape[1]
     out_ref[:, :done, :] = head_ref[...]
 
@@ -187,7 +189,7 @@
     return jnp.maximum(1.0 - reach / (W + 1), 0.0)
 
 
-def unpack(codes_ref, diagonal_ref, near_high, near_low, next_high, next_low, back_high, back_low):
+def unpack(codes_ref, diagonal_ref, v_ref, near_high, near_low, next_high, next_low, back_high, back_low, out_ref):
     peers = codes_ref.shape[0]
     rows = TILE // peers
 
@@ -226,6 +228,7 @@
                 else:
                     put(next_high, next_low, p, q, zero)
                     put(back_high, back_low, q, p, zero)
+    encode(product(v_ref[...], next_high, next_low), out_ref)
 
 
 def product(v, high_ref, low_ref):
@@ -255,10 +258,6 @@
 
 def start_code(v_ref, out_ref):
     encode(v_ref[...], out_ref)
-
-
-def outward(v_ref, high_ref, low_ref, out_ref):
-    encode(product(v_ref[...], high_ref, low_ref), out_ref)
 
 
 def inward(v_ref, high_ref, low_ref, out_ref):
@@ -385,17 +384,21 @@
     next_first = lax.ppermute(first, "genome", to_left)
     second = lax.optimization_barrier((genotypes, first))[0][:, half:].astype(bf16)
     next_second = lax.ppermute(second, "genome", to_left)
-    own = call(own_products, shape(near, 2 * depth, TILE, dtype=i16), first, second)
+    own, turned = call(
+        own_products,
+        (jax.ShapeDtypeStruct((near, 2 * depth, TILE), i16), shape(half, local_samples, dtype=bf16)),
+        first,
+        second,
+    )
     own = lax.all_to_all(own, "cols", 0, 0, axis_index_groups=sides)
-    head = call(head_products, shape(peers, 8 * rows, TILE, dtype=i16), first, second, next_first)
+    head = call(head_products, shape(peers, 8 * rows, TILE, dtype=i16), first, turned, next_first)
     keep, far = call(fold, (shape(depth, TILE, dtype=i32), shape(depth, TILE, dtype=i16)), own)
     z = z_scores.T
     vector = shape(*z.shape)
     code = shape(z.shape[0] // 16 * 16 + 16, z.shape[1], dtype=i16)
     z_code = call(start_code, code, z)
     far = lax.ppermute(far, "cols", [(k, (k + near) % peers) for k in cols])
-    nxt = call(tail_products, shape(peers, depth, TILE, dtype=i16), second, next_second, head)
-    z_code, nxt = lax.optimization_barrier((z_code, nxt))
+    nxt = call(tail_products, shape(peers, depth, TILE, dtype=i16), turned, next_second, head)
     nxt = lax.all_to_all(nxt, "cols", 0, 0)
     z_next = lax.ppermute(z_code, "genome", to_left)
     codes, diagonal_row = call(
@@ -405,9 +408,10 @@
         far,
         nxt,
     )
+    codes, z_next = lax.optimization_barrier((codes, z_next))
     codes = lax.all_to_all(codes, "cols", 0, 0)
     square = shape(W, W, dtype=bf16)
-    near_h, near_l, next_h, next_l, back_h, back_l = call(unpack, (square,) * 6, codes, diagonal_row)
+    near_h, near_l, next_h, next_l, back_h, back_l, out = call(unpack, (square,) * 6 + (code,), codes, diagonal_row, z)
 
     inside = [(k, k ^ 1) for k in range(blocks)]
     across = [(k, ((k + 1) ^ 1) - 1) for k in range(1, blocks - 1)]
@@ -420,7 +424,7 @@
         inn = lax.ppermute(inn, "genome", inside)
         return w, call(inward, vector, w, near_h, near_l), out, inn
 
-    came = lax.ppermute(call(outward, code, z, next_h, next_l), "genome", to_right)
+    came = lax.ppermute(out, "genome", to_right)
     one, *rest = step(first_gather, call(inward, vector, z, near_h, near_l), came, z_next)
     two, part, out, inn = step(next_gather, *rest)
     early = call(early_moments, shape(8, 256), z, one, two)

time: 142 us -> 144 us (1.014)
  blocking collectives: 23.6 us -> 51.8 us
  waiting for transfers between devices: 36.9 us -> 18.1 us
  starting transfers between devices: 60.6 us -> 54 us
    all_to_all x0 -> x1, blocking collectives: none -> 26.8 us  [shards(): codes = lax.all_to_all(codes, 'cols', 0, 0)]
    all_to_all x1 -> x0, waiting for transfers between devices: 16.9 us -> none  [shards(): codes = lax.all_to_all(codes, 'cols', 0, 0)]
    all_to_all x1 -> x0, starting transfers between devices: 6.83 us -> none  [shards(): codes = lax.all_to_all(codes, 'cols', 0, 0)]
    all_to_all x1, waiting for transfers between devices: 3.89 us -> 0.01 us  [shards(): nxt = lax.all_to_all(nxt, 'cols', 0, 0)]
    pallas_call x16 -> x15, Pallas kernels: 15.5 us -> 14.4 us  [call(): pl.pallas_call(kernel, out_shape=outs, in_specs=[spec] * len(args), out_s...]
  transfers between devices with their start and end apart: 12 -> 11, of which waited for: 8 -> 6; matrix products, arithmetic and copies ran while one was open for 1% -> 1% of each run, Pallas kernels for 7% -> 6%
where the time goes in v7:
time: 144 us; the launch traced here: 143 us
  starting transfers between devices  54 us (38%)
  blocking collectives  51.8 us (36%)
  waiting for transfers between devices  18.1 us (13%)
  Pallas kernels  14.4 us (10%)
  other arithmetic  3.41 us (2%)
    all_to_all x1, blocking collectives, shards(): codes = lax.all_to_all(codes, 'cols', 0, 0)  26.8 us
    all_to_all x1, blocking collectives, shards(): moments = lax.all_to_all(moments, 'genome', 0, 0)  25 us
    pallas_call x15, Pallas kernels, call(): pl.pallas_call(kernel, out_shape=outs, in_specs=[spec] * len(args), out_s...  14.4 us
    all_to_all x1, starting transfers between devices, shards(): nxt = lax.all_to_all(nxt, 'cols', 0, 0)  11.7 us
    ppermute x1, starting transfers between devices, shards(): next_first = lax.ppermute(first, 'genome', to_left)  8.75 us
    ppermute x2, starting transfers between devices, step(): out = lax.ppermute(out, 'genome', across)  7.93 us
    ppermute x1, starting transfers between devices, shards(): far = lax.ppermute(far, 'cols', [(k, (k + near) % peers) for k in cols])  7.18 us
    ppermute x1, waiting for transfers between devices, shards(): next_second = lax.ppermute(second, 'genome', to_left)  7.17 us
  transfers between devices with their start and end apart: 11, of which 6 were waited for; matrix products, arithmetic and copies ran while one was open for 1% of the time, Pallas kernels for 6%

profile of v7, /device:TPU:1, one launch (start us, length us, event | category | flops | bytes accessed | tf_op | source)
XLA Modules:
  0.0 143.3 jit_solution(7433598707146086295)
XLA Ops:
  0.6 1.7 %slice_convert_fusion.1.first_ref = bf16[1920,256]{1,0:T(8,128)(2,1)S(1)} fusion(s32[1920,512]{1,0:T(8,128)} %param.2), kind=kLoop, calls=%fused_computation.1 | loop fusion | flops 491520 | bytes 2949120 | tf_op jit(solution)/shard_map/convert.1
  2.3 8.7 %collective-permute-start.2 = (bf16[1920,256]{1,0:T(8,128)(2,1)S(1)}, bf16[1920,256]{1,0:T(8,128)(2,1)}, u32[]{:S(2)}, u32[]{:S(2)}) collective-permute-start(bf16[1920,256]{1,0:T(8,128)(2,1)S(1)} %slice_convert_fusion.1.first_ref), channel_id=1, source_target_pairs={{16,0},{32,16},{48,32},{64,48},{80,64},{96,80},{112,96},{128,112},... | collective-permute-start | bytes 2949128 | tf_op jit(solution)/shard_map/ppermute | solution.py:384
  11.1 1.7 %slice_convert_fusion.second_ref = bf16[1920,256]{1,0:T(8,128)(2,1)S(1)} fusion(s32[1920,512]{1,0:T(8,128)} %param.2), kind=kLoop, calls=%fused_computation | loop fusion | flops 491520 | bytes 2949120 | tf_op jit(solution)/shard_map/convert
  12.8 1.9 %collective-permute-start.1 = (bf16[1920,256]{1,0:T(8,128)(2,1)S(1)}, bf16[1920,256]{1,0:T(8,128)(2,1)}, u32[]{:S(2)}, u32[]{:S(2)}) collective-permute-start(bf16[1920,256]{1,0:T(8,128)(2,1)S(1)} %slice_convert_fusion.second_ref), channel_id=1, source_target_pairs={{16,0},{32,16},{48,32},{64,48},{80,64},{96,80},{112,96},{128,112},... | collective-permute-start | bytes 2949128 | tf_op jit(solution)/shard_map/ppermute | solution.py:386
  14.7 1.3 shard_map.41
  16.0 0.0 copy-start.1
  16.0 0.8 copy-done.1
  16.8 0.0 copy-start
  16.8 4.2 %all-to-all-start = ((s16[8,192,128]{2,1,0:T(8,128)(2,1)}), s16[8,192,128]{2,1,0:T(8,128)(2,1)}, u32[]{:S(2)}, u32[]{:S(2)}) async-start(s16[8,192,128]{2,1,0:T(8,128)(2,1)} %copy-done.1), calls=%async_computation | async-start | bytes 786432 | tf_op jit(solution)/shard_map/all_to_all | solution.py:393
  21.0 0.0 collective-permute-done.2.next_ref
  21.0 1.9 %shard_map.43.head_ref = s16[16,64,128]{2,1,0:T(8,128)(2,1)S(1)} custom-call(bf16[1920,256]{1,0:T(8,128)(2,1)S(1)} %slice_convert_fusion.1.first_ref, bf16[256,1920]{1,0:T(8,128)(2,1)S(1)} %get-tuple-element.32.turned_ref, bf16[1920,256]{1,0:T(8,128)(2,1)} %collective-permute-done.2.next_ref), custom_call_target="tpu_custom_call" | custom-call | tf_op jit(solution)/shard_map/pallas_call | solution.py:37
  23.0 7.2 %collective-permute-done.1.next_ref = bf16[1920,256]{1,0:T(8,128)(2,1)} collective-permute-done((bf16[1920,256]{1,0:T(8,128)(2,1)S(1)}, bf16[1920,256]{1,0:T(8,128)(2,1)}, u32[]{:S(2)}, u32[]{:S(2)}) %collective-permute-start.1) | collective-permute-done | bytes 983072 | tf_op jit(solution)/shard_map/ppermute | solution.py:386
  30.1 2.4 %shard_map.44 = s16[16,96,128]{2,1,0:T(8,128)(2,1)} custom-call(bf16[256,1920]{1,0:T(8,128)(2,1)S(1)} %get-tuple-element.32.turned_ref, bf16[1920,256]{1,0:T(8,128)(2,1)} %collective-permute-done.1.next_ref, s16[16,64,128]{2,1,0:T(8,128)(2,1)S(1)} %shard_map.43.head_ref), custom_call_target="tpu_custom_call" | custom-call | tf_op jit(solution)/shard_map/pallas_call | solution.py:37
  32.6 2.8 %all-to-all-done.came_ref = s16[8,192,128]{2,1,0:T(8,128)(2,1)} async-done(((s16[8,192,128]{2,1,0:T(8,128)(2,1)}), s16[8,192,128]{2,1,0:T(8,128)(2,1)}, u32[]{:S(2)}, u32[]{:S(2)}) %all-to-all-start) | async-done | bytes 393248 | tf_op jit(solution)/shard_map/all_to_all | solution.py:393
  35.3 11.7 %all-to-all-start.1 = ((s16[16,96,128]{2,1,0:T(8,128)(2,1)}), s16[16,96,128]{2,1,0:T(8,128)(2,1)S(1)}, u32[]{:S(2)}, u32[]{:S(2)}) async-start(s16[16,96,128]{2,1,0:T(8,128)(2,1)} %shard_map.44), calls=%async_computation.1 | async-start | bytes 786432 | tf_op jit(solution)/shard_map/all_to_all | solution.py:402
  47.0 0.0 copy-done
  47.1 0.2 shard_map.46
  47.2 1.9 %collective-permute-start.3 = (s16[192,512]{1,0:T(8,128)(2,1)S(1)}, s16[192,512]{1,0:T(8,128)(2,1)S(1)}, u32[]{:S(2)}, u32[]{:S(2)}) collective-permute-start(s16[192,512]{1,0:T(8,128)(2,1)S(1)} %shard_map.46), channel_id=1, source_target_pairs={{16,0},{32,16},{48,32},{64,48},{80,64},{96,80},{112,96},{128,112},... | collective-permute-start | bytes 589832 | tf_op jit(solution)/shard_map/ppermute | solution.py:403
  49.1 1.1 shard_map.42
  50.2 7.2 %collective-permute-start = (s16[96,128]{1,0:T(8,128)(2,1)S(1)}, s16[96,128]{1,0:T(8,128)(2,1)S(1)}, u32[]{:S(2)}, u32[]{:S(2)}) collective-permute-start(s16[96,128]{1,0:T(8,128)(2,1)S(1)} %get-tuple-element.31), channel_id=1, source_target_pairs={{0,8},{1,9},{2,10},{3,11},{4,12},{5,13},{6,14},{7,15},{8,0},{9,1},... | collective-permute-start | bytes 73736 | tf_op jit(solution)/shard_map/ppermute | solution.py:400
  57.4 4.2 %collective-permute-done.far_ref = s16[96,128]{1,0:T(8,128)(2,1)S(1)} collective-permute-done((s16[96,128]{1,0:T(8,128)(2,1)S(1)}, s16[96,128]{1,0:T(8,128)(2,1)S(1)}, u32[]{:S(2)}, u32[]{:S(2)}) %collective-permute-start) | collective-permute-done | bytes 24608 | tf_op jit(solution)/shard_map/ppermute | solution.py:400
  61.6 0.0 all-to-all-done.1.next_ref
  61.6 0.2 shard_map.45
  61.8 0.0 collective-permute-done.3.next_ref
  61.8 26.8 %all_to_all.20.codes_ref = s16[16,128,128]{2,1,0:T(8,128)(2,1)S(1)} all-to-all(s16[16,128,128]{2,1,0:T(8,128)(2,1)S(1)} %get-tuple-element.34), channel_id=1, replica_groups=mesh['genome'=32,'cols'=16] {'cols'}, dimensions={0} | all-to-all | bytes 1048576 | tf_op jit(solution)/shard_map/all_to_all | solution.py:412
  88.6 1.2 shard_map.47
  89.9 6.5 %collective-permute-start.4 = (s16[192,512]{1,0:T(8,128)(2,1)S(1)}, s16[192,512]{1,0:T(8,128)(2,1)S(1)}, u32[]{:S(2)}, u32[]{:S(2)}) collective-permute-start(s16[192,512]{1,0:T(8,128)(2,1)S(1)} %get-tuple-element.38), channel_id=1, source_target_pairs={{0,16},{16,32},{32,48},{48,64},{64,80},{80,96},{96,112},{112,128},... | collective-permute-start | bytes 589832 | tf_op jit(solution)/shard_map/ppermute | solution.py:427
  96.4 0.5 shard_map.48.part_ref
  96.9 2.1 %collective-permute-done.4.came_ref = s16[192,512]{1,0:T(8,128)(2,1)S(1)} collective-permute-done((s16[192,512]{1,0:T(8,128)(2,1)S(1)}, s16[192,512]{1,0:T(8,128)(2,1)S(1)}, u32[]{:S(2)}, u32[]{:S(2)}) %collective-permute-start.4) | collective-permute-done | bytes 196640 | tf_op jit(solution)/shard_map/ppermute | solution.py:427
  99.0 1.2 shard_map.49
  100.2 4.3 %collective-permute-start.5 = (s16[192,512]{1,0:T(8,128)(2,1)S(1)}, s16[192,512]{1,0:T(8,128)(2,1)S(1)}, u32[]{:S(2)}, u32[]{:S(2)}) collective-permute-start(s16[192,512]{1,0:T(8,128)(2,1)S(1)} %get-tuple-element.45), channel_id=1, source_target_pairs={{16,32},{32,16},{48,64},{64,48},{80,96},{96,80},{112,128},{128,112... | collective-permute-start | bytes 589832 | tf_op jit(solution)/shard_map/ppermute | solution.py:423
  104.6 1.9 %collective-permute-start.6 = (s16[192,512]{1,0:T(8,128)(2,1)S(1)}, s16[192,512]{1,0:T(8,128)(2,1)S(1)}, u32[]{:S(2)}, u32[]{:S(2)}) collective-permute-start(s16[192,512]{1,0:T(8,128)(2,1)S(1)} %get-tuple-element.46), channel_id=1, source_target_pairs={{0,16},{16,0},{32,48},{48,32},{64,80},{80,64},{96,112},{112,96},{1... | collective-permute-start | bytes 589832 | tf_op jit(solution)/shard_map/ppermute | solution.py:424
  106.5 0.5 shard_map.50.part_ref
  107.0 0.9 collective-permute-done.5.across_in
  107.9 0.0 collective-permute-done.6.inside_in
  107.9 1.2 shard_map.51
  109.2 3.6 %collective-permute-start.7 = (s16[192,512]{1,0:T(8,128)(2,1)S(1)}, s16[192,512]{1,0:T(8,128)(2,1)S(1)}, u32[]{:S(2)}, u32[]{:S(2)}) collective-permute-start(s16[192,512]{1,0:T(8,128)(2,1)S(1)} %get-tuple-element.48), channel_id=1, source_target_pairs={{16,32},{32,16},{48,64},{64,48},{80,96},{96,80},{112,128},{128,112... | collective-permute-start | bytes 589832 | tf_op jit(solution)/shard_map/ppermute | solution.py:423
  112.8 1.9 %collective-permute-start.8 = (s16[192,512]{1,0:T(8,128)(2,1)S(1)}, s16[192,512]{1,0:T(8,128)(2,1)S(1)}, u32[]{:S(2)}, u32[]{:S(2)}) collective-permute-start(s16[192,512]{1,0:T(8,128)(2,1)S(1)} %get-tuple-element.49), channel_id=1, source_target_pairs={{0,16},{16,0},{32,48},{48,32},{64,80},{80,64},{96,112},{112,96},{1... | collective-permute-start | bytes 589832 | tf_op jit(solution)/shard_map/ppermute | solution.py:424
  114.7 0.2 shard_map.53.early_ref
  114.9 0.5 shard_map.52.part_ref
  115.4 0.9 collective-permute-done.7.across_in
  116.3 0.0 collective-permute-done.8.inside_in
  116.3 0.7 shard_map.54
  117.0 25.0 %all_to_all.21.moments_ref = f32[32,8,256]{2,1,0:T(8,128)S(1)} all-to-all(f32[32,8,256]{2,1,0:T(8,128)S(1)} %get-tuple-element.50), channel_id=1, replica_groups=mesh['genome'=32,'cols'=16] {'genome'}, dimensions={0} | all-to-all | bytes 524288 | tf_op jit(solution)/shard_map/all_to_all | solution.py:434
  142.0 1.4 shard_map.55
Async XLA Ops:
  2.3 18.7 %collective-permute-start.2 = (bf16[1920,256]{1,0:T(8,128)(2,1)S(1)}, bf16[1920,256]{1,0:T(8,128)(2,1)}, u32[]{:S(2)}, u32[]{:S(2)}) collective-permute-start(bf16[1920,256]{1,0:T(8,128)(2,1)S(1)} %slice_convert_fusion.1.first_ref), channel_id=1, source_target_pairs={{16,0},{32,16},{48,32},{64,48},{80,64},{96,80},{112,96},{128,112},... | collective-permute-start | bytes 2949128 | tf_op jit(solution)/shard_map/ppermute | solution.py:384
  12.8 17.3 %collective-permute-start.1 = (bf16[1920,256]{1,0:T(8,128)(2,1)S(1)}, bf16[1920,256]{1,0:T(8,128)(2,1)}, u32[]{:S(2)}, u32[]{:S(2)}) collective-permute-start(bf16[1920,256]{1,0:T(8,128)(2,1)S(1)} %slice_convert_fusion.second_ref), channel_id=1, source_target_pairs={{16,0},{32,16},{48,32},{64,48},{80,64},{96,80},{112,96},{128,112},... | collective-permute-start | bytes 2949128 | tf_op jit(solution)/shard_map/ppermute | solution.py:386
  16.0 0.8 copy-start.1
  16.8 30.3 %copy-start = (f32[512,184]{0,1:T(8,128)S(1)}, f32[512,184]{0,1:T(8,128)}, u32[]{:S(2)}) copy-start(f32[512,184]{0,1:T(8,128)} %param.3) | copy-start | bytes 1130500
  16.8 18.6 %all-to-all-start = ((s16[8,192,128]{2,1,0:T(8,128)(2,1)}), s16[8,192,128]{2,1,0:T(8,128)(2,1)}, u32[]{:S(2)}, u32[]{:S(2)}) async-start(s16[8,192,128]{2,1,0:T(8,128)(2,1)} %copy-done.1), calls=%async_computation | async-start | bytes 786432 | tf_op jit(solution)/shard_map/all_to_all | solution.py:393
  35.3 26.3 %all-to-all-start.1 = ((s16[16,96,128]{2,1,0:T(8,128)(2,1)}), s16[16,96,128]{2,1,0:T(8,128)(2,1)S(1)}, u32[]{:S(2)}, u32[]{:S(2)}) async-start(s16[16,96,128]{2,1,0:T(8,128)(2,1)} %shard_map.44), calls=%async_computation.1 | async-start | bytes 786432 | tf_op jit(solution)/shard_map/all_to_all | solution.py:402
  47.2 14.6 %collective-permute-start.3 = (s16[192,512]{1,0:T(8,128)(2,1)S(1)}, s16[192,512]{1,0:T(8,128)(2,1)S(1)}, u32[]{:S(2)}, u32[]{:S(2)}) collective-permute-start(s16[192,512]{1,0:T(8,128)(2,1)S(1)} %shard_map.46), channel_id=1, source_target_pairs={{16,0},{32,16},{48,32},{64,48},{80,64},{96,80},{112,96},{128,112},... | collective-permute-start | bytes 589832 | tf_op jit(solution)/shard_map/ppermute | solution.py:403
  50.2 11.4 %collective-permute-start = (s16[96,128]{1,0:T(8,128)(2,1)S(1)}, s16[96,128]{1,0:T(8,128)(2,1)S(1)}, u32[]{:S(2)}, u32[]{:S(2)}) collective-permute-start(s16[96,128]{1,0:T(8,128)(2,1)S(1)} %get-tuple-element.31), channel_id=1, source_target_pairs={{0,8},{1,9},{2,10},{3,11},{4,12},{5,13},{6,14},{7,15},{8,0},{9,1},... | collective-permute-start | bytes 73736 | tf_op jit(solution)/shard_map/ppermute | solution.py:400
  89.9 9.1 %collective-permute-start.4 = (s16[192,512]{1,0:T(8,128)(2,1)S(1)}, s16[192,512]{1,0:T(8,128)(2,1)S(1)}, u32[]{:S(2)}, u32[]{:S(2)}) collective-permute-start(s16[192,512]{1,0:T(8,128)(2,1)S(1)} %get-tuple-element.38), channel_id=1, source_target_pairs={{0,16},{16,32},{32,48},{48,64},{64,80},{80,96},{96,112},{112,128},... | collective-permute-start | bytes 589832 | tf_op jit(solution)/shard_map/ppermute | solution.py:427
  100.2 7.7 %collective-permute-start.5 = (s16[192,512]{1,0:T(8,128)(2,1)S(1)}, s16[192,512]{1,0:T(8,128)(2,1)S(1)}, u32[]{:S(2)}, u32[]{:S(2)}) collective-permute-start(s16[192,512]{1,0:T(8,128)(2,1)S(1)} %get-tuple-element.45), channel_id=1, source_target_pairs={{16,32},{32,16},{48,64},{64,48},{80,96},{96,80},{112,128},{128,112... | collective-permute-start | bytes 589832 | tf_op jit(solution)/shard_map/ppermute | solution.py:423
  104.6 3.3 %collective-permute-start.6 = (s16[192,512]{1,0:T(8,128)(2,1)S(1)}, s16[192,512]{1,0:T(8,128)(2,1)S(1)}, u32[]{:S(2)}, u32[]{:S(2)}) collective-permute-start(s16[192,512]{1,0:T(8,128)(2,1)S(1)} %get-tuple-element.46), channel_id=1, source_target_pairs={{0,16},{16,0},{32,48},{48,32},{64,80},{80,64},{96,112},{112,96},{1... | collective-permute-start | bytes 589832 | tf_op jit(solution)/shard_map/ppermute | solution.py:424
  109.2 7.2 %collective-permute-start.7 = (s16[192,512]{1,0:T(8,128)(2,1)S(1)}, s16[192,512]{1,0:T(8,128)(2,1)S(1)}, u32[]{:S(2)}, u32[]{:S(2)}) collective-permute-start(s16[192,512]{1,0:T(8,128)(2,1)S(1)} %get-tuple-element.48), channel_id=1, source_target_pairs={{16,32},{32,16},{48,64},{64,48},{80,96},{96,80},{112,128},{128,112... | collective-permute-start | bytes 589832 | tf_op jit(solution)/shard_map/ppermute | solution.py:423
  112.8 3.6 %collective-permute-start.8 = (s16[192,512]{1,0:T(8,128)(2,1)S(1)}, s16[192,512]{1,0:T(8,128)(2,1)S(1)}, u32[]{:S(2)}, u32[]{:S(2)}) collective-permute-start(s16[192,512]{1,0:T(8,128)(2,1)S(1)} %get-tuple-element.49), channel_id=1, source_target_pairs={{0,16},{16,0},{32,48},{48,32},{64,80},{80,64},{96,112},{112,96},{1... | collective-permute-start | bytes 589832 | tf_op jit(solution)/shard_map/ppermute | solution.py:424

commit v8 on v7

--- a/solution.py
+++ b/solution.py
@@ -19,6 +19,7 @@
 TAIL = tuple(t for t in LOWER if t[1] >= SIDE // 2)
 NT = len(UPPER)
 CODE = 32000.0
+SLOT = 192
 HALF = 32768
 f32, bf16, i16, i32 = jnp.float32, jnp.bfloat16, jnp.int16, jnp.int32
 
@@ -320,8 +321,10 @@
 def last_vector(part_ref, across_in, inside_in, back_h, back_l, c_ref, early_ref, out_ref, moments_ref):
     w = gather(part_ref, *arrived(across_in, inside_in), back_h, back_l)
     out_ref[...] = w
-    row = lax.broadcasted_iota(i32, early_ref.shape, 0)
-    moments = jnp.where(row == 5, turn(along(c_ref[...], w)), early_ref[...])
+    early = early_ref[...]
+    rows = [early[k : k + 1, :SLOT] for k in range(5)] + [turn(along(c_ref[...], w))[:, :SLOT]]
+    fill = moments_ref.shape[2] - 6 * SLOT
+    moments = jnp.concatenate(rows + [jnp.zeros((1, fill), f32)], axis=1)
     for k in range(moments_ref.shape[0]):
         moments_ref[k] = moments
 
@@ -330,7 +333,8 @@
     total = moments_ref[0]
     for k in range(1, moments_ref.shape[0]):
         total = total + moments_ref[k]
-    moment = [total[k : k + 1] / total[:1] for k in range(6)]
+    first = total[:, :256]
+    moment = [total[:, k * SLOT : k * SLOT + 256] / first for k in range(6)]
 
     def inner(x, y, power):
         return sum(
@@ -357,7 +361,7 @@
             ]
             norm_now = norm_next
     rows = effects + residual
-    table = jnp.concatenate(rows + [jnp.zeros((TILE - len(rows), total.shape[1]), f32)], axis=0).T
+    table = jnp.concatenate(rows + [jnp.zeros((TILE - len(rows), 256), f32)], axis=0).T
     table = table[: a_ref.shape[0]]
     col = [table[:, k : k + 1] for k in range(len(rows))]
     a, b, c, d = a_ref[...], b_ref[...], c_ref[...], d_ref[...]
@@ -429,7 +433,7 @@
     two, part, out, inn = step(next_gather, *rest)
     early = call(early_moments, shape(8, 256), z, one, two)
     three, moments = call(
-        last_vector, (vector, shape(blocks, 8, 256)), part, out, inn, back_h, back_l, two, early
+        last_vector, (vector, shape(blocks, 1, 1280)), part, out, inn, back_h, back_l, two, early
     )
     moments = lax.all_to_all(moments, "genome", 0, 0)
     effects, residual = call(combine, (jax.ShapeDtypeStruct(z.shape, f32),) * 2, moments, z, one, two, three)

time: 144 us -> 142 us (0.986)
  blocking collectives: 51.8 us -> 49.7 us
    all_to_all x1, blocking collectives: 25 us -> 22.8 us  [shards(): moments = lax.all_to_all(moments, 'genome', 0, 0)]
where the time goes in v8:
time: 142 us; the launch traced here: 141 us
  starting transfers between devices  54 us (38%)
  blocking collectives  49.7 us (35%)
  waiting for transfers between devices  18.1 us (13%)
  Pallas kernels  14.5 us (10%)
  other arithmetic  3.41 us (2%)
    all_to_all x1, blocking collectives, shards(): codes = lax.all_to_all(codes, 'cols', 0, 0)  26.8 us
    all_to_all x1, blocking collectives, shards(): moments = lax.all_to_all(moments, 'genome', 0, 0)  22.8 us
    pallas_call x15, Pallas kernels, call(): pl.pallas_call(kernel, out_shape=outs, in_specs=[spec] * len(args), out_s...  14.5 us
    all_to_all x1, starting transfers between devices, shards(): nxt = lax.all_to_all(nxt, 'cols', 0, 0)  11.7 us
    ppermute x1, starting transfers between devices, shards(): next_first = lax.ppermute(first, 'genome', to_left)  8.75 us
    ppermute x2, starting transfers between devices, step(): out = lax.ppermute(out, 'genome', across)  7.93 us
    ppermute x1, starting transfers between devices, shards(): far = lax.ppermute(far, 'cols', [(k, (k + near) % peers) for k in cols])  7.18 us
    ppermute x1, waiting for transfers between devices, shards(): next_second = lax.ppermute(second, 'genome', to_left)  7.17 us
  transfers between devices with their start and end apart: 11, of which 6 were waited for; matrix products, arithmetic and copies ran while one was open for 1% of the time, Pallas kernels for 6%

profile of v8, /device:TPU:1, one launch (start us, length us, event | category | flops | bytes accessed | tf_op | source)
XLA Modules:
  0.0 141.3 jit_solution(17124510134228884776)
XLA Ops:
  0.6 1.7 %slice_convert_fusion.1.first_ref = bf16[1920,256]{1,0:T(8,128)(2,1)S(1)} fusion(s32[1920,512]{1,0:T(8,128)} %param.2), kind=kLoop, calls=%fused_computation.1 | loop fusion | flops 491520 | bytes 2949120 | tf_op jit(solution)/shard_map/convert.1
  2.3 8.7 %collective-permute-start.2 = (bf16[1920,256]{1,0:T(8,128)(2,1)S(1)}, bf16[1920,256]{1,0:T(8,128)(2,1)}, u32[]{:S(2)}, u32[]{:S(2)}) collective-permute-start(bf16[1920,256]{1,0:T(8,128)(2,1)S(1)} %slice_convert_fusion.1.first_ref), channel_id=1, source_target_pairs={{16,0},{32,16},{48,32},{64,48},{80,64},{96,80},{112,96},{128,112},... | collective-permute-start | bytes 2949128 | tf_op jit(solution)/shard_map/ppermute | solution.py:388
  11.1 1.7 %slice_convert_fusion.second_ref = bf16[1920,256]{1,0:T(8,128)(2,1)S(1)} fusion(s32[1920,512]{1,0:T(8,128)} %param.2), kind=kLoop, calls=%fused_computation | loop fusion | flops 491520 | bytes 2949120 | tf_op jit(solution)/shard_map/convert
  12.8 1.9 %collective-permute-start.1 = (bf16[1920,256]{1,0:T(8,128)(2,1)S(1)}, bf16[1920,256]{1,0:T(8,128)(2,1)}, u32[]{:S(2)}, u32[]{:S(2)}) collective-permute-start(bf16[1920,256]{1,0:T(8,128)(2,1)S(1)} %slice_convert_fusion.second_ref), channel_id=1, source_target_pairs={{16,0},{32,16},{48,32},{64,48},{80,64},{96,80},{112,96},{128,112},... | collective-permute-start | bytes 2949128 | tf_op jit(solution)/shard_map/ppermute | solution.py:390
  14.7 1.3 shard_map.41
  16.0 0.0 copy-start.1
  16.0 0.8 copy-done.1
  16.8 0.0 copy-start
  16.8 4.2 %all-to-all-start = ((s16[8,192,128]{2,1,0:T(8,128)(2,1)}), s16[8,192,128]{2,1,0:T(8,128)(2,1)}, u32[]{:S(2)}, u32[]{:S(2)}) async-start(s16[8,192,128]{2,1,0:T(8,128)(2,1)} %copy-done.1), calls=%async_computation | async-start | bytes 786432 | tf_op jit(solution)/shard_map/all_to_all | solution.py:397
  21.0 0.0 collective-permute-done.2.next_ref
  21.0 1.9 %shard_map.43.head_ref = s16[16,64,128]{2,1,0:T(8,128)(2,1)S(1)} custom-call(bf16[1920,256]{1,0:T(8,128)(2,1)S(1)} %slice_convert_fusion.1.first_ref, bf16[256,1920]{1,0:T(8,128)(2,1)S(1)} %get-tuple-element.32.turned_ref, bf16[1920,256]{1,0:T(8,128)(2,1)} %collective-permute-done.2.next_ref), custom_call_target="tpu_custom_call" | custom-call | tf_op jit(solution)/shard_map/pallas_call | solution.py:38
  23.0 7.2 %collective-permute-done.1.next_ref = bf16[1920,256]{1,0:T(8,128)(2,1)} collective-permute-done((bf16[1920,256]{1,0:T(8,128)(2,1)S(1)}, bf16[1920,256]{1,0:T(8,128)(2,1)}, u32[]{:S(2)}, u32[]{:S(2)}) %collective-permute-start.1) | collective-permute-done | bytes 983072 | tf_op jit(solution)/shard_map/ppermute | solution.py:390
  30.1 2.4 %shard_map.44 = s16[16,96,128]{2,1,0:T(8,128)(2,1)} custom-call(bf16[256,1920]{1,0:T(8,128)(2,1)S(1)} %get-tuple-element.32.turned_ref, bf16[1920,256]{1,0:T(8,128)(2,1)} %collective-permute-done.1.next_ref, s16[16,64,128]{2,1,0:T(8,128)(2,1)S(1)} %shard_map.43.head_ref), custom_call_target="tpu_custom_call" | custom-call | tf_op jit(solution)/shard_map/pallas_call | solution.py:38
  32.6 2.8 %all-to-all-done.came_ref = s16[8,192,128]{2,1,0:T(8,128)(2,1)} async-done(((s16[8,192,128]{2,1,0:T(8,128)(2,1)}), s16[8,192,128]{2,1,0:T(8,128)(2,1)}, u32[]{:S(2)}, u32[]{:S(2)}) %all-to-all-start) | async-done | bytes 393248 | tf_op jit(solution)/shard_map/all_to_all | solution.py:397
  35.3 11.7 %all-to-all-start.1 = ((s16[16,96,128]{2,1,0:T(8,128)(2,1)}), s16[16,96,128]{2,1,0:T(8,128)(2,1)S(1)}, u32[]{:S(2)}, u32[]{:S(2)}) async-start(s16[16,96,128]{2,1,0:T(8,128)(2,1)} %shard_map.44), calls=%async_computation.1 | async-start | bytes 786432 | tf_op jit(solution)/shard_map/all_to_all | solution.py:406
  47.0 0.0 copy-done
  47.1 0.2 shard_map.46
  47.2 1.9 %collective-permute-start.3 = (s16[192,512]{1,0:T(8,128)(2,1)S(1)}, s16[192,512]{1,0:T(8,128)(2,1)S(1)}, u32[]{:S(2)}, u32[]{:S(2)}) collective-permute-start(s16[192,512]{1,0:T(8,128)(2,1)S(1)} %shard_map.46), channel_id=1, source_target_pairs={{16,0},{32,16},{48,32},{64,48},{80,64},{96,80},{112,96},{128,112},... | collective-permute-start | bytes 589832 | tf_op jit(solution)/shard_map/ppermute | solution.py:407
  49.1 1.1 shard_map.42
  50.2 7.2 %collective-permute-start = (s16[96,128]{1,0:T(8,128)(2,1)S(1)}, s16[96,128]{1,0:T(8,128)(2,1)S(1)}, u32[]{:S(2)}, u32[]{:S(2)}) collective-permute-start(s16[96,128]{1,0:T(8,128)(2,1)S(1)} %get-tuple-element.31), channel_id=1, source_target_pairs={{0,8},{1,9},{2,10},{3,11},{4,12},{5,13},{6,14},{7,15},{8,0},{9,1},... | collective-permute-start | bytes 73736 | tf_op jit(solution)/shard_map/ppermute | solution.py:404
  57.4 4.2 %collective-permute-done.far_ref = s16[96,128]{1,0:T(8,128)(2,1)S(1)} collective-permute-done((s16[96,128]{1,0:T(8,128)(2,1)S(1)}, s16[96,128]{1,0:T(8,128)(2,1)S(1)}, u32[]{:S(2)}, u32[]{:S(2)}) %collective-permute-start) | collective-permute-done | bytes 24608 | tf_op jit(solution)/shard_map/ppermute | solution.py:404
  61.6 0.0 all-to-all-done.1.next_ref
  61.6 0.2 shard_map.45
  61.8 0.0 collective-permute-done.3.next_ref
  61.8 26.8 %all_to_all.20.codes_ref = s16[16,128,128]{2,1,0:T(8,128)(2,1)S(1)} all-to-all(s16[16,128,128]{2,1,0:T(8,128)(2,1)S(1)} %get-tuple-element.34), channel_id=1, replica_groups=mesh['genome'=32,'cols'=16] {'cols'}, dimensions={0} | all-to-all | bytes 1048576 | tf_op jit(solution)/shard_map/all_to_all | solution.py:416
  88.6 1.2 shard_map.47
  89.9 6.5 %collective-permute-start.4 = (s16[192,512]{1,0:T(8,128)(2,1)S(1)}, s16[192,512]{1,0:T(8,128)(2,1)S(1)}, u32[]{:S(2)}, u32[]{:S(2)}) collective-permute-start(s16[192,512]{1,0:T(8,128)(2,1)S(1)} %get-tuple-element.38), channel_id=1, source_target_pairs={{0,16},{16,32},{32,48},{48,64},{64,80},{80,96},{96,112},{112,128},... | collective-permute-start | bytes 589832 | tf_op jit(solution)/shard_map/ppermute | solution.py:431
  96.4 0.5 shard_map.48.part_ref
  96.9 2.1 %collective-permute-done.4.came_ref = s16[192,512]{1,0:T(8,128)(2,1)S(1)} collective-permute-done((s16[192,512]{1,0:T(8,128)(2,1)S(1)}, s16[192,512]{1,0:T(8,128)(2,1)S(1)}, u32[]{:S(2)}, u32[]{:S(2)}) %collective-permute-start.4) | collective-permute-done | bytes 196640 | tf_op jit(solution)/shard_map/ppermute | solution.py:431
  99.0 1.2 shard_map.49
  100.2 4.3 %collective-permute-start.5 = (s16[192,512]{1,0:T(8,128)(2,1)S(1)}, s16[192,512]{1,0:T(8,128)(2,1)S(1)}, u32[]{:S(2)}, u32[]{:S(2)}) collective-permute-start(s16[192,512]{1,0:T(8,128)(2,1)S(1)} %get-tuple-element.45), channel_id=1, source_target_pairs={{16,32},{32,16},{48,64},{64,48},{80,96},{96,80},{112,128},{128,112... | collective-permute-start | bytes 589832 | tf_op jit(solution)/shard_map/ppermute | solution.py:427
  104.6 1.9 %collective-permute-start.6 = (s16[192,512]{1,0:T(8,128)(2,1)S(1)}, s16[192,512]{1,0:T(8,128)(2,1)S(1)}, u32[]{:S(2)}, u32[]{:S(2)}) collective-permute-start(s16[192,512]{1,0:T(8,128)(2,1)S(1)} %get-tuple-element.46), channel_id=1, source_target_pairs={{0,16},{16,0},{32,48},{48,32},{64,80},{80,64},{96,112},{112,96},{1... | collective-permute-start | bytes 589832 | tf_op jit(solution)/shard_map/ppermute | solution.py:428
  106.5 0.5 shard_map.50.part_ref
  107.0 0.9 collective-permute-done.5.across_in
  107.9 0.0 collective-permute-done.6.inside_in
  107.9 1.2 shard_map.51
  109.2 3.6 %collective-permute-start.7 = (s16[192,512]{1,0:T(8,128)(2,1)S(1)}, s16[192,512]{1,0:T(8,128)(2,1)S(1)}, u32[]{:S(2)}, u32[]{:S(2)}) collective-permute-start(s16[192,512]{1,0:T(8,128)(2,1)S(1)} %get-tuple-element.48), channel_id=1, source_target_pairs={{16,32},{32,16},{48,64},{64,48},{80,96},{96,80},{112,128},{128,112... | collective-permute-start | bytes 589832 | tf_op jit(solution)/shard_map/ppermute | solution.py:427
  112.8 1.9 %collective-permute-start.8 = (s16[192,512]{1,0:T(8,128)(2,1)S(1)}, s16[192,512]{1,0:T(8,128)(2,1)S(1)}, u32[]{:S(2)}, u32[]{:S(2)}) collective-permute-start(s16[192,512]{1,0:T(8,128)(2,1)S(1)} %get-tuple-element.49), channel_id=1, source_target_pairs={{0,16},{16,0},{32,48},{48,32},{64,80},{80,64},{96,112},{112,96},{1... | collective-permute-start | bytes 589832 | tf_op jit(solution)/shard_map/ppermute | solution.py:428
  114.7 0.2 shard_map.53.early_ref
  114.9 0.5 shard_map.52.part_ref
  115.4 0.9 collective-permute-done.7.across_in
  116.3 0.0 collective-permute-done.8.inside_in
  116.3 0.7 shard_map.54
  117.1 22.8 %all_to_all.21.moments_ref = f32[32,1,1280]{2,1,0:T(1,128)S(1)} all-to-all(f32[32,1,1280]{2,1,0:T(1,128)S(1)} %get-tuple-element.50), channel_id=1, replica_groups=mesh['genome'=32,'cols'=16] {'genome'}, dimensions={0} | all-to-all | bytes 327680 | tf_op jit(solution)/shard_map/all_to_all | solution.py:438
  139.9 1.4 %shard_map.55 = (f32[184,512]{1,0:T(8,128)}, f32[184,512]{1,0:T(8,128)}) custom-call(f32[32,1,1280]{2,1,0:T(1,128)S(1)} %all_to_all.21.moments_ref, f32[184,512]{1,0:T(8,128)S(1)} %bitcast.7, f32[184,512]{1,0:T(8,128)S(1)} %get-tuple-element.44.v_ref.b_ref, f32[184,512]{1,0:T(8,128)S(1)} %get-tuple-element.47.v_ref.c_ref, f32[184,512]{1,0:T(8,128)S(1)} %get-tuple-element.51.d_ref), custom_call_target="tpu_custom_call" | custom-call | tf_op jit(solution)/shard_map/pallas_call | solution.py:38
Async XLA Ops:
  2.3 18.7 %collective-permute-start.2 = (bf16[1920,256]{1,0:T(8,128)(2,1)S(1)}, bf16[1920,256]{1,0:T(8,128)(2,1)}, u32[]{:S(2)}, u32[]{:S(2)}) collective-permute-start(bf16[1920,256]{1,0:T(8,128)(2,1)S(1)} %slice_convert_fusion.1.first_ref), channel_id=1, source_target_pairs={{16,0},{32,16},{48,32},{64,48},{80,64},{96,80},{112,96},{128,112},... | collective-permute-start | bytes 2949128 | tf_op jit(solution)/shard_map/ppermute | solution.py:388
  12.8 17.3 %collective-permute-start.1 = (bf16[1920,256]{1,0:T(8,128)(2,1)S(1)}, bf16[1920,256]{1,0:T(8,128)(2,1)}, u32[]{:S(2)}, u32[]{:S(2)}) collective-permute-start(bf16[1920,256]{1,0:T(8,128)(2,1)S(1)} %slice_convert_fusion.second_ref), channel_id=1, source_target_pairs={{16,0},{32,16},{48,32},{64,48},{80,64},{96,80},{112,96},{128,112},... | collective-permute-start | bytes 2949128 | tf_op jit(solution)/shard_map/ppermute | solution.py:390
  16.0 0.8 copy-start.1
  16.8 30.3 %copy-start = (f32[512,184]{0,1:T(8,128)S(1)}, f32[512,184]{0,1:T(8,128)}, u32[]{:S(2)}) copy-start(f32[512,184]{0,1:T(8,128)} %param.3) | copy-start | bytes 1130500
  16.8 18.6 %all-to-all-start = ((s16[8,192,128]{2,1,0:T(8,128)(2,1)}), s16[8,192,128]{2,1,0:T(8,128)(2,1)}, u32[]{:S(2)}, u32[]{:S(2)}) async-start(s16[8,192,128]{2,1,0:T(8,128)(2,1)} %copy-done.1), calls=%async_computation | async-start | bytes 786432 | tf_op jit(solution)/shard_map/all_to_all | solution.py:397
  35.3 26.3 %all-to-all-start.1 = ((s16[16,96,128]{2,1,0:T(8,128)(2,1)}), s16[16,96,128]{2,1,0:T(8,128)(2,1)S(1)}, u32[]{:S(2)}, u32[]{:S(2)}) async-start(s16[16,96,128]{2,1,0:T(8,128)(2,1)} %shard_map.44), calls=%async_computation.1 | async-start | bytes 786432 | tf_op jit(solution)/shard_map/all_to_all | solution.py:406
  47.2 14.6 %collective-permute-start.3 = (s16[192,512]{1,0:T(8,128)(2,1)S(1)}, s16[192,512]{1,0:T(8,128)(2,1)S(1)}, u32[]{:S(2)}, u32[]{:S(2)}) collective-permute-start(s16[192,512]{1,0:T(8,128)(2,1)S(1)} %shard_map.46), channel_id=1, source_target_pairs={{16,0},{32,16},{48,32},{64,48},{80,64},{96,80},{112,96},{128,112},... | collective-permute-start | bytes 589832 | tf_op jit(solution)/shard_map/ppermute | solution.py:407
  50.2 11.4 %collective-permute-start = (s16[96,128]{1,0:T(8,128)(2,1)S(1)}, s16[96,128]{1,0:T(8,128)(2,1)S(1)}, u32[]{:S(2)}, u32[]{:S(2)}) collective-permute-start(s16[96,128]{1,0:T(8,128)(2,1)S(1)} %get-tuple-element.31), channel_id=1, source_target_pairs={{0,8},{1,9},{2,10},{3,11},{4,12},{5,13},{6,14},{7,15},{8,0},{9,1},... | collective-permute-start | bytes 73736 | tf_op jit(solution)/shard_map/ppermute | solution.py:404
  89.9 9.1 %collective-permute-start.4 = (s16[192,512]{1,0:T(8,128)(2,1)S(1)}, s16[192,512]{1,0:T(8,128)(2,1)S(1)}, u32[]{:S(2)}, u32[]{:S(2)}) collective-permute-start(s16[192,512]{1,0:T(8,128)(2,1)S(1)} %get-tuple-element.38), channel_id=1, source_target_pairs={{0,16},{16,32},{32,48},{48,64},{64,80},{80,96},{96,112},{112,128},... | collective-permute-start | bytes 589832 | tf_op jit(solution)/shard_map/ppermute | solution.py:431
  100.2 7.7 %collective-permute-start.5 = (s16[192,512]{1,0:T(8,128)(2,1)S(1)}, s16[192,512]{1,0:T(8,128)(2,1)S(1)}, u32[]{:S(2)}, u32[]{:S(2)}) collective-permute-start(s16[192,512]{1,0:T(8,128)(2,1)S(1)} %get-tuple-element.45), channel_id=1, source_target_pairs={{16,32},{32,16},{48,64},{64,48},{80,96},{96,80},{112,128},{128,112... | collective-permute-start | bytes 589832 | tf_op jit(solution)/shard_map/ppermute | solution.py:427
  104.6 3.3 %collective-permute-start.6 = (s16[192,512]{1,0:T(8,128)(2,1)S(1)}, s16[192,512]{1,0:T(8,128)(2,1)S(1)}, u32[]{:S(2)}, u32[]{:S(2)}) collective-permute-start(s16[192,512]{1,0:T(8,128)(2,1)S(1)} %get-tuple-element.46), channel_id=1, source_target_pairs={{0,16},{16,0},{32,48},{48,32},{64,80},{80,64},{96,112},{112,96},{1... | collective-permute-start | bytes 589832 | tf_op jit(solution)/shard_map/ppermute | solution.py:428
  109.2 7.2 %collective-permute-start.7 = (s16[192,512]{1,0:T(8,128)(2,1)S(1)}, s16[192,512]{1,0:T(8,128)(2,1)S(1)}, u32[]{:S(2)}, u32[]{:S(2)}) collective-permute-start(s16[192,512]{1,0:T(8,128)(2,1)S(1)} %get-tuple-element.48), channel_id=1, source_target_pairs={{16,32},{32,16},{48,64},{64,48},{80,96},{96,80},{112,128},{128,112... | collective-permute-start | bytes 589832 | tf_op jit(solution)/shard_map/ppermute | solution.py:427
  112.8 3.6 %collective-permute-start.8 = (s16[192,512]{1,0:T(8,128)(2,1)S(1)}, s16[192,512]{1,0:T(8,128)(2,1)S(1)}, u32[]{:S(2)}, u32[]{:S(2)}) collective-permute-start(s16[192,512]{1,0:T(8,128)(2,1)S(1)} %get-tuple-element.49), channel_id=1, source_target_pairs={{0,16},{16,0},{32,48},{48,32},{64,80},{80,64},{96,112},{112,96},{1... | collective-permute-start | bytes 589832 | tf_op jit(solution)/shard_map/ppermute | solution.py:428

commit v9 on v8

--- a/solution.py
+++ b/solution.py
@@ -54,8 +54,10 @@
 
 def pack_tiles(tiles, block, peers, put):
     rows = TILE // peers
-    pieces = [tile.reshape(peers, rows, TILE) for tile in tiles] + sums(block, peers, rows)
-    for u in range(len(pieces) // 2):
+    pieces = [tile.reshape(peers, rows, TILE) for tile in tiles]
+    if block is not None:
+        pieces += sums(block, peers, rows)
+    for u in range((len(pieces) + 1) // 2):
         pair = jnp.concatenate(pieces[2 * u : 2 * u + 2], axis=1)
         put(2 * rows * u, pair.astype(i32).astype(i16))
 
@@ -118,7 +120,12 @@
         out_ref[:, done + at : done + at + value.shape[1], :] = value
 
     half = SIDE // 2
-    pack_tiles([tile_of(gram, p - half, q - half) for p, q in TAIL], block, out_ref.shape[0], put)
+    peers = out_ref.shape[0]
+    rows = TILE // peers
+    both = sums(block, peers, rows)[0][:, :SIDE]
+    both = jnp.concatenate([jnp.zeros_like(both), both], axis=1).astype(i32)
+    put(-rows, (both + head_ref[:, done - rows : done, :].astype(i32)).astype(i16))
+    pack_tiles([tile_of(gram, p - half, q - half) for p, q in TAIL], None, peers, put)
 
 
 def fold(came_ref, keep_ref, send_ref):
@@ -151,9 +158,10 @@
         return mean, variance, 1.0 / jnp.sqrt(jnp.maximum(variance, FLOOR))
 
     mean, variance, scale = stats(own[NT * rows :])
-    slot = {tile: t for t, tile in enumerate(HEAD + ("head",) + TAIL + ("tail",))}
+    slot = {tile: t for t, tile in enumerate(HEAD + ("sums",) + TAIL)}
     half = SIDE // 2
-    parts = [nxt[slot[name] * rows : slot[name] * rows + SIDE] for name in ("head", "tail")]
+    at = slot["sums"] * rows
+    parts = nxt[at : at + SIDE], nxt[at + SIDE : at + 2 * SIDE]
     next_mean, _, next_scale = stats(jnp.concatenate([v[k : k + half] for k in (0, half) for v in parts], axis=0))
     diagonal_ref[...] = jnp.concatenate([variance * scale * scale, jnp.zeros((8 - SIDE, TILE), f32)], axis=0)
     lane = lax.broadcasted_iota(i32, (rows, TILE), 1)
@@ -402,7 +410,7 @@
     code = shape(z.shape[0] // 16 * 16 + 16, z.shape[1], dtype=i16)
     z_code = call(start_code, code, z)
     far = lax.ppermute(far, "cols", [(k, (k + near) % peers) for k in cols])
-    nxt = call(tail_products, shape(peers, depth, TILE, dtype=i16), turned, next_second, head)
+    nxt = call(tail_products, shape(peers, (NT + 1) * rows, TILE, dtype=i16), turned, next_second, head)
     nxt = lax.all_to_all(nxt, "cols", 0, 0)
     z_next = lax.ppermute(z_code, "genome", to_left)
     codes, diagonal_row = call(

time: 142 us -> 142 us (level)
  no operation moved by 1% of the time
where the time goes in v9:
time: 142 us; the launch traced here: 141 us
  starting transfers between devices  53 us (37%)
  blocking collectives  50 us (35%)
  waiting for transfers between devices  18.8 us (13%)
  Pallas kernels  14.5 us (10%)
  other arithmetic  3.41 us (2%)
    all_to_all x1, blocking collectives, shards(): codes = lax.all_to_all(codes, 'cols', 0, 0)  27.1 us
    all_to_all x1, blocking collectives, shards(): moments = lax.all_to_all(moments, 'genome', 0, 0)  22.8 us
    pallas_call x15, Pallas kernels, call(): pl.pallas_call(kernel, out_shape=outs, in_specs=[spec] * len(args), out_s...  14.5 us
    all_to_all x1, starting transfers between devices, shards(): nxt = lax.all_to_all(nxt, 'cols', 0, 0)  11.7 us
    ppermute x1, starting transfers between devices, shards(): next_first = lax.ppermute(first, 'genome', to_left)  8.75 us
    ppermute x2, starting transfers between devices, step(): out = lax.ppermute(out, 'genome', across)  7.92 us
    ppermute x1, starting transfers between devices, shards(): far = lax.ppermute(far, 'cols', [(k, (k + near) % peers) for k in cols])  7.18 us
    ppermute x1, waiting for transfers between devices, shards(): next_second = lax.ppermute(second, 'genome', to_left)  7.17 us
  transfers between devices with their start and end apart: 11, of which 6 were waited for; matrix products, arithmetic and copies ran while one was open for 1% of the time, Pallas kernels for 6%

profile of v9, /device:TPU:1, one launch (start us, length us, event | category | flops | bytes accessed | tf_op | source)
XLA Modules:
  0.0 141.3 jit_solution(12200556452359163461)
XLA Ops:
  0.6 1.7 %slice_convert_fusion.1.first_ref = bf16[1920,256]{1,0:T(8,128)(2,1)S(1)} fusion(s32[1920,512]{1,0:T(8,128)} %param.2), kind=kLoop, calls=%fused_computation.1 | loop fusion | flops 491520 | bytes 2949120 | tf_op jit(solution)/shard_map/convert.1
  2.3 8.7 %collective-permute-start.2 = (bf16[1920,256]{1,0:T(8,128)(2,1)S(1)}, bf16[1920,256]{1,0:T(8,128)(2,1)}, u32[]{:S(2)}, u32[]{:S(2)}) collective-permute-start(bf16[1920,256]{1,0:T(8,128)(2,1)S(1)} %slice_convert_fusion.1.first_ref), channel_id=1, source_target_pairs={{16,0},{32,16},{48,32},{64,48},{80,64},{96,80},{112,96},{128,112},... | collective-permute-start | bytes 2949128 | tf_op jit(solution)/shard_map/ppermute | solution.py:396
  11.1 1.7 %slice_convert_fusion.second_ref = bf16[1920,256]{1,0:T(8,128)(2,1)S(1)} fusion(s32[1920,512]{1,0:T(8,128)} %param.2), kind=kLoop, calls=%fused_computation | loop fusion | flops 491520 | bytes 2949120 | tf_op jit(solution)/shard_map/convert
  12.8 1.9 %collective-permute-start.1 = (bf16[1920,256]{1,0:T(8,128)(2,1)S(1)}, bf16[1920,256]{1,0:T(8,128)(2,1)}, u32[]{:S(2)}, u32[]{:S(2)}) collective-permute-start(bf16[1920,256]{1,0:T(8,128)(2,1)S(1)} %slice_convert_fusion.second_ref), channel_id=1, source_target_pairs={{16,0},{32,16},{48,32},{64,48},{80,64},{96,80},{112,96},{128,112},... | collective-permute-start | bytes 2949128 | tf_op jit(solution)/shard_map/ppermute | solution.py:398
  14.7 1.3 shard_map.41
  16.0 0.0 copy-start.1
  16.0 0.8 copy-done.1
  16.8 0.0 copy-start
  16.8 4.2 %all-to-all-start = ((s16[8,192,128]{2,1,0:T(8,128)(2,1)}), s16[8,192,128]{2,1,0:T(8,128)(2,1)}, u32[]{:S(2)}, u32[]{:S(2)}) async-start(s16[8,192,128]{2,1,0:T(8,128)(2,1)} %copy-done.1), calls=%async_computation | async-start | bytes 786432 | tf_op jit(solution)/shard_map/all_to_all | solution.py:405
  21.0 0.0 collective-permute-done.2.next_ref
  21.0 1.9 %shard_map.43.head_ref = s16[16,64,128]{2,1,0:T(8,128)(2,1)S(1)} custom-call(bf16[1920,256]{1,0:T(8,128)(2,1)S(1)} %slice_convert_fusion.1.first_ref, bf16[256,1920]{1,0:T(8,128)(2,1)S(1)} %get-tuple-element.32.turned_ref, bf16[1920,256]{1,0:T(8,128)(2,1)} %collective-permute-done.2.next_ref), custom_call_target="tpu_custom_call" | custom-call | tf_op jit(solution)/shard_map/pallas_call | solution.py:38
  23.0 7.2 %collective-permute-done.1.next_ref = bf16[1920,256]{1,0:T(8,128)(2,1)} collective-permute-done((bf16[1920,256]{1,0:T(8,128)(2,1)S(1)}, bf16[1920,256]{1,0:T(8,128)(2,1)}, u32[]{:S(2)}, u32[]{:S(2)}) %collective-permute-start.1) | collective-permute-done | bytes 983072 | tf_op jit(solution)/shard_map/ppermute | solution.py:398
  30.1 2.4 %shard_map.44 = s16[16,88,128]{2,1,0:T(8,128)(2,1)} custom-call(bf16[256,1920]{1,0:T(8,128)(2,1)S(1)} %get-tuple-element.32.turned_ref, bf16[1920,256]{1,0:T(8,128)(2,1)} %collective-permute-done.1.next_ref, s16[16,64,128]{2,1,0:T(8,128)(2,1)S(1)} %shard_map.43.head_ref), custom_call_target="tpu_custom_call" | custom-call | tf_op jit(solution)/shard_map/pallas_call | solution.py:38
  32.5 2.8 %all-to-all-done.came_ref = s16[8,192,128]{2,1,0:T(8,128)(2,1)} async-done(((s16[8,192,128]{2,1,0:T(8,128)(2,1)}), s16[8,192,128]{2,1,0:T(8,128)(2,1)}, u32[]{:S(2)}, u32[]{:S(2)}) %all-to-all-start) | async-done | bytes 393248 | tf_op jit(solution)/shard_map/all_to_all | solution.py:405
  35.3 11.7 %all-to-all-start.1 = ((s16[16,88,128]{2,1,0:T(8,128)(2,1)}), s16[16,88,128]{2,1,0:T(8,128)(2,1)S(1)}, u32[]{:S(2)}, u32[]{:S(2)}) async-start(s16[16,88,128]{2,1,0:T(8,128)(2,1)} %shard_map.44), calls=%async_computation.1 | async-start | bytes 720896 | tf_op jit(solution)/shard_map/all_to_all | solution.py:414
  47.0 0.0 copy-done
  47.0 0.2 shard_map.46
  47.2 1.9 %collective-permute-start.3 = (s16[192,512]{1,0:T(8,128)(2,1)S(1)}, s16[192,512]{1,0:T(8,128)(2,1)S(1)}, u32[]{:S(2)}, u32[]{:S(2)}) collective-permute-start(s16[192,512]{1,0:T(8,128)(2,1)S(1)} %shard_map.46), channel_id=1, source_target_pairs={{16,0},{32,16},{48,32},{64,48},{80,64},{96,80},{112,96},{128,112},... | collective-permute-start | bytes 589832 | tf_op jit(solution)/shard_map/ppermute | solution.py:415
  49.1 1.1 shard_map.42
  50.2 7.2 %collective-permute-start = (s16[96,128]{1,0:T(8,128)(2,1)S(1)}, s16[96,128]{1,0:T(8,128)(2,1)S(1)}, u32[]{:S(2)}, u32[]{:S(2)}) collective-permute-start(s16[96,128]{1,0:T(8,128)(2,1)S(1)} %get-tuple-element.31), channel_id=1, source_target_pairs={{0,8},{1,9},{2,10},{3,11},{4,12},{5,13},{6,14},{7,15},{8,0},{9,1},... | collective-permute-start | bytes 73736 | tf_op jit(solution)/shard_map/ppermute | solution.py:412
  57.3 3.5 %collective-permute-done.far_ref = s16[96,128]{1,0:T(8,128)(2,1)S(1)} collective-permute-done((s16[96,128]{1,0:T(8,128)(2,1)S(1)}, s16[96,128]{1,0:T(8,128)(2,1)S(1)}, u32[]{:S(2)}, u32[]{:S(2)}) %collective-permute-start) | collective-permute-done | bytes 24608 | tf_op jit(solution)/shard_map/ppermute | solution.py:412
  60.9 0.0 all-to-all-done.1.next_ref
  60.9 0.2 shard_map.45
  61.1 0.0 collective-permute-done.3.next_ref
  61.1 27.1 %all_to_all.20.codes_ref = s16[16,128,128]{2,1,0:T(8,128)(2,1)S(1)} all-to-all(s16[16,128,128]{2,1,0:T(8,128)(2,1)S(1)} %get-tuple-element.34), channel_id=1, replica_groups=mesh['genome'=32,'cols'=16] {'cols'}, dimensions={0} | all-to-all | bytes 1048576 | tf_op jit(solution)/shard_map/all_to_all | solution.py:424
  88.2 1.2 shard_map.47
  89.4 5.6 %collective-permute-start.4 = (s16[192,512]{1,0:T(8,128)(2,1)S(1)}, s16[192,512]{1,0:T(8,128)(2,1)S(1)}, u32[]{:S(2)}, u32[]{:S(2)}) collective-permute-start(s16[192,512]{1,0:T(8,128)(2,1)S(1)} %get-tuple-element.38), channel_id=1, source_target_pairs={{0,16},{16,32},{32,48},{48,64},{64,80},{80,96},{96,112},{112,128},... | collective-permute-start | bytes 589832 | tf_op jit(solution)/shard_map/ppermute | solution.py:439
  95.1 0.5 shard_map.48.part_ref
  95.6 2.1 %collective-permute-done.4.came_ref = s16[192,512]{1,0:T(8,128)(2,1)S(1)} collective-permute-done((s16[192,512]{1,0:T(8,128)(2,1)S(1)}, s16[192,512]{1,0:T(8,128)(2,1)S(1)}, u32[]{:S(2)}, u32[]{:S(2)}) %collective-permute-start.4) | collective-permute-done | bytes 196640 | tf_op jit(solution)/shard_map/ppermute | solution.py:439
  97.7 1.2 shard_map.49
  98.9 4.3 %collective-permute-start.5 = (s16[192,512]{1,0:T(8,128)(2,1)S(1)}, s16[192,512]{1,0:T(8,128)(2,1)S(1)}, u32[]{:S(2)}, u32[]{:S(2)}) collective-permute-start(s16[192,512]{1,0:T(8,128)(2,1)S(1)} %get-tuple-element.45), channel_id=1, source_target_pairs={{16,32},{32,16},{48,64},{64,48},{80,96},{96,80},{112,128},{128,112... | collective-permute-start | bytes 589832 | tf_op jit(solution)/shard_map/ppermute | solution.py:435
  103.2 1.9 %collective-permute-start.6 = (s16[192,512]{1,0:T(8,128)(2,1)S(1)}, s16[192,512]{1,0:T(8,128)(2,1)S(1)}, u32[]{:S(2)}, u32[]{:S(2)}) collective-permute-start(s16[192,512]{1,0:T(8,128)(2,1)S(1)} %get-tuple-element.46), channel_id=1, source_target_pairs={{0,16},{16,0},{32,48},{48,32},{64,80},{80,64},{96,112},{112,96},{1... | collective-permute-start | bytes 589832 | tf_op jit(solution)/shard_map/ppermute | solution.py:436
  105.2 0.5 shard_map.50.part_ref
  105.6 0.9 collective-permute-done.5.across_in
  106.6 0.0 collective-permute-done.6.inside_in
  106.6 1.2 shard_map.51
  107.8 3.6 %collective-permute-start.7 = (s16[192,512]{1,0:T(8,128)(2,1)S(1)}, s16[192,512]{1,0:T(8,128)(2,1)S(1)}, u32[]{:S(2)}, u32[]{:S(2)}) collective-permute-start(s16[192,512]{1,0:T(8,128)(2,1)S(1)} %get-tuple-element.48), channel_id=1, source_target_pairs={{16,32},{32,16},{48,64},{64,48},{80,96},{96,80},{112,128},{128,112... | collective-permute-start | bytes 589832 | tf_op jit(solution)/shard_map/ppermute | solution.py:435
  111.4 1.9 %collective-permute-start.8 = (s16[192,512]{1,0:T(8,128)(2,1)S(1)}, s16[192,512]{1,0:T(8,128)(2,1)S(1)}, u32[]{:S(2)}, u32[]{:S(2)}) collective-permute-start(s16[192,512]{1,0:T(8,128)(2,1)S(1)} %get-tuple-element.49), channel_id=1, source_target_pairs={{0,16},{16,0},{32,48},{48,32},{64,80},{80,64},{96,112},{112,96},{1... | collective-permute-start | bytes 589832 | tf_op jit(solution)/shard_map/ppermute | solution.py:436
  113.3 0.2 shard_map.53.early_ref
  113.6 0.5 shard_map.52.part_ref
  114.1 2.2 %collective-permute-done.7.across_in = s16[192,512]{1,0:T(8,128)(2,1)S(1)} collective-permute-done((s16[192,512]{1,0:T(8,128)(2,1)S(1)}, s16[192,512]{1,0:T(8,128)(2,1)S(1)}, u32[]{:S(2)}, u32[]{:S(2)}) %collective-permute-start.7) | collective-permute-done | bytes 196640 | tf_op jit(solution)/shard_map/ppermute | solution.py:435
  116.3 0.0 collective-permute-done.8.inside_in
  116.3 0.7 shard_map.54
  117.1 22.8 %all_to_all.21.moments_ref = f32[32,1,1280]{2,1,0:T(1,128)S(1)} all-to-all(f32[32,1,1280]{2,1,0:T(1,128)S(1)} %get-tuple-element.50), channel_id=1, replica_groups=mesh['genome'=32,'cols'=16] {'genome'}, dimensions={0} | all-to-all | bytes 327680 | tf_op jit(solution)/shard_map/all_to_all | solution.py:446
  139.9 1.4 %shard_map.55 = (f32[184,512]{1,0:T(8,128)}, f32[184,512]{1,0:T(8,128)}) custom-call(f32[32,1,1280]{2,1,0:T(1,128)S(1)} %all_to_all.21.moments_ref, f32[184,512]{1,0:T(8,128)S(1)} %bitcast.7, f32[184,512]{1,0:T(8,128)S(1)} %get-tuple-element.44.v_ref.b_ref, f32[184,512]{1,0:T(8,128)S(1)} %get-tuple-element.47.v_ref.c_ref, f32[184,512]{1,0:T(8,128)S(1)} %get-tuple-element.51.d_ref), custom_call_target="tpu_custom_call" | custom-call | tf_op jit(solution)/shard_map/pallas_call | solution.py:38
Async XLA Ops:
  2.3 18.7 %collective-permute-start.2 = (bf16[1920,256]{1,0:T(8,128)(2,1)S(1)}, bf16[1920,256]{1,0:T(8,128)(2,1)}, u32[]{:S(2)}, u32[]{:S(2)}) collective-permute-start(bf16[1920,256]{1,0:T(8,128)(2,1)S(1)} %slice_convert_fusion.1.first_ref), channel_id=1, source_target_pairs={{16,0},{32,16},{48,32},{64,48},{80,64},{96,80},{112,96},{128,112},... | collective-permute-start | bytes 2949128 | tf_op jit(solution)/shard_map/ppermute | solution.py:396
  12.8 17.3 %collective-permute-start.1 = (bf16[1920,256]{1,0:T(8,128)(2,1)S(1)}, bf16[1920,256]{1,0:T(8,128)(2,1)}, u32[]{:S(2)}, u32[]{:S(2)}) collective-permute-start(bf16[1920,256]{1,0:T(8,128)(2,1)S(1)} %slice_convert_fusion.second_ref), channel_id=1, source_target_pairs={{16,0},{32,16},{48,32},{64,48},{80,64},{96,80},{112,96},{128,112},... | collective-permute-start | bytes 2949128 | tf_op jit(solution)/shard_map/ppermute | solution.py:398
  16.0 0.8 copy-start.1
  16.8 30.2 %copy-start = (f32[512,184]{0,1:T(8,128)S(1)}, f32[512,184]{0,1:T(8,128)}, u32[]{:S(2)}) copy-start(f32[512,184]{0,1:T(8,128)} %param.3) | copy-start | bytes 1130500
  16.8 18.6 %all-to-all-start = ((s16[8,192,128]{2,1,0:T(8,128)(2,1)}), s16[8,192,128]{2,1,0:T(8,128)(2,1)}, u32[]{:S(2)}, u32[]{:S(2)}) async-start(s16[8,192,128]{2,1,0:T(8,128)(2,1)} %copy-done.1), calls=%async_computation | async-start | bytes 786432 | tf_op jit(solution)/shard_map/all_to_all | solution.py:405
  35.3 25.5 %all-to-all-start.1 = ((s16[16,88,128]{2,1,0:T(8,128)(2,1)}), s16[16,88,128]{2,1,0:T(8,128)(2,1)S(1)}, u32[]{:S(2)}, u32[]{:S(2)}) async-start(s16[16,88,128]{2,1,0:T(8,128)(2,1)} %shard_map.44), calls=%async_computation.1 | async-start | bytes 720896 | tf_op jit(solution)/shard_map/all_to_all | solution.py:414
  47.2 13.9 %collective-permute-start.3 = (s16[192,512]{1,0:T(8,128)(2,1)S(1)}, s16[192,512]{1,0:T(8,128)(2,1)S(1)}, u32[]{:S(2)}, u32[]{:S(2)}) collective-permute-start(s16[192,512]{1,0:T(8,128)(2,1)S(1)} %shard_map.46), channel_id=1, source_target_pairs={{16,0},{32,16},{48,32},{64,48},{80,64},{96,80},{112,96},{128,112},... | collective-permute-start | bytes 589832 | tf_op jit(solution)/shard_map/ppermute | solution.py:415
  50.2 10.7 %collective-permute-start = (s16[96,128]{1,0:T(8,128)(2,1)S(1)}, s16[96,128]{1,0:T(8,128)(2,1)S(1)}, u32[]{:S(2)}, u32[]{:S(2)}) collective-permute-start(s16[96,128]{1,0:T(8,128)(2,1)S(1)} %get-tuple-element.31), channel_id=1, source_target_pairs={{0,8},{1,9},{2,10},{3,11},{4,12},{5,13},{6,14},{7,15},{8,0},{9,1},... | collective-permute-start | bytes 73736 | tf_op jit(solution)/shard_map/ppermute | solution.py:412
  89.4 8.2 %collective-permute-start.4 = (s16[192,512]{1,0:T(8,128)(2,1)S(1)}, s16[192,512]{1,0:T(8,128)(2,1)S(1)}, u32[]{:S(2)}, u32[]{:S(2)}) collective-permute-start(s16[192,512]{1,0:T(8,128)(2,1)S(1)} %get-tuple-element.38), channel_id=1, source_target_pairs={{0,16},{16,32},{32,48},{48,64},{64,80},{80,96},{96,112},{112,128},... | collective-permute-start | bytes 589832 | tf_op jit(solution)/shard_map/ppermute | solution.py:439
  98.9 7.7 %collective-permute-start.5 = (s16[192,512]{1,0:T(8,128)(2,1)S(1)}, s16[192,512]{1,0:T(8,128)(2,1)S(1)}, u32[]{:S(2)}, u32[]{:S(2)}) collective-permute-start(s16[192,512]{1,0:T(8,128)(2,1)S(1)} %get-tuple-element.45), channel_id=1, source_target_pairs={{16,32},{32,16},{48,64},{64,48},{80,96},{96,80},{112,128},{128,112... | collective-permute-start | bytes 589832 | tf_op jit(solution)/shard_map/ppermute | solution.py:435
  103.2 3.3 %collective-permute-start.6 = (s16[192,512]{1,0:T(8,128)(2,1)S(1)}, s16[192,512]{1,0:T(8,128)(2,1)S(1)}, u32[]{:S(2)}, u32[]{:S(2)}) collective-permute-start(s16[192,512]{1,0:T(8,128)(2,1)S(1)} %get-tuple-element.46), channel_id=1, source_target_pairs={{0,16},{16,0},{32,48},{48,32},{64,80},{80,64},{96,112},{112,96},{1... | collective-permute-start | bytes 589832 | tf_op jit(solution)/shard_map/ppermute | solution.py:436
  107.8 8.5 %collective-permute-start.7 = (s16[192,512]{1,0:T(8,128)(2,1)S(1)}, s16[192,512]{1,0:T(8,128)(2,1)S(1)}, u32[]{:S(2)}, u32[]{:S(2)}) collective-permute-start(s16[192,512]{1,0:T(8,128)(2,1)S(1)} %get-tuple-element.48), channel_id=1, source_target_pairs={{16,32},{32,16},{48,64},{64,48},{80,96},{96,80},{112,128},{128,112... | collective-permute-start | bytes 589832 | tf_op jit(solution)/shard_map/ppermute | solution.py:435
  111.4 4.9 %collective-permute-start.8 = (s16[192,512]{1,0:T(8,128)(2,1)S(1)}, s16[192,512]{1,0:T(8,128)(2,1)S(1)}, u32[]{:S(2)}, u32[]{:S(2)}) collective-permute-start(s16[192,512]{1,0:T(8,128)(2,1)S(1)} %get-tuple-element.49), channel_id=1, source_target_pairs={{0,16},{16,0},{32,48},{48,32},{64,80},{80,64},{96,112},{112,96},{1... | collective-permute-start | bytes 589832 | tf_op jit(solution)/shard_map/ppermute | solution.py:436
